TPU v7x, 256 devices: a whole 4x4x8 slice. The times are simulated.
256 devices in a mesh: rep: 16 (over y_lo, z), tp: 16 (over x, y_hi, core).
Axes of the slice: x: 4, y: 4 (y_hi: 2, y_lo: 2; y = y_hi * 2 + y_lo), z: 8, core: 2. Of those that a mesh axis runs over, the one named last changes fastest.
Arguments:
- tokens: bfloat16 [16384, 8192], P('rep', 'tp'), may hold values from -6 to 6
- grad_out: bfloat16 [16384, 4096], P('rep', 'tp'), may hold values from -0.046875 to 0.046875
- lengths: int32 [16, 16], replicated, may hold values from 0 to 256, as said below
- master: float32 [8192, 2048], P('rep', 'tp'), may hold values from -3 to 3
- first: float32 [8192, 2048], P('rep', 'tp'), may hold values from -6 to 6
- second: float32 [8192, 2048], P('rep', 'tp'), may hold values from 0.25 to 4
Outputs:
- new_master: float32 [8192, 2048], P('rep', 'tp')
- new_first: float32 [8192, 2048], P('rep', 'tp')
- new_second: float32 [8192, 2048], P('rep', 'tp')
- healthy_weights: bfloat16 [8192, 2048], P(None, 'tp')
- slot_weights: bfloat16 [16, 8192, 4096], P('rep', None, 'tp')
Inputs may be any that keep to these rules, and one draw needn't show every extreme that they name: `lengths`: each row is one replica's split of the 2048 columns over its devices in tp order: the entries are multiples of 64, sum to 2048, the nonzero ones come first and number at least half of the row; a row is either all 128 or has an entry equal to 256, and some row has an entry equal to 256.
All inputs are finite; a program needn't handle non-finite values.
Results may differ from a plain program's by a relative error of at most 0.0019.
Values may be sent and summed in bfloat16 or wider, within the bound.
No kernel may reach another device: no remote copies, remote signals or barrier semaphores. Data moves between devices by JAX's collectives and lax.ppermute only.
A program may use at most 128 MiB of HBM per device.

v0:
```python
import jax
import jax.numpy as jnp
from jax import lax
from jax.sharding import Mesh
from jax.sharding import PartitionSpec as P

COLS = 2048
STEP = 1000
REP = ("rep_0", "rep_1")


decay_first = 0.9
decay_second = 0.999
learning_rate = 0.02
weight_decay = 0.1
epsilon = 1e-08


def own_block(parts, axes, turns):
    inside = parts.shape[1:]
    parts = parts.reshape(*(lax.axis_size(a) for a in axes), *inside)
    parts = jnp.moveaxis(parts, turns, range(len(axes))).reshape(-1, *inside)
    for k in turns:
        parts = lax.psum_scatter(parts, axes[k], scatter_dimension=0, tiled=True)
    return parts[0]


def in_blocks(value, dim, size):
    before, after = (value.shape[:dim], value.shape[dim + 1 :])
    return jnp.moveaxis(value.reshape(*before, size, -1, *after), dim, 0)


def summed_rows(value, axes, turns, dim):
    size = lax.axis_size(axes)
    return own_block(in_blocks(value, dim, size), axes, turns)


def from_everyone(value, axis):
    copies = jnp.broadcast_to(value, (lax.axis_size(axis), *value.shape))
    return lax.all_to_all(copies, axis, split_axis=0, concat_axis=0, tiled=True)


def laid_out(parts, dim):
    shape = list(parts.shape[1:])
    shape[dim] *= parts.shape[0]
    return jnp.moveaxis(parts, 0, dim).reshape(shape)


def gathered_copies(value, axis, dim):
    parts = from_everyone(value, axis)
    return laid_out(parts, dim)


def adam_update(master, first, second, gradient):
    scale_first = 1.0 - decay_first**STEP
    scale_second = 1.0 - decay_second**STEP
    new_first = decay_first * first + (1.0 - decay_first) * gradient
    new_second = decay_second * second + (1.0 - decay_second) * gradient * gradient
    direction = new_first / scale_first / (jnp.sqrt(new_second / scale_second) + epsilon)
    new_master = master - learning_rate * (direction + weight_decay * master)
    return (new_master, new_first, new_second)


def on_device(tokens, grad_out, lengths, master, first, second):
    shards = lax.axis_size("tp")
    replicas = lax.axis_size(REP)
    column_index = lax.axis_index("tp")
    replica_index = lax.axis_index(REP)
    token_count = tokens.shape[0]
    slot_width = grad_out.shape[1]
    block_width = COLS // shards
    begins_all = jnp.cumsum(lengths, axis=1) - lengths
    is_mine = jnp.arange(shards, dtype=jnp.int32) == column_index
    own_lengths = lax.dynamic_index_in_dim(lengths, replica_index, 0, keepdims=False)
    own_begins = lax.dynamic_index_in_dim(begins_all, replica_index, 0, keepdims=False)
    my_begin = jnp.sum(jnp.where(is_mine, own_begins, 0))
    my_length = jnp.sum(jnp.where(is_mine, own_lengths, 0))
    columns = jnp.arange(COLS, dtype=jnp.int32)
    offset = columns - my_begin
    inside = (offset >= 0) & (offset < my_length)
    picked = jnp.take(grad_out, jnp.clip(offset, 0, slot_width - 1), axis=1)
    spread = jnp.where(inside[None, :], picked, jnp.zeros_like(picked)).reshape(
        token_count, shards, block_width
    )
    received = lax.all_to_all(spread, "tp", split_axis=1, concat_axis=1, tiled=True)
    grad_block = jnp.sum(received, axis=1)
    grad_columns = lax.dot_general(
        lax.all_gather(tokens, "tp", axis=1, tiled=True),
        grad_block,
        (((0,), (0,)), ((), ())),
        preferred_element_type=jnp.float32,
    )
    summed = summed_rows(grad_columns.astype(jnp.bfloat16), REP, (1, 0), 0).astype(jnp.float32)
    new_master, new_first, new_second = adam_update(master, first, second, summed)
    weights = new_master.astype(jnp.bfloat16)
    healthy = gathered_copies(weights, REP, 0)
    replica_rows = lax.all_gather(weights, "tp", axis=1, tiled=True)
    slot_begins = jnp.sum(jnp.where(is_mine[None, :], begins_all, 0), axis=1)
    slot_lengths = jnp.sum(jnp.where(is_mine[None, :], lengths, 0), axis=1)
    within = jnp.arange(slot_width, dtype=jnp.int32)
    source_cols = slot_begins[:, None] + within[None, :]
    valid = within[None, :] < slot_lengths[:, None]
    taken = jnp.take(replica_rows, jnp.clip(source_cols, 0, COLS - 1).reshape(-1), axis=1)
    outgoing = jnp.where(valid.reshape(-1)[None, :], taken, jnp.zeros_like(taken))
    outgoing = outgoing.reshape(replica_rows.shape[0], replicas, slot_width)
    arrived = lax.all_to_all(outgoing, REP, split_axis=1, concat_axis=0, tiled=True)
    slot_weights = arrived.reshape(1, -1, slot_width)
    return (new_master, new_first, new_second, healthy, slot_weights)


def solution(mesh):
    torus = Mesh(mesh.devices.reshape(2, 8, mesh.shape["tp"]), ("rep_0", "rep_1", "tp"))
    placed = (P(REP, "tp"), P(REP, "tp"), P(), P(REP, "tp"), P(REP, "tp"), P(REP, "tp"))
    return jax.shard_map(
        on_device,
        mesh=torus,
        in_specs=placed,
        out_specs=(P(REP, "tp"), P(REP, "tp"), P(REP, "tp"), P(None, "tp"), P(REP, None, "tp")),
        check_vma=False,
    )
```

profile of v0, /device:TPU:32, one launch (start us, length us, event | category | flops | bytes accessed | tf_op | source)
XLA Modules:
  0.0 450.8 jit_solution(10688095374911271748)
XLA Ops:
  7.2 0.0 all-gather.3.cloned.1.call-start
  7.2 0.7 all-gather.3.cloned.1.call-update
  7.9 0.0 reduce-scatter.3.cloned.1.call-start
  8.0 0.9 reduce_window_sum.11
  8.8 1.2 copy.34
  10.1 0.8 select_reduce_fusion.1
  10.9 1.3 fusion.12
  12.2 0.7 compare_select_fusion.1
  12.9 9.6 %gather_fusion = bf16[2048,1024]{1,0:T(8,128)(2,1)} fusion(bf16[1024,256]{0,1:T(8,128)(2,1)S(1)} %copy.34, s32[2048]{0:T(1024)S(1)} %broadcast_clamp_fusion.1), kind=kCustom, calls=%fused_computation | custom fusion | bytes 8396800 | tf_op jit(solution)/shard_map/jit(_take)/gather | solution.py:81
  22.5 0.7 fusion.10
  23.2 1.3 fusion.11
  24.5 3.1 select_select_fusion.1
  27.6 73.9 %all_to_all.25 = bf16[1024,16,128]{0,2,1:T(8,128)(2,1)} all-to-all(bf16[1024,16,128]{0,2,1:T(8,128)(2,1)S(1)} %select_select_fusion.1), channel_id=1, replica_groups=mesh['rep_0'=2,'rep_1'=8,'tp'=16] {'tp'}, dimensions={1} | all-to-all | bytes 8388608 | tf_op jit(solution)/shard_map/all_to_all | solution.py:85
  101.5 3.1 reduce_sum.50
  104.7 63.9 %all-gather.3.cloned.1.call-done = bf16[1024,8192]{1,0:T(8,128)(2,1)} async-done(((bf16[1024,512]{1,0:T(8,128)(2,1)}), bf16[1024,8192]{1,0:T(8,128)(2,1)}) %all-gather.3.cloned.1.call-update) | async-done | bytes 16777232 | tf_op jit(solution)/shard_map/all_gather | solution.py:88
  168.6 8.1 %convolution_convert_fusion = bf16[128,8192]{1,0:T(8,128)(2,1)S(1)} fusion(bf16[1024,128]{0,1:T(8,128)(2,1)S(1)} %reduce_sum.50, bf16[1024,8192]{1,0:T(8,128)(2,1)} %all-gather.3.cloned.1.call-done), kind=kOutput, calls=%fused_computation.2 | convolution fusion | flops 2148532224 | bytes 19136512 | tf_op jit(solution)/shard_map/dot_general | solution.py:87
  176.7 0.9 copy.44
  177.6 0.0 copy-start
  177.6 0.0 copy-start.1
  177.6 0.0 copy-start.2
  177.6 2.5 copy.35
  180.1 0.0 reduce-scatter.3.cloned.1.call-update
  180.1 0.0 reduce-scatter.5.cloned.1.call-start
  180.2 41.0 %reduce-scatter.3.cloned.1.call-done = bf16[2,512,128]{1,2,0:T(8,128)(2,1)} async-done(((bf16[16,512,128]{1,2,0:T(8,128)(2,1)}), bf16[2,512,128]{1,2,0:T(8,128)(2,1)}) %reduce-scatter.3.cloned.1.call-update) | async-done | bytes 262160 | tf_op jit(solution)/shard_map/reduce_scatter | solution.py:24
  221.2 0.0 reduce-scatter.5.cloned.1.call-update
  221.2 0.0 all-gather.5.cloned.1.call-start
  221.2 0.0 copy-done
  221.2 0.1 copy.33
  221.4 0.0 copy-done.1
  221.4 0.1 copy.36
  221.5 0.0 copy-done.2
  221.5 0.1 copy.38
  221.7 18.0 %reduce-scatter.5.cloned.1.call-done = bf16[1,512,128]{1,2,0:T(8,128)(2,1)} async-done(((bf16[2,512,128]{1,2,0:T(8,128)(2,1)}), bf16[1,512,128]{1,2,0:T(8,128)(2,1)}) %reduce-scatter.5.cloned.1.call-update) | async-done | bytes 131088 | tf_op jit(solution)/shard_map/reduce_scatter | solution.py:24
  239.7 1.8 fusion.14
  241.5 0.0 all-gather.5.cloned.1.call-update
  241.5 1.0 copy.39
  242.5 1.7 broadcast_in_dim.78
  244.3 7.5 %all-to-all-start.1 = ((bf16[16,512,128]{2,1,0:T(8,128)(2,1)}), bf16[16,512,128]{2,1,0:T(8,128)(2,1)S(1)}, u32[]{:S(2)}, u32[]{:S(2)}) async-start(bf16[16,512,128]{2,1,0:T(8,128)(2,1)} %broadcast_in_dim.78), calls=%async_computation.3 | async-start | bytes 4194304 | tf_op jit(solution)/shard_map/all_to_all | solution.py:40
  251.8 0.1 fusion.2
  251.9 0.1 iota_compare_fusion
  252.0 52.9 %all-gather.5.cloned.1.call-done = bf16[512,2048]{0,1:T(8,128)(2,1)} async-done(((bf16[512,128]{0,1:T(8,128)(2,1)}), bf16[512,2048]{0,1:T(8,128)(2,1)}) %all-gather.5.cloned.1.call-update) | async-done | bytes 2097168 | tf_op jit(solution)/shard_map/all_gather | solution.py:97
  304.9 19.3 %gather_fusion.1 = bf16[4096,512]{1,0:T(8,128)(2,1)} fusion(bf16[512,2048]{0,1:T(8,128)(2,1)} %all-gather.5.cloned.1.call-done, s32[4096]{0:T(1024)S(1)} %broadcast_clamp_fusion), kind=kCustom, calls=%fused_computation.1 | custom fusion | bytes 8404992 | tf_op jit(solution)/shard_map/jit(_take)/gather | solution.py:103
  324.2 5.2 %select_select_fusion = bf16[512,16,256]{0,2,1:T(8,128)(2,1)} fusion(bf16[512,16,256]{0,2,1:T(8,128)(2,1)} %bitcast.43, pred[16,256]{1,0:T(8,128)(4,1)S(1)} %get-tuple-element.30, pred[16,256]{1,0:T(8,128)(4,1)S(1)} %get-tuple-element.29), kind=kLoop, calls=%fused_computation.3 | loop fusion | flops 4194304 | bytes 8396800 | tf_op jit(solution)/shard_map/jit(_where)/select_n | solution.py:104
  329.5 0.0 all-to-all-done.1
  329.5 11.3 %all-to-all-start.2 = ((bf16[512,16,256]{0,2,1:T(8,128)(2,1)}), bf16[512,16,256]{0,2,1:T(8,128)(2,1)}, u32[]{:S(2)}, u32[]{:S(2)}) async-start(bf16[512,16,256]{0,2,1:T(8,128)(2,1)} %select_select_fusion), calls=%async_computation.4 | async-start | bytes 8388608 | tf_op jit(solution)/shard_map/all_to_all | solution.py:106
  340.7 0.8 copy.41
  341.6 0.8 copy.42
  342.4 0.8 copy.43
  343.2 93.3 %all-to-all-done.2 = bf16[512,16,256]{0,2,1:T(8,128)(2,1)} async-done(((bf16[512,16,256]{0,2,1:T(8,128)(2,1)}), bf16[512,16,256]{0,2,1:T(8,128)(2,1)}, u32[]{:S(2)}, u32[]{:S(2)}) %all-to-all-start.2) | async-done | bytes 4194336 | tf_op jit(solution)/shard_map/all_to_all | solution.py:106
  436.6 6.4 %copy.40 = bf16[16,512,1,256]{3,1,0,2:T(8,128)(2,1)} copy(bf16[16,512,1,256]{1,3,0,2:T(8,128)(2,1)} %bitcast.15) | data formatting | bytes 8388608 | tf_op jit(solution)/shard_map/all_to_all | solution.py:106
  443.0 1.3 copy.47
  (5 shorter events, 0.1 us)
Async XLA Ops:
  7.2 161.4 %all-gather.3.cloned.1.call-start = ((), (), s32[]{:S(2)}) async-start(), calls=%async_computation.5 | async-start | bytes 17825792 | tf_op jit(solution)/shard_map/all_gather | solution.py:88
  7.9 213.3 %reduce-scatter.3.cloned.1.call-start = ((), (), s32[]{:S(2)}) async-start(), calls=%async_computation.6 | async-start | bytes 2359296 | tf_op jit(solution)/shard_map/reduce_scatter | solution.py:24
  177.6 43.7 %copy-start = (f32[512,128]{1,0:T(8,128)S(1)}, f32[512,128]{1,0:T(8,128)}, u32[]{:S(2)}) copy-start(f32[512,128]{1,0:T(8,128)} %param.10) | copy-start | bytes 786436
  177.6 43.8 %copy-start.1 = (f32[512,128]{1,0:T(8,128)S(1)}, f32[512,128]{1,0:T(8,128)}, u32[]{:S(2)}) copy-start(f32[512,128]{1,0:T(8,128)} %param.11) | copy-start | bytes 786436
  177.6 43.9 %copy-start.2 = (f32[512,128]{1,0:T(8,128)S(1)}, f32[512,128]{1,0:T(8,128)}, u32[]{:S(2)}) copy-start(f32[512,128]{1,0:T(8,128)} %param.9) | copy-start | bytes 786436
  180.1 59.6 %reduce-scatter.5.cloned.1.call-start = ((), (), s32[]{:S(2)}) async-start(), calls=%async_computation.7 | async-start | bytes 393216 | tf_op jit(solution)/shard_map/reduce_scatter | solution.py:24
  221.2 83.7 %all-gather.5.cloned.1.call-start = ((), (), s32[]{:S(2)}) async-start(), calls=%async_computation.8 | async-start | bytes 2228224 | tf_op jit(solution)/shard_map/all_gather | solution.py:97
  244.3 85.2 %all-to-all-start.1 = ((bf16[16,512,128]{2,1,0:T(8,128)(2,1)}), bf16[16,512,128]{2,1,0:T(8,128)(2,1)S(1)}, u32[]{:S(2)}, u32[]{:S(2)}) async-start(bf16[16,512,128]{2,1,0:T(8,128)(2,1)} %broadcast_in_dim.78), calls=%async_computation.3 | async-start | bytes 4194304 | tf_op jit(solution)/shard_map/all_to_all | solution.py:40
  329.5 107.1 %all-to-all-start.2 = ((bf16[512,16,256]{0,2,1:T(8,128)(2,1)}), bf16[512,16,256]{0,2,1:T(8,128)(2,1)}, u32[]{:S(2)}, u32[]{:S(2)}) async-start(bf16[512,16,256]{0,2,1:T(8,128)(2,1)} %select_select_fusion), calls=%async_computation.4 | async-start | bytes 8388608 | tf_op jit(solution)/shard_map/all_to_all | solution.py:106
Sparse Core Ops, SparseCore 0:
  10.5 158.0 all-gather.2
  180.3 40.8 reduce-scatter.2
  223.7 16.0 reduce-scatter.4
  242.8 62.0 all-gather.4
where the time goes:
time: 452 us; the launch traced here: 451 us
  waiting for transfers between devices  270 us (60%)
  blocking collectives  73.9 us (16%)
  local copies, waits for them, and re-layouts  46.9 us (10%)
  other arithmetic  19.1 us (4%)
  starting transfers between devices  18.9 us (4%)
  between operations  13.9 us (3%)
  matrix products  8.12 us (2%)
    all_to_all x1, waiting for transfers between devices, on_device(): lax.all_to_all(outgoing, REP, split_axis=1, concat_axis=0, tiled=True)  93.3 us
    all_to_all x1, blocking collectives, on_device(): lax.all_to_all(spread, 'tp', split_axis=1, concat_axis=1, tiled=True)  73.9 us
    all_gather x1, waiting for transfers between devices, on_device(): lax.all_gather(tokens, 'tp', axis=1, tiled=True)  63.9 us
    reduce_scatter x2, waiting for transfers between devices, own_block(): parts = lax.psum_scatter(parts, axes[k], scatter_dimension=0, tiled=True)  59 us
    all_gather x1, waiting for transfers between devices, on_device(): replica_rows = lax.all_gather(weights, 'tp', axis=1, tiled=True)  52.9 us
    gather x1, local copies, waits for them, and re-layouts, on_device(): jnp.take(replica_rows, jnp.clip(source_cols, 0, COLS - 1).reshape(-1), ax...  19.3 us
    all_to_all x1, starting transfers between devices, on_device(): lax.all_to_all(outgoing, REP, split_axis=1, concat_axis=0, tiled=True)  11.3 us
    gather x1, local copies, waits for them, and re-layouts, on_device(): picked = jnp.take(grad_out, jnp.clip(offset, 0, slot_width - 1), axis=1)  9.61 us
  transfers between devices with their start and end apart: 6, of which 5 were waited for; matrix products, arithmetic and copies ran while one was open for 12% of the time, Pallas kernels for 0%

commit v1 on v0

v1 whole, which is shorter than its diff:
```python
import jax
import jax.numpy as jnp
from jax import lax
from jax.experimental import pallas as pl
from jax.experimental.pallas import tpu as pltpu
from jax.sharding import Mesh
from jax.sharding import PartitionSpec as P

STEP = 1000
UNIT = 64
AXES = ("yl", "zh", "z0", "x", "yh", "co")
REP = ("yl", "zh", "z0")
TP = ("x", "yh", "co")
Z = ("zh", "z0")
GROUP = ("yl", "z0", "x", "yh", "co")
SWAP = [(0, 1), (1, 0)]

decay_first = 0.9
decay_second = 0.999
learning_rate = 0.02
weight_decay = 0.1
epsilon = 1e-08


def adam_update(master, first, second, gradient):
    scale_first = 1.0 - decay_first**STEP
    scale_second = 1.0 - decay_second**STEP
    new_first = decay_first * first + (1.0 - decay_first) * gradient
    new_second = decay_second * second + (1.0 - decay_second) * gradient * gradient
    direction = new_first / scale_first / (jnp.sqrt(new_second / scale_second) + epsilon)
    new_master = master - learning_rate * (direction + weight_decay * master)
    return (new_master, new_first, new_second)


def column_block(yl, z0, co, x, yh):
    return 4 * (yl ^ (x >> 1)) + 2 * (z0 ^ (x & 1)) + (co ^ yh)


def home_permutation():
    pairs = []
    for yl in range(2):
        for zh in range(4):
            for z0 in range(2):
                for x in range(4):
                    for yh in range(2):
                        for co in range(2):
                            half, right = zh >> 1, zh & 1
                            source = ((((yl * 4 + zh) * 2 + z0) * 4 + x) * 2 + yh) * 2 + co
                            row = 4 * x + 2 * yh + (co ^ half)
                            col = 2 * column_block(yl, z0, co, x, yh) + right
                            pairs.append((source, row * 16 + col))
    return pairs


def swapped_halves(tile):
    return pltpu.roll(tile.astype(jnp.float32), UNIT, 1)


def pack_kernel(place_ref, lengths_ref, slots_ref, out_ref, table_ref):
    replica = place_ref[0]
    begin = jnp.int32(0)
    for j in range(16):
        count = lengths_ref[replica, j] // UNIT
        for k in range(4):

            @pl.when(k < count)
            def _(begin=begin, j=j, k=k):
                table_ref[begin + k] = jnp.int32(4 * j + k)

        begin = begin + count
    lane = lax.broadcasted_iota(jnp.int32, slots_ref.shape[1:], 1)
    for d in range(16):
        left, right = table_ref[2 * d], table_ref[2 * d + 1]
        tile_l, tile_r = slots_ref[left // 2], slots_ref[right // 2]
        low = jnp.where(left % 2 == 0, tile_l.astype(jnp.float32), swapped_halves(tile_l))
        high = jnp.where(right % 2 == 1, tile_r.astype(jnp.float32), swapped_halves(tile_r))
        dense = jnp.where(lane < UNIT, low, high).astype(out_ref.dtype)
        block, part = d // 2, 128 * (d % 2)
        for x in range(4):
            for yh in range(2):
                for yl in range(2):
                    for z0 in range(2):
                        for co in range(2):
                            if column_block(yl, z0, co, x, yh) == block:
                                out_ref[yl, z0, 2 * x + yh, co, :, part : part + 128] = dense


def packed_columns(slots, lengths, place):
    tokens = slots.shape[1]
    smem = pl.BlockSpec(memory_space=pltpu.SMEM)
    vmem = pl.BlockSpec(memory_space=pltpu.VMEM)
    return pl.pallas_call(
        pack_kernel,
        out_shape=jax.ShapeDtypeStruct((2, 2, 8, 2, tokens, 256), slots.dtype),
        in_specs=[smem, smem, vmem],
        out_specs=vmem,
        scratch_shapes=[pltpu.SMEM((32,), jnp.int32)],
        cost_estimate=pl.CostEstimate(flops=1_000_000, bytes_accessed=5_000_000, transcendentals=0),
        name="pack",
    )(place, lengths, slots)


def unpack_kernel(place_ref, lengths_ref, weights_ref, out_ref, windows_ref):
    group = pl.program_id(0)
    replica = 8 * (group // 2) + 2 * place_ref[1] + group % 2
    zh, blocks, rows, width = weights_ref.shape
    lane = lax.broadcasted_iota(jnp.int32, (zh, rows, width), 2)

    @pl.when(group == 0)
    def _():
        def turned(t):
            tile = weights_ref[:, t].reshape(zh * rows, width)
            return pltpu.roll(tile.astype(jnp.float32), UNIT, 1).reshape(zh, rows, width)

        def window(t, low):
            high = turned(jnp.minimum(t + 1, blocks - 1))
            windows_ref[2 * t] = weights_ref[:, t]
            windows_ref[2 * t + 1] = jnp.where(lane < UNIT, low, high).astype(windows_ref.dtype)
            return high

        lax.fori_loop(0, blocks, window, turned(0))

    def slot(j, begin):
        count = lengths_ref[replica, j] // UNIT
        for k in range(2):
            value = windows_ref[jnp.minimum(begin + 2 * k, 2 * blocks - 1)]
            keep = lane < (count - 2 * k) * UNIT
            out_ref[j, :, :, width * k : width * (k + 1)] = jnp.where(keep, value, jnp.zeros_like(value))
        return begin + count

    lax.fori_loop(0, 16, slot, jnp.int32(0), unroll=True)


def slot_columns(weights, lengths, place):
    zh, blocks, rows, width = weights.shape
    smem = pl.BlockSpec(memory_space=pltpu.SMEM)
    return pl.pallas_call(
        unpack_kernel,
        out_shape=jax.ShapeDtypeStruct((64, zh, rows, 256), weights.dtype),
        grid=(4,),
        in_specs=[smem, smem, pl.BlockSpec((zh, blocks, rows, width), lambda g: (0, 0, 0, 0))],
        out_specs=pl.BlockSpec((16, zh, rows, 256), lambda g: (g, 0, 0, 0)),
        scratch_shapes=[pltpu.VMEM((2 * blocks, zh, rows, width), weights.dtype)],
        cost_estimate=pl.CostEstimate(flops=10_000_000, bytes_accessed=5_000_000, transcendentals=0),
        name="unpack",
    )(place, lengths, weights)


def ring(step):
    return [(k, (k + step) % 8) for k in range(8)]


def all_rows(weights):
    yl, z = lax.axis_index("yl"), lax.axis_index(Z)
    other = lax.ppermute(weights, "yl", SWAP)
    pair = jnp.stack([jnp.where(yl == 0, weights, other), jnp.where(yl == 0, other, weights)])
    out = jnp.zeros((2, 8, *weights.shape), weights.dtype)

    def put(out, piece, first, distance):
        return lax.dynamic_update_slice(out, piece[:, None], (first, (z + distance) % 8, 0, 0))

    out = put(out, pair, 0, 0)
    up, down = pair, pair
    for k in range(1, 4):
        up = lax.ppermute(up, Z, ring(1))
        down = lax.ppermute(down, Z, ring(-1))
        out = put(out, up, 0, 8 - k)
        out = put(out, down, 0, k)
    out = put(out, lax.ppermute(up[:1], Z, ring(1)), 0, 4)
    out = put(out, lax.ppermute(down[1:], Z, ring(-1)), 1, 4)
    return out.reshape(-1, weights.shape[1])


def product(tokens, dense):
    return lax.dot_general(tokens, dense, (((0,), (0,)), ((), ())), preferred_element_type=jnp.float32)


def on_device(tokens, grad_out, lengths, master, first, second):
    yl, z0 = lax.axis_index("yl"), lax.axis_index("z0")
    place = jnp.stack([lax.axis_index(REP), lax.axis_index("zh")]).astype(jnp.int32)
    token_count, slot_width = grad_out.shape
    half = token_count // 2

    across_y = lax.ppermute(tokens, "yl", SWAP)
    across_z = lax.ppermute(tokens, "z0", SWAP)
    across_top = lax.ppermute(across_y[:half], "z0", SWAP)
    across_bottom = lax.ppermute(across_z[half:], "yl", SWAP)
    own = [tokens, across_y, across_z, across_top, across_bottom]
    theirs = [lax.ppermute(part, "co", SWAP) for part in own]

    parts = jnp.swapaxes(grad_out.reshape(16, token_count // 16, 2, 128), 1, 2)
    slots = lax.all_to_all(parts, TP, split_axis=0, concat_axis=0, tiled=True)
    spread = packed_columns(slots.reshape(32, token_count // 16, 128), lengths, place)
    spread = spread.reshape(64, token_count // 16, 256)
    dense = lax.all_to_all(spread, GROUP, split_axis=0, concat_axis=0, tiled=True)
    dense = dense.reshape(4, token_count, 256)
    d00, d10, d01, d11 = (
        lax.dynamic_index_in_dim(dense, 2 * (yl ^ a) + (z0 ^ b), 0, False)
        for a, b in ((0, 0), (1, 0), (0, 1), (1, 1))
    )
    columns = [d00, d10, d01, d11[:half], d11[half:]]
    blocks = []
    for features in (own, theirs):
        total = sum(product(t, d) for t, d in zip(features, columns))
        total = total.astype(jnp.bfloat16)
        blocks += [total[:, :128], total[:, 128:]]
    arrived = lax.all_to_all(jnp.stack(blocks), "zh", split_axis=0, concat_axis=0, tiled=True)
    summed = jnp.sum(arrived.astype(jnp.float32), axis=0).astype(jnp.bfloat16)
    gradient = lax.ppermute(summed, AXES, home_permutation()).astype(jnp.float32)

    new_master, new_first, new_second = adam_update(master, first, second, gradient)
    weights = new_master.astype(jnp.bfloat16)

    rows = lax.all_to_all(weights.reshape(16, 32, 128), TP, split_axis=0, concat_axis=0, tiled=True)
    rows = jnp.broadcast_to(rows[None], (4, *rows.shape))
    rows = lax.all_to_all(rows, "zh", split_axis=0, concat_axis=0, tiled=True)
    outgoing = slot_columns(rows, lengths, place)
    incoming = lax.all_to_all(outgoing, GROUP, split_axis=0, concat_axis=0, tiled=True)
    slot_weights = incoming.reshape(2, 2, 16, 4, 32, slot_width).transpose(0, 3, 1, 2, 4, 5)
    slot_weights = slot_weights.reshape(1, -1, slot_width)
    healthy = all_rows(weights)
    return (new_master, new_first, new_second, healthy, slot_weights)


def solution(mesh):
    torus = Mesh(mesh.devices.reshape(2, 4, 2, 4, 2, 2), AXES)
    placed = (P(REP, TP), P(REP, TP), P(), P(REP, TP), P(REP, TP), P(REP, TP))

    return jax.shard_map(
        on_device,
        mesh=torus,
        in_specs=placed,
        out_specs=(P(REP, TP), P(REP, TP), P(REP, TP), P(None, TP), P(REP, None, TP)),
        check_vma=False,
    )
```

time: 452 us -> 294 us (0.65)
  the two profiles are of different devices: /device:TPU:32 before, /device:TPU:22 now
where the time goes in v1:
time: 294 us; the launch traced here: 293 us
  waiting for transfers between devices  140 us (48%)
  blocking collectives  58.5 us (20%)
  starting transfers between devices  54.2 us (18%)
  local copies, waits for them, and re-layouts  15.5 us (5%)
  matrix products  14.4 us (5%)
  Pallas kernels  8.28 us (3%)
    ppermute x1, waiting for transfers between devices, all_rows(): other = lax.ppermute(weights, 'yl', SWAP)  50.8 us
    ppermute x1, waiting for transfers between devices, on_device(): across_y = lax.ppermute(tokens, 'yl', SWAP)  44.1 us
    all_to_all x1, blocking collectives, on_device(): lax.all_to_all(jnp.stack(blocks), 'zh', split_axis=0, concat_axis=0, tile...  25.3 us
    all_to_all x1, blocking collectives, on_device(): rows = lax.all_to_all(rows, 'zh', split_axis=0, concat_axis=0, tiled=True)  23 us
    dot_general x10, matrix products, product(): lax.dot_general(tokens, dense, (((0,), (0,)), ((), ())), preferred_elemen...  14.4 us
    ppermute x3, waiting for transfers between devices, all_rows(): up = lax.ppermute(up, Z, ring(1))  12.9 us
    ppermute x1, waiting for transfers between devices, on_device(): across_top = lax.ppermute(across_y[:half], 'z0', SWAP)  11.2 us
    all_to_all x1, blocking collectives, on_device(): lax.all_to_all(weights.reshape(16, 32, 128), TP, split_axis=0, concat_axi...  10.2 us
  transfers between devices with their start and end apart: 22, of which 12 were waited for; matrix products, arithmetic and copies ran while one was open for 5% of the time, Pallas kernels for 0%

profile of v1, /device:TPU:22, one launch (start us, length us, event | category | flops | bytes accessed | tf_op | source)
XLA Modules:
  0.0 292.9 jit_solution(14065440187120552731)
XLA Ops:
  0.6 1.2 reshape.37
  1.8 0.9 copy.59
  2.7 7.2 %all-to-all-start = ((bf16[16,2,64,128]{3,2,1,0:T(8,128)(2,1)}), bf16[16,2,64,128]{3,2,1,0:T(8,128)(2,1)S(1)}, u32[]{:S(2)}, u32[]{:S(2)}) async-start(bf16[16,2,64,128]{3,2,1,0:T(8,128)(2,1)} %bitcast.93), calls=%async_computation | async-start | bytes 1048576 | tf_op jit(solution)/shard_map/all_to_all | solution.py:192
  9.9 0.6 pad_add_fusion.place_ref
  10.5 6.7 %all-to-all-done = bf16[16,2,64,128]{3,2,1,0:T(8,128)(2,1)S(1)} async-done(((bf16[16,2,64,128]{3,2,1,0:T(8,128)(2,1)}), bf16[16,2,64,128]{3,2,1,0:T(8,128)(2,1)S(1)}, u32[]{:S(2)}, u32[]{:S(2)}) %all-to-all-start) | async-done | bytes 524320 | tf_op jit(solution)/shard_map/all_to_all | solution.py:192
  17.2 0.8 copy-done
  18.0 2.9 pack.1
  20.9 9.5 %all-to-all-start.1 = ((bf16[64,64,256]{2,1,0:T(8,128)(2,1)}), bf16[64,64,256]{2,1,0:T(8,128)(2,1)S(1)}, u32[]{:S(2)}, u32[]{:S(2)}) async-start(bf16[64,64,256]{2,1,0:T(8,128)(2,1)} %bitcast.104), calls=%async_computation.1 | async-start | bytes 4194304 | tf_op jit(solution)/shard_map/all_to_all | solution.py:195
  30.4 1.4 collective-permute-start
  31.9 1.6 collective-permute-start.1
  33.4 44.1 %collective-permute-done = bf16[1024,512]{1,0:T(8,128)(2,1)} collective-permute-done((bf16[1024,512]{1,0:T(8,128)(2,1)}, bf16[1024,512]{1,0:T(8,128)(2,1)}, u32[]{:S(2)}, u32[]{:S(2)}) %collective-permute-start) | collective-permute-done | bytes 1048608 | tf_op jit(solution)/shard_map/ppermute | solution.py:184
  77.6 1.1 slice.48
  78.6 2.9 collective-permute-start.2
  81.6 1.0 collective-permute-start.3
  82.6 11.2 %collective-permute-done.2 = bf16[512,512]{1,0:T(8,128)(2,1)} collective-permute-done((bf16[512,512]{1,0:T(8,128)(2,1)S(1)}, bf16[512,512]{1,0:T(8,128)(2,1)}, u32[]{:S(2)}, u32[]{:S(2)}) %collective-permute-start.2) | collective-permute-done | bytes 524320 | tf_op jit(solution)/shard_map/ppermute | solution.py:186
  93.8 0.5 collective-permute-start.4
  94.3 1.1 collective-permute-done.3
  95.4 0.5 collective-permute-start.5
  95.9 0.1 collective-permute-done.7
  96.0 1.4 fusion.24
  97.4 0.9 collective-permute-done.8
  98.3 1.4 fusion.26
  99.6 1.7 fusion.14
  101.3 1.7 fusion.12
  103.0 1.7 convolution_add_fusion.1
  104.8 1.7 fusion.6
  106.5 1.4 fusion.27
  107.8 1.4 fusion.25
  109.2 1.7 convolution_add_fusion.3
  110.9 0.5 fusion.7
  111.5 25.3 %all_to_all.30 = bf16[4,512,128]{1,2,0:T(8,128)(2,1)S(1)} all-to-all(bf16[4,512,128]{1,2,0:T(8,128)(2,1)S(1)} %pad_maximum_fusion), channel_id=1, replica_groups=mesh['yl'=2,'zh'=4,'z0'=2,'x'=4,'yh'=2,'co'=2] {'zh'}, dimensions={0} | all-to-all | bytes 1048576 | tf_op jit(solution)/shard_map/all_to_all | solution.py:207
  136.9 0.1 reduce_sum.12
  137.0 3.6 %collective-permute-start.9 = (bf16[512,128]{0,1:T(8,128)(2,1)S(1)}, bf16[512,128]{0,1:T(8,128)(2,1)S(1)}, u32[]{:S(2)}, u32[]{:S(2)}) collective-permute-start(bf16[512,128]{0,1:T(8,128)(2,1)S(1)} %reduce_sum.12), channel_id=1, source_target_pairs={{0,0},{1,18},{2,34},{3,48},{4,68},{5,86},{6,102},{7,116},{8,136},{... | collective-permute-start | bytes 393224 | tf_op jit(solution)/shard_map/ppermute | solution.py:209
  140.6 0.1 copy.43
  140.7 0.1 copy.41
  140.9 0.1 copy.39
  141.0 9.4 %collective-permute-done.9 = bf16[512,128]{0,1:T(8,128)(2,1)S(1)} collective-permute-done((bf16[512,128]{0,1:T(8,128)(2,1)S(1)}, bf16[512,128]{0,1:T(8,128)(2,1)S(1)}, u32[]{:S(2)}, u32[]{:S(2)}) %collective-permute-start.9) | collective-permute-done | bytes 131104 | tf_op jit(solution)/shard_map/ppermute | solution.py:209
  150.4 0.2 fusion.38
  150.6 0.1 copy.53
  150.7 10.2 %all_to_all.31 = bf16[16,32,128]{2,1,0:T(8,128)(2,1)S(1)} all-to-all(bf16[16,32,128]{2,1,0:T(8,128)(2,1)S(1)} %bitcast.108), channel_id=1, replica_groups=mesh['yl'=2,'zh'=4,'z0'=2,'x'=4,'yh'=2,'co'=2] {'x','yh','co'}, dimensions={0} | all-to-all | bytes 262144 | tf_op jit(solution)/shard_map/all_to_all | solution.py:214
  161.0 23.0 %all_to_all.32.weights_ref = bf16[4,16,32,128]{3,2,1,0:T(8,128)(2,1)} all-to-all(bf16[4,16,32,128]{3,2,1,0:T(8,128)(2,1)S(1)} %broadcast_in_dim.46), channel_id=1, replica_groups=mesh['yl'=2,'zh'=4,'z0'=2,'x'=4,'yh'=2,'co'=2] {'zh'}, dimensions={0} | all-to-all | bytes 1048576 | tf_op jit(solution)/shard_map/all_to_all | solution.py:216
  184.0 5.4 %unpack.1 = bf16[64,4,32,256]{3,2,1,0:T(8,128)(2,1)} custom-call(s32[2]{0:T(128)} %pad_add_fusion.place_ref, s32[16,16]{1,0:T(8,128)} %lengths_ref.3, bf16[4,16,32,128]{3,2,1,0:T(8,128)(2,1)} %all_to_all.32.weights_ref), custom_call_target="tpu_custom_call" | custom-call | flops 10000000 | bytes 5000000 | tf_op jit(solution)/shard_map/unpack/pallas_call | solution.py:137
  189.4 9.6 %all-to-all-start.5 = ((bf16[64,4,32,256]{3,2,1,0:T(8,128)(2,1)}), bf16[64,4,32,256]{3,2,1,0:T(8,128)(2,1)}, u32[]{:S(2)}, u32[]{:S(2)}) async-start(bf16[64,4,32,256]{3,2,1,0:T(8,128)(2,1)} %unpack.1), calls=%async_computation.5 | async-start | bytes 8388608 | tf_op jit(solution)/shard_map/all_to_all | solution.py:218
  198.9 1.5 collective-permute-start.10
  200.4 50.8 %collective-permute-done.10 = bf16[512,128]{0,1:T(8,128)(2,1)S(1)} collective-permute-done((bf16[512,128]{0,1:T(8,128)(2,1)S(1)}, bf16[512,128]{0,1:T(8,128)(2,1)S(1)}, u32[]{:S(2)}, u32[]{:S(2)}) %collective-permute-start.10) | collective-permute-done | bytes 131104 | tf_op jit(solution)/shard_map/ppermute | solution.py:155
  251.2 4.5 %collective-permute-start.11 = (bf16[2,512,128]{1,2,0:T(8,128)(2,1)S(1)}, bf16[2,512,128]{1,2,0:T(8,128)(2,1)S(1)}, u32[]{:S(2)}, u32[]{:S(2)}) collective-permute-start(bf16[2,512,128]{1,2,0:T(8,128)(2,1)S(1)} %pad_maximum_fusion.1), channel_id=1, source_target_pairs={{0,16},{16,32},{32,48},{48,64},{64,80},{80,96},{96,112},{112,0},{1... | collective-permute-start | bytes 786440 | tf_op jit(solution)/shard_map/ppermute | solution.py:165
  255.8 0.8 copy.55
  256.6 0.8 copy.56
  257.4 0.8 copy.57
  258.3 0.2 broadcast_in_dim.36
  258.5 3.1 %collective-permute-done.11 = bf16[2,512,128]{1,2,0:T(8,128)(2,1)S(1)} collective-permute-done((bf16[2,512,128]{1,2,0:T(8,128)(2,1)S(1)}, bf16[2,512,128]{1,2,0:T(8,128)(2,1)S(1)}, u32[]{:S(2)}, u32[]{:S(2)}) %collective-permute-start.11) | collective-permute-done | bytes 262176 | tf_op jit(solution)/shard_map/ppermute | solution.py:165
  261.6 2.4 collective-permute-start.13
  264.0 1.2 collective-permute-start.14
  265.3 5.2 %collective-permute-done.13 = bf16[2,512,128]{1,2,0:T(8,128)(2,1)S(1)} collective-permute-done((bf16[2,512,128]{1,2,0:T(8,128)(2,1)S(1)}, bf16[2,512,128]{1,2,0:T(8,128)(2,1)S(1)}, u32[]{:S(2)}, u32[]{:S(2)}) %collective-permute-start.13) | collective-permute-done | bytes 262176 | tf_op jit(solution)/shard_map/ppermute | solution.py:165
  270.5 0.9 collective-permute-start.15
  271.5 2.4 collective-permute-start.16
  273.9 4.6 %collective-permute-done.15 = bf16[2,512,128]{1,2,0:T(8,128)(2,1)S(1)} collective-permute-done((bf16[2,512,128]{1,2,0:T(8,128)(2,1)S(1)}, bf16[2,512,128]{1,2,0:T(8,128)(2,1)S(1)}, u32[]{:S(2)}, u32[]{:S(2)}) %collective-permute-start.15) | collective-permute-done | bytes 262176 | tf_op jit(solution)/shard_map/ppermute | solution.py:165
  278.6 0.1 collective-permute-start.17
  278.7 3.3 %collective-permute-start.18 = (bf16[1,512,128]{1,2,0:T(8,128)(2,1)S(1)}, bf16[1,512,128]{1,2,0:T(8,128)(2,1)S(1)}, u32[]{:S(2)}, u32[]{:S(2)}) collective-permute-start(bf16[1,512,128]{1,2,0:T(8,128)(2,1)S(1)} %slice.55), channel_id=1, source_target_pairs={{0,112},{16,0},{32,16},{48,32},{64,48},{80,64},{96,80},{112,96},{1... | collective-permute-start | bytes 393224 | tf_op jit(solution)/shard_map/ppermute | solution.py:170
  282.0 2.8 collective-permute-done.17
  284.9 2.4 copy.51
  287.2 0.1 copy.52
  287.4 0.7 constant_dynamic-update-slice_fusion
  288.0 4.8 %copy.54 = bf16[2,4,2,16,32,256]{5,4,3,2,1,0:T(8,128)(2,1)} copy(bf16[2,4,2,16,32,256]{5,4,1,3,2,0:T(8,128)(2,1)} %bitcast.38) | data formatting | bytes 8388608 | tf_op jit(solution)/shard_map/transpose | solution.py:219
  (38 shorter events, 0.5 us)
Async XLA Ops:
  2.7 14.5 %all-to-all-start = ((bf16[16,2,64,128]{3,2,1,0:T(8,128)(2,1)}), bf16[16,2,64,128]{3,2,1,0:T(8,128)(2,1)S(1)}, u32[]{:S(2)}, u32[]{:S(2)}) async-start(bf16[16,2,64,128]{3,2,1,0:T(8,128)(2,1)} %bitcast.93), calls=%async_computation | async-start | bytes 1048576 | tf_op jit(solution)/shard_map/all_to_all | solution.py:192
  17.2 0.8 copy-start
  20.9 75.1 %all-to-all-start.1 = ((bf16[64,64,256]{2,1,0:T(8,128)(2,1)}), bf16[64,64,256]{2,1,0:T(8,128)(2,1)S(1)}, u32[]{:S(2)}, u32[]{:S(2)}) async-start(bf16[64,64,256]{2,1,0:T(8,128)(2,1)} %bitcast.104), calls=%async_computation.1 | async-start | bytes 4194304 | tf_op jit(solution)/shard_map/all_to_all | solution.py:195
  30.4 47.1 %collective-permute-start = (bf16[1024,512]{1,0:T(8,128)(2,1)}, bf16[1024,512]{1,0:T(8,128)(2,1)}, u32[]{:S(2)}, u32[]{:S(2)}) collective-permute-start(bf16[1024,512]{1,0:T(8,128)(2,1)} %param.6), channel_id=1, source_target_pairs={{0,128},{128,0},{1,129},{129,1},{2,130},{130,2},{3,131},{131,3},{4... | collective-permute-start | bytes 3145736 | tf_op jit(solution)/shard_map/ppermute | solution.py:184
  31.9 49.7 %collective-permute-start.1 = (bf16[1024,512]{1,0:T(8,128)(2,1)}, bf16[1024,512]{1,0:T(8,128)(2,1)S(1)}, u32[]{:S(2)}, u32[]{:S(2)}) collective-permute-start(bf16[1024,512]{1,0:T(8,128)(2,1)} %param.6), channel_id=1, source_target_pairs={{0,16},{16,0},{1,17},{17,1},{2,18},{18,2},{3,19},{19,3},{4,20},{20... | collective-permute-start | bytes 3145736 | tf_op jit(solution)/shard_map/ppermute | solution.py:185
  78.6 15.1 %collective-permute-start.2 = (bf16[512,512]{1,0:T(8,128)(2,1)S(1)}, bf16[512,512]{1,0:T(8,128)(2,1)}, u32[]{:S(2)}, u32[]{:S(2)}) collective-permute-start(bf16[512,512]{1,0:T(8,128)(2,1)S(1)} %slice.48), channel_id=1, source_target_pairs={{0,16},{16,0},{1,17},{17,1},{2,18},{18,2},{3,19},{19,3},{4,20},{20... | collective-permute-start | bytes 1572872 | tf_op jit(solution)/shard_map/ppermute | solution.py:186
  81.6 13.8 %collective-permute-start.3 = (bf16[512,512]{1,0:T(8,128)(2,1)S(1)}, bf16[512,512]{1,0:T(8,128)(2,1)}, u32[]{:S(2)}, u32[]{:S(2)}) collective-permute-start(bf16[512,512]{1,0:T(8,128)(2,1)S(1)} %slice.49), channel_id=1, source_target_pairs={{0,128},{128,0},{1,129},{129,1},{2,130},{130,2},{3,131},{131,3},{4... | collective-permute-start | bytes 1572872 | tf_op jit(solution)/shard_map/ppermute | solution.py:187
  93.8 2.3 collective-permute-start.7
  93.8 7.6 %collective-permute-start.4 = (bf16[1024,512]{1,0:T(8,128)(2,1)}, bf16[1024,512]{1,0:T(8,128)(2,1)}, u32[]{:S(2)}, u32[]{:S(2)}) collective-permute-start(bf16[1024,512]{1,0:T(8,128)(2,1)} %param.6), channel_id=1, source_target_pairs={{0,1},{1,0},{2,3},{3,2},{4,5},{5,4},{6,7},{7,6},{8,9},{9,8},{10,11... | collective-permute-start | bytes 3145736 | tf_op jit(solution)/shard_map/ppermute | solution.py:189
  95.4 2.9 collective-permute-start.8
  95.4 7.7 %collective-permute-start.5 = (bf16[1024,512]{1,0:T(8,128)(2,1)}, bf16[1024,512]{1,0:T(8,128)(2,1)}, u32[]{:S(2)}, u32[]{:S(2)}) collective-permute-start(bf16[1024,512]{1,0:T(8,128)(2,1)} %collective-permute-done), channel_id=1, source_target_pairs={{0,1},{1,0},{2,3},{3,2},{4,5},{5,4},{6,7},{7,6},{8,9},{9,8},{10,11... | collective-permute-start | bytes 3145736 | tf_op jit(solution)/shard_map/ppermute | solution.py:189
  95.9 8.9 %collective-permute-start.6 = (bf16[1024,512]{1,0:T(8,128)(2,1)S(1)}, bf16[1024,512]{1,0:T(8,128)(2,1)}, u32[]{:S(2)}, u32[]{:S(2)}) collective-permute-start(bf16[1024,512]{1,0:T(8,128)(2,1)S(1)} %collective-permute-done.1), channel_id=1, source_target_pairs={{0,1},{1,0},{2,3},{3,2},{4,5},{5,4},{6,7},{7,6},{8,9},{9,8},{10,11... | collective-permute-start | bytes 3145736 | tf_op jit(solution)/shard_map/ppermute | solution.py:189
  111.4 29.2 %copy-start.1 = (f32[512,128]{1,0:T(8,128)S(1)}, f32[512,128]{1,0:T(8,128)}, u32[]{:S(2)}) copy-start(f32[512,128]{1,0:T(8,128)} %param.9) | copy-start | bytes 786436
  111.4 29.3 %copy-start.2 = (f32[512,128]{1,0:T(8,128)S(1)}, f32[512,128]{1,0:T(8,128)}, u32[]{:S(2)}) copy-start(f32[512,128]{1,0:T(8,128)} %param.11) | copy-start | bytes 786436
  111.4 29.4 %copy-start.3 = (f32[512,128]{1,0:T(8,128)S(1)}, f32[512,128]{1,0:T(8,128)}, u32[]{:S(2)}) copy-start(f32[512,128]{1,0:T(8,128)} %param.10) | copy-start | bytes 786436
  137.0 13.4 %collective-permute-start.9 = (bf16[512,128]{0,1:T(8,128)(2,1)S(1)}, bf16[512,128]{0,1:T(8,128)(2,1)S(1)}, u32[]{:S(2)}, u32[]{:S(2)}) collective-permute-start(bf16[512,128]{0,1:T(8,128)(2,1)S(1)} %reduce_sum.12), channel_id=1, source_target_pairs={{0,0},{1,18},{2,34},{3,48},{4,68},{5,86},{6,102},{7,116},{8,136},{... | collective-permute-start | bytes 393224 | tf_op jit(solution)/shard_map/ppermute | solution.py:209
  189.4 98.7 %all-to-all-start.5 = ((bf16[64,4,32,256]{3,2,1,0:T(8,128)(2,1)}), bf16[64,4,32,256]{3,2,1,0:T(8,128)(2,1)}, u32[]{:S(2)}, u32[]{:S(2)}) async-start(bf16[64,4,32,256]{3,2,1,0:T(8,128)(2,1)} %unpack.1), calls=%async_computation.5 | async-start | bytes 8388608 | tf_op jit(solution)/shard_map/all_to_all | solution.py:218
  198.9 52.2 %collective-permute-start.10 = (bf16[512,128]{0,1:T(8,128)(2,1)S(1)}, bf16[512,128]{0,1:T(8,128)(2,1)S(1)}, u32[]{:S(2)}, u32[]{:S(2)}) collective-permute-start(bf16[512,128]{0,1:T(8,128)(2,1)S(1)} %get-tuple-element.15), channel_id=1, source_target_pairs={{0,128},{128,0},{1,129},{129,1},{2,130},{130,2},{3,131},{131,3},{4... | collective-permute-start | bytes 393224 | tf_op jit(solution)/shard_map/ppermute | solution.py:155
  251.2 10.4 %collective-permute-start.11 = (bf16[2,512,128]{1,2,0:T(8,128)(2,1)S(1)}, bf16[2,512,128]{1,2,0:T(8,128)(2,1)S(1)}, u32[]{:S(2)}, u32[]{:S(2)}) collective-permute-start(bf16[2,512,128]{1,2,0:T(8,128)(2,1)S(1)} %pad_maximum_fusion.1), channel_id=1, source_target_pairs={{0,16},{16,32},{32,48},{48,64},{64,80},{80,96},{96,112},{112,0},{1... | collective-permute-start | bytes 786440 | tf_op jit(solution)/shard_map/ppermute | solution.py:165
  255.8 8.3 %collective-permute-start.12 = (bf16[2,512,128]{1,2,0:T(8,128)(2,1)S(1)}, bf16[2,512,128]{1,2,0:T(8,128)(2,1)S(1)}, u32[]{:S(2)}, u32[]{:S(2)}) collective-permute-start(bf16[2,512,128]{1,2,0:T(8,128)(2,1)S(1)} %pad_maximum_fusion.1), channel_id=1, source_target_pairs={{0,112},{16,0},{32,16},{48,32},{64,48},{80,64},{96,80},{112,96},{1... | collective-permute-start | bytes 786440 | tf_op jit(solution)/shard_map/ppermute | solution.py:166
  261.6 8.9 %collective-permute-start.13 = (bf16[2,512,128]{1,2,0:T(8,128)(2,1)S(1)}, bf16[2,512,128]{1,2,0:T(8,128)(2,1)S(1)}, u32[]{:S(2)}, u32[]{:S(2)}) collective-permute-start(bf16[2,512,128]{1,2,0:T(8,128)(2,1)S(1)} %collective-permute-done.11), channel_id=1, source_target_pairs={{0,16},{16,32},{32,48},{48,64},{64,80},{80,96},{96,112},{112,0},{1... | collective-permute-start | bytes 786440 | tf_op jit(solution)/shard_map/ppermute | solution.py:165
  264.0 7.4 %collective-permute-start.14 = (bf16[2,512,128]{1,2,0:T(8,128)(2,1)S(1)}, bf16[2,512,128]{1,2,0:T(8,128)(2,1)S(1)}, u32[]{:S(2)}, u32[]{:S(2)}) collective-permute-start(bf16[2,512,128]{1,2,0:T(8,128)(2,1)S(1)} %collective-permute-done.12), channel_id=1, source_target_pairs={{0,112},{16,0},{32,16},{48,32},{64,48},{80,64},{96,80},{112,96},{1... | collective-permute-start | bytes 786440 | tf_op jit(solution)/shard_map/ppermute | solution.py:166
  270.5 8.1 %collective-permute-start.15 = (bf16[2,512,128]{1,2,0:T(8,128)(2,1)S(1)}, bf16[2,512,128]{1,2,0:T(8,128)(2,1)S(1)}, u32[]{:S(2)}, u32[]{:S(2)}) collective-permute-start(bf16[2,512,128]{1,2,0:T(8,128)(2,1)S(1)} %collective-permute-done.13), channel_id=1, source_target_pairs={{0,16},{16,32},{32,48},{48,64},{64,80},{80,96},{96,112},{112,0},{1... | collective-permute-start | bytes 786440 | tf_op jit(solution)/shard_map/ppermute | solution.py:165
  271.5 7.2 %collective-permute-start.16 = (bf16[2,512,128]{1,2,0:T(8,128)(2,1)S(1)}, bf16[2,512,128]{1,2,0:T(8,128)(2,1)S(1)}, u32[]{:S(2)}, u32[]{:S(2)}) collective-permute-start(bf16[2,512,128]{1,2,0:T(8,128)(2,1)S(1)} %collective-permute-done.14), channel_id=1, source_target_pairs={{0,112},{16,0},{32,16},{48,32},{64,48},{80,64},{96,80},{112,96},{1... | collective-permute-start | bytes 786440 | tf_op jit(solution)/shard_map/ppermute | solution.py:166
  278.6 6.3 %collective-permute-start.17 = (bf16[1,512,128]{1,2,0:T(8,128)(2,1)S(1)}, bf16[1,512,128]{1,2,0:T(8,128)(2,1)S(1)}, u32[]{:S(2)}, u32[]{:S(2)}) collective-permute-start(bf16[1,512,128]{1,2,0:T(8,128)(2,1)S(1)} %slice.54), channel_id=1, source_target_pairs={{0,16},{16,32},{32,48},{48,64},{64,80},{80,96},{96,112},{112,0},{1... | collective-permute-start | bytes 393224 | tf_op jit(solution)/shard_map/ppermute | solution.py:169
  278.7 8.5 %collective-permute-start.18 = (bf16[1,512,128]{1,2,0:T(8,128)(2,1)S(1)}, bf16[1,512,128]{1,2,0:T(8,128)(2,1)S(1)}, u32[]{:S(2)}, u32[]{:S(2)}) collective-permute-start(bf16[1,512,128]{1,2,0:T(8,128)(2,1)S(1)} %slice.55), channel_id=1, source_target_pairs={{0,112},{16,0},{32,16},{48,32},{64,48},{80,64},{96,80},{112,96},{1... | collective-permute-start | bytes 393224 | tf_op jit(solution)/shard_map/ppermute | solution.py:170

commit v2 on v1

--- a/solution.py
+++ b/solution.py
@@ -12,7 +12,9 @@
 REP = ("yl", "zh", "z0")
 TP = ("x", "yh", "co")
 Z = ("zh", "z0")
+PAIR = ("z0", "x", "yh", "co")
 GROUP = ("yl", "z0", "x", "yh", "co")
+SUM = ("yl", "zh")
 SWAP = [(0, 1), (1, 0)]
 
 decay_first = 0.9
@@ -32,8 +34,12 @@
     return (new_master, new_first, new_second)
 
 
-def column_block(yl, z0, co, x, yh):
-    return 4 * (yl ^ (x >> 1)) + 2 * (z0 ^ (x & 1)) + (co ^ yh)
+def sum_block(yl, zh):
+    return zh // 2, 2 * yl + zh % 2
+
+
+def column_block(z0, co, x, yh):
+    return 2 * (z0 ^ (x % 2)) + (co ^ (x % 2) ^ yh)
 
 
 def home_permutation():
@@ -44,10 +50,10 @@
                 for x in range(4):
                     for yh in range(2):
                         for co in range(2):
-                            half, right = zh >> 1, zh & 1
+                            half, part = sum_block(yl, zh)
                             source = ((((yl * 4 + zh) * 2 + z0) * 4 + x) * 2 + yh) * 2 + co
                             row = 4 * x + 2 * yh + (co ^ half)
-                            col = 2 * column_block(yl, z0, co, x, yh) + right
+                            col = 4 * column_block(z0, co, x, yh) + part
                             pairs.append((source, row * 16 + col))
     return pairs
 
@@ -68,21 +74,24 @@
                 table_ref[begin + k] = jnp.int32(4 * j + k)
 
         begin = begin + count
-    lane = lax.broadcasted_iota(jnp.int32, slots_ref.shape[1:], 1)
+    lane = lax.broadcasted_iota(jnp.int32, (slots_ref.shape[1], 128), 1)
+
+    def tile_of(unit):
+        return slots_ref[unit // 4, :, pl.ds(pl.multiple_of((unit // 2) % 2 * 128, 128), 128)]
+
     for d in range(16):
         left, right = table_ref[2 * d], table_ref[2 * d + 1]
-        tile_l, tile_r = slots_ref[left // 2], slots_ref[right // 2]
+        tile_l, tile_r = tile_of(left), tile_of(right)
         low = jnp.where(left % 2 == 0, tile_l.astype(jnp.float32), swapped_halves(tile_l))
         high = jnp.where(right % 2 == 1, tile_r.astype(jnp.float32), swapped_halves(tile_r))
         dense = jnp.where(lane < UNIT, low, high).astype(out_ref.dtype)
-        block, part = d // 2, 128 * (d % 2)
+        block, part = d // 4, 128 * (d % 4)
         for x in range(4):
             for yh in range(2):
-                for yl in range(2):
-                    for z0 in range(2):
-                        for co in range(2):
-                            if column_block(yl, z0, co, x, yh) == block:
-                                out_ref[yl, z0, 2 * x + yh, co, :, part : part + 128] = dense
+                for z0 in range(2):
+                    for co in range(2):
+                        if column_block(z0, co, x, yh) == block:
+                            out_ref[z0, 2 * x + yh, co, :, part : part + 128] = dense
 
 
 def packed_columns(slots, lengths, place):
@@ -91,7 +100,7 @@
     vmem = pl.BlockSpec(memory_space=pltpu.VMEM)
     return pl.pallas_call(
         pack_kernel,
-        out_shape=jax.ShapeDtypeStruct((2, 2, 8, 2, tokens, 256), slots.dtype),
+        out_shape=jax.ShapeDtypeStruct((2, 8, 2, tokens, 512), slots.dtype),
         in_specs=[smem, smem, vmem],
         out_specs=vmem,
         scratch_shapes=[pltpu.SMEM((32,), jnp.int32)],
@@ -166,8 +175,10 @@
         down = lax.ppermute(down, Z, ring(-1))
         out = put(out, up, 0, 8 - k)
         out = put(out, down, 0, k)
-    out = put(out, lax.ppermute(up[:1], Z, ring(1)), 0, 4)
-    out = put(out, lax.ppermute(down[1:], Z, ring(-1)), 1, 4)
+    up = lax.ppermute(up[:1], Z, ring(1))
+    down = lax.ppermute(down[1:], Z, ring(-1))
+    out = put(out, up, 0, 4)
+    out = put(out, down, 1, 4)
     return out.reshape(-1, weights.shape[1])
 
 
@@ -176,35 +187,30 @@
 
 
 def on_device(tokens, grad_out, lengths, master, first, second):
-    yl, z0 = lax.axis_index("yl"), lax.axis_index("z0")
+    z0 = lax.axis_index("z0")
     place = jnp.stack([lax.axis_index(REP), lax.axis_index("zh")]).astype(jnp.int32)
     token_count, slot_width = grad_out.shape
-    half = token_count // 2
-
-    across_y = lax.ppermute(tokens, "yl", SWAP)
-    across_z = lax.ppermute(tokens, "z0", SWAP)
-    across_top = lax.ppermute(across_y[:half], "z0", SWAP)
-    across_bottom = lax.ppermute(across_z[half:], "yl", SWAP)
-    own = [tokens, across_y, across_z, across_top, across_bottom]
+
+    across = lax.ppermute(tokens, "z0", SWAP)
+    own = [tokens, across]
     theirs = [lax.ppermute(part, "co", SWAP) for part in own]
 
-    parts = jnp.swapaxes(grad_out.reshape(16, token_count // 16, 2, 128), 1, 2)
+    parts = grad_out.reshape(16, token_count // 16, slot_width)
     slots = lax.all_to_all(parts, TP, split_axis=0, concat_axis=0, tiled=True)
-    spread = packed_columns(slots.reshape(32, token_count // 16, 128), lengths, place)
-    spread = spread.reshape(64, token_count // 16, 256)
-    dense = lax.all_to_all(spread, GROUP, split_axis=0, concat_axis=0, tiled=True)
-    dense = dense.reshape(4, token_count, 256)
-    d00, d10, d01, d11 = (
-        lax.dynamic_index_in_dim(dense, 2 * (yl ^ a) + (z0 ^ b), 0, False)
-        for a, b in ((0, 0), (1, 0), (0, 1), (1, 1))
-    )
-    columns = [d00, d10, d01, d11[:half], d11[half:]]
+    spread = packed_columns(slots, lengths, place).reshape(32, token_count // 16, 512)
+    dense = lax.all_to_all(spread, PAIR, split_axis=0, concat_axis=0, tiled=True)
+    dense = dense.reshape(2, token_count, 512)
+    columns = [lax.dynamic_index_in_dim(dense, z0 ^ k, 0, False) for k in range(2)]
+    totals = [
+        sum(product(t, d) for t, d in zip(features, columns)).astype(jnp.bfloat16)
+        for features in (own, theirs)
+    ]
     blocks = []
-    for features in (own, theirs):
-        total = sum(product(t, d) for t, d in zip(features, columns))
-        total = total.astype(jnp.bfloat16)
-        blocks += [total[:, :128], total[:, 128:]]
-    arrived = lax.all_to_all(jnp.stack(blocks), "zh", split_axis=0, concat_axis=0, tiled=True)
+    for yl in range(2):
+        for zh in range(4):
+            half, part = sum_block(yl, zh)
+            blocks.append(totals[half][:, 128 * part : 128 * (part + 1)])
+    arrived = lax.all_to_all(jnp.stack(blocks), SUM, split_axis=0, concat_axis=0, tiled=True)
     summed = jnp.sum(arrived.astype(jnp.float32), axis=0).astype(jnp.bfloat16)
     gradient = lax.ppermute(summed, AXES, home_permutation()).astype(jnp.float32)
 

time: 294 us -> 278 us (0.946)
  the two profiles are of different devices: /device:TPU:22 before, /device:TPU:118 now
where the time goes in v2:
time: 278 us
  waiting for transfers between devices  134 us (48%)
  blocking collectives  67 us (24%)
  starting transfers between devices  44.6 us (16%)
  local copies, waits for them, and re-layouts  13.3 us (5%)
  Pallas kernels  8.45 us (3%)
  matrix products  7.84 us (3%)
    ppermute x1, waiting for transfers between devices, all_rows(): other = lax.ppermute(weights, 'yl', SWAP)  53.7 us
    ppermute x1, waiting for transfers between devices, on_device(): across = lax.ppermute(tokens, 'z0', SWAP)  46.5 us
    all_to_all x1, blocking collectives, on_device(): lax.all_to_all(jnp.stack(blocks), SUM, split_axis=0, concat_axis=0, tiled...  32.4 us
    all_to_all x1, blocking collectives, on_device(): rows = lax.all_to_all(rows, 'zh', split_axis=0, concat_axis=0, tiled=True)  22.8 us
    ppermute x3, waiting for transfers between devices, all_rows(): up = lax.ppermute(up, Z, ring(1))  12.7 us
    all_to_all x1, blocking collectives, on_device(): lax.all_to_all(weights.reshape(16, 32, 128), TP, split_axis=0, concat_axi...  11.8 us
    all_to_all x1, starting transfers between devices, on_device(): lax.all_to_all(outgoing, GROUP, split_axis=0, concat_axis=0, tiled=True)  10.7 us
    all_to_all x1, starting transfers between devices, on_device(): lax.all_to_all(spread, PAIR, split_axis=0, concat_axis=0, tiled=True)  8.7 us
  transfers between devices with their start and end apart: 16, of which 8 were waited for; matrix products, arithmetic and copies ran while one was open for 5% of the time, Pallas kernels for 0%

profile of v2, /device:TPU:118, one launch (start us, length us, event | category | flops | bytes accessed | tf_op | source)
XLA Modules:
  0.0 277.5 jit_solution(2709357800005516797)
XLA Ops:
  0.6 7.2 %all-to-all-start = ((bf16[16,64,256]{2,1,0:T(8,128)(2,1)}), bf16[16,64,256]{2,1,0:T(8,128)(2,1)S(1)}, u32[]{:S(2)}, u32[]{:S(2)}) async-start(bf16[16,64,256]{2,1,0:T(8,128)(2,1)} %bitcast.103), calls=%async_computation | async-start | bytes 1048576 | tf_op jit(solution)/shard_map/all_to_all | solution.py:199
  7.8 0.6 pad_add_fusion.place_ref
  8.4 6.7 %all-to-all-done.slots_ref = bf16[16,64,256]{2,1,0:T(8,128)(2,1)S(1)} async-done(((bf16[16,64,256]{2,1,0:T(8,128)(2,1)}), bf16[16,64,256]{2,1,0:T(8,128)(2,1)S(1)}, u32[]{:S(2)}, u32[]{:S(2)}) %all-to-all-start) | async-done | bytes 524320 | tf_op jit(solution)/shard_map/all_to_all | solution.py:199
  15.1 0.8 copy-done
  15.9 3.1 %pack.1 = bf16[2,8,2,64,512]{4,3,2,1,0:T(8,128)(2,1)} custom-call(s32[2]{0:T(128)} %pad_add_fusion.place_ref, s32[16,16]{1,0:T(8,128)} %lengths_ref.3, bf16[16,64,256]{2,1,0:T(8,128)(2,1)} %copy-done), custom_call_target="tpu_custom_call" | custom-call | flops 1000000 | bytes 5000000 | tf_op jit(solution)/shard_map/pack/pallas_call | solution.py:101
  19.0 8.7 %all-to-all-start.1 = ((bf16[32,64,512]{2,1,0:T(8,128)(2,1)}), bf16[32,64,512]{2,1,0:T(8,128)(2,1)S(1)}, u32[]{:S(2)}, u32[]{:S(2)}) async-start(bf16[32,64,512]{2,1,0:T(8,128)(2,1)} %bitcast.96), calls=%async_computation.1 | async-start | bytes 4194304 | tf_op jit(solution)/shard_map/all_to_all | solution.py:201
  27.7 0.6 collective-permute-start
  28.3 0.0 collective-permute-start.1
  28.3 46.5 %collective-permute-done = bf16[1024,512]{1,0:T(8,128)(2,1)} collective-permute-done((bf16[1024,512]{1,0:T(8,128)(2,1)}, bf16[1024,512]{1,0:T(8,128)(2,1)}, u32[]{:S(2)}, u32[]{:S(2)}) %collective-permute-start) | collective-permute-done | bytes 1048608 | tf_op jit(solution)/shard_map/ppermute | solution.py:194
  74.8 0.0 collective-permute-start.2
  74.8 0.0 all-to-all-done.1
  74.9 2.0 fusion.8
  76.8 2.0 fusion.3
  78.8 0.0 collective-permute-done.1
  78.8 2.0 fusion.6
  80.8 0.0 collective-permute-done.2
  80.8 2.0 fusion.2
  82.8 0.0 copy-start.1
  82.9 0.0 copy-start.2
  82.9 0.0 copy-start.3
  82.9 32.4 %all_to_all.30 = bf16[8,512,128]{1,2,0:T(8,128)(2,1)S(1)} all-to-all(bf16[8,512,128]{1,2,0:T(8,128)(2,1)S(1)} %fusion.16), channel_id=1, replica_groups=mesh['yl'=2,'zh'=4,'z0'=2,'x'=4,'yh'=2,'co'=2] {'yl','zh'}, dimensions={0} | all-to-all | bytes 2097152 | tf_op jit(solution)/shard_map/all_to_all | solution.py:213
  115.4 0.1 reduce_sum.12
  115.5 5.0 %collective-permute-start.3 = (bf16[512,128]{0,1:T(8,128)(2,1)S(1)}, bf16[512,128]{0,1:T(8,128)(2,1)S(1)}, u32[]{:S(2)}, u32[]{:S(2)}) collective-permute-start(bf16[512,128]{0,1:T(8,128)(2,1)S(1)} %reduce_sum.12), channel_id=1, source_target_pairs={{0,0},{1,20},{2,36},{3,48},{4,76},{5,88},{6,104},{7,124},{8,128},{... | collective-permute-start | bytes 393224 | tf_op jit(solution)/shard_map/ppermute | solution.py:215
  120.5 0.1 copy.40
  120.7 0.0 copy-done.2
  120.7 0.1 copy.37
  120.8 0.1 copy.38
  121.0 7.9 %collective-permute-done.3 = bf16[512,128]{0,1:T(8,128)(2,1)S(1)} collective-permute-done((bf16[512,128]{0,1:T(8,128)(2,1)S(1)}, bf16[512,128]{0,1:T(8,128)(2,1)S(1)}, u32[]{:S(2)}, u32[]{:S(2)}) %collective-permute-start.3) | collective-permute-done | bytes 131104 | tf_op jit(solution)/shard_map/ppermute | solution.py:215
  128.9 0.2 fusion.28
  129.1 0.1 copy.50
  129.2 11.8 %all_to_all.31 = bf16[16,32,128]{2,1,0:T(8,128)(2,1)S(1)} all-to-all(bf16[16,32,128]{2,1,0:T(8,128)(2,1)S(1)} %bitcast.104), channel_id=1, replica_groups=mesh['yl'=2,'zh'=4,'z0'=2,'x'=4,'yh'=2,'co'=2] {'x','yh','co'}, dimensions={0} | all-to-all | bytes 262144 | tf_op jit(solution)/shard_map/all_to_all | solution.py:220
  141.0 0.1 broadcast_in_dim.46
  141.1 22.8 %all_to_all.32.weights_ref = bf16[4,16,32,128]{3,2,1,0:T(8,128)(2,1)} all-to-all(bf16[4,16,32,128]{3,2,1,0:T(8,128)(2,1)S(1)} %broadcast_in_dim.46), channel_id=1, replica_groups=mesh['yl'=2,'zh'=4,'z0'=2,'x'=4,'yh'=2,'co'=2] {'zh'}, dimensions={0} | all-to-all | bytes 1048576 | tf_op jit(solution)/shard_map/all_to_all | solution.py:222
  163.9 5.4 %unpack.1 = bf16[64,4,32,256]{3,2,1,0:T(8,128)(2,1)} custom-call(s32[2]{0:T(128)} %pad_add_fusion.place_ref, s32[16,16]{1,0:T(8,128)} %lengths_ref.3, bf16[4,16,32,128]{3,2,1,0:T(8,128)(2,1)} %all_to_all.32.weights_ref), custom_call_target="tpu_custom_call" | custom-call | flops 10000000 | bytes 5000000 | tf_op jit(solution)/shard_map/unpack/pallas_call | solution.py:146
  169.3 10.7 %all-to-all-start.5 = ((bf16[64,4,32,256]{3,2,1,0:T(8,128)(2,1)}), bf16[64,4,32,256]{3,2,1,0:T(8,128)(2,1)}, u32[]{:S(2)}, u32[]{:S(2)}) async-start(bf16[64,4,32,256]{3,2,1,0:T(8,128)(2,1)} %unpack.1), calls=%async_computation.5 | async-start | bytes 8388608 | tf_op jit(solution)/shard_map/all_to_all | solution.py:224
  180.0 1.5 collective-permute-start.4
  181.5 53.7 %collective-permute-done.4 = bf16[512,128]{0,1:T(8,128)(2,1)S(1)} collective-permute-done((bf16[512,128]{0,1:T(8,128)(2,1)S(1)}, bf16[512,128]{0,1:T(8,128)(2,1)S(1)}, u32[]{:S(2)}, u32[]{:S(2)}) %collective-permute-start.4) | collective-permute-done | bytes 131104 | tf_op jit(solution)/shard_map/ppermute | solution.py:164
  235.2 0.7 pad_maximum_fusion
  235.9 0.0 collective-permute-start.5
  235.9 2.0 collective-permute-start.6
  237.9 0.8 copy.52
  238.8 0.8 copy.54
  239.6 0.8 copy.53
  240.4 0.2 broadcast_in_dim.36
  240.7 3.8 %collective-permute-done.5 = bf16[2,512,128]{1,2,0:T(8,128)(2,1)} collective-permute-done((bf16[2,512,128]{1,2,0:T(8,128)(2,1)}, bf16[2,512,128]{1,2,0:T(8,128)(2,1)}, u32[]{:S(2)}, u32[]{:S(2)}) %collective-permute-start.5) | collective-permute-done | bytes 262176 | tf_op jit(solution)/shard_map/ppermute | solution.py:174
  244.5 1.5 collective-permute-start.7
  246.0 0.0 collective-permute-done.6
  246.0 0.5 collective-permute-start.8
  246.5 1.0 bitcast_dynamic-update-slice_fusion.5
  247.5 4.6 %collective-permute-done.7 = bf16[2,512,128]{1,2,0:T(8,128)(2,1)S(1)} collective-permute-done((bf16[2,512,128]{1,2,0:T(8,128)(2,1)}, bf16[2,512,128]{1,2,0:T(8,128)(2,1)S(1)}, u32[]{:S(2)}, u32[]{:S(2)}) %collective-permute-start.7) | collective-permute-done | bytes 262176 | tf_op jit(solution)/shard_map/ppermute | solution.py:174
  252.1 3.0 %collective-permute-start.9 = (bf16[2,512,128]{1,2,0:T(8,128)(2,1)S(1)}, bf16[2,512,128]{1,2,0:T(8,128)(2,1)S(1)}, u32[]{:S(2)}, u32[]{:S(2)}) collective-permute-start(bf16[2,512,128]{1,2,0:T(8,128)(2,1)S(1)} %collective-permute-done.7), channel_id=1, source_target_pairs={{0,16},{16,32},{32,48},{48,64},{64,80},{80,96},{96,112},{112,0},{1... | collective-permute-start | bytes 786440 | tf_op jit(solution)/shard_map/ppermute | solution.py:174
  255.1 0.0 collective-permute-done.8
  255.1 0.0 collective-permute-start.10
  255.2 4.3 %collective-permute-done.9 = bf16[2,512,128]{1,2,0:T(8,128)(2,1)S(1)} collective-permute-done((bf16[2,512,128]{1,2,0:T(8,128)(2,1)S(1)}, bf16[2,512,128]{1,2,0:T(8,128)(2,1)S(1)}, u32[]{:S(2)}, u32[]{:S(2)}) %collective-permute-start.9) | collective-permute-done | bytes 262176 | tf_op jit(solution)/shard_map/ppermute | solution.py:174
  259.5 3.8 %collective-permute-start.11 = (bf16[1,512,128]{1,2,0:T(8,128)(2,1)S(1)}, bf16[1,512,128]{1,2,0:T(8,128)(2,1)S(1)}, u32[]{:S(2)}, u32[]{:S(2)}) collective-permute-start(bf16[1,512,128]{1,2,0:T(8,128)(2,1)S(1)} %slice.48), channel_id=1, source_target_pairs={{0,16},{16,32},{32,48},{48,64},{64,80},{80,96},{96,112},{112,0},{1... | collective-permute-start | bytes 393224 | tf_op jit(solution)/shard_map/ppermute | solution.py:178
  263.2 0.0 collective-permute-done.10
  263.3 0.1 collective-permute-start.12
  263.4 6.1 %collective-permute-done.12 = bf16[1,512,128]{1,2,0:T(8,128)(2,1)S(1)} collective-permute-done((bf16[1,512,128]{1,2,0:T(8,128)(2,1)S(1)}, bf16[1,512,128]{1,2,0:T(8,128)(2,1)S(1)}, u32[]{:S(2)}, u32[]{:S(2)}) %collective-permute-start.12) | collective-permute-done | bytes 131104 | tf_op jit(solution)/shard_map/ppermute | solution.py:179
  269.5 0.1 copy.49
  269.6 0.0 collective-permute-done.11
  269.7 2.4 copy.48
  272.0 0.7 constant_dynamic-update-slice_fusion
  272.7 0.0 all-to-all-done.5
  272.7 4.8 %copy.51 = bf16[2,4,2,16,32,256]{5,4,3,2,1,0:T(8,128)(2,1)} copy(bf16[2,4,2,16,32,256]{5,4,1,3,2,0:T(8,128)(2,1)} %bitcast.38) | data formatting | bytes 8388608 | tf_op jit(solution)/shard_map/transpose | solution.py:225
  (21 shorter events, 0.3 us)
Async XLA Ops:
  0.6 14.5 %all-to-all-start = ((bf16[16,64,256]{2,1,0:T(8,128)(2,1)}), bf16[16,64,256]{2,1,0:T(8,128)(2,1)S(1)}, u32[]{:S(2)}, u32[]{:S(2)}) async-start(bf16[16,64,256]{2,1,0:T(8,128)(2,1)} %bitcast.103), calls=%async_computation | async-start | bytes 1048576 | tf_op jit(solution)/shard_map/all_to_all | solution.py:199
  15.1 0.8 copy-start
  19.0 55.8 %all-to-all-start.1 = ((bf16[32,64,512]{2,1,0:T(8,128)(2,1)}), bf16[32,64,512]{2,1,0:T(8,128)(2,1)S(1)}, u32[]{:S(2)}, u32[]{:S(2)}) async-start(bf16[32,64,512]{2,1,0:T(8,128)(2,1)} %bitcast.96), calls=%async_computation.1 | async-start | bytes 4194304 | tf_op jit(solution)/shard_map/all_to_all | solution.py:201
  27.7 47.1 %collective-permute-start = (bf16[1024,512]{1,0:T(8,128)(2,1)}, bf16[1024,512]{1,0:T(8,128)(2,1)}, u32[]{:S(2)}, u32[]{:S(2)}) collective-permute-start(bf16[1024,512]{1,0:T(8,128)(2,1)} %param.6), channel_id=1, source_target_pairs={{0,16},{16,0},{1,17},{17,1},{2,18},{18,2},{3,19},{19,3},{4,20},{20... | collective-permute-start | bytes 3145736 | tf_op jit(solution)/shard_map/ppermute | solution.py:194
  28.3 50.5 %collective-permute-start.1 = (bf16[1024,512]{1,0:T(8,128)(2,1)}, bf16[1024,512]{1,0:T(8,128)(2,1)}, u32[]{:S(2)}, u32[]{:S(2)}) collective-permute-start(bf16[1024,512]{1,0:T(8,128)(2,1)} %param.6), channel_id=1, source_target_pairs={{0,1},{1,0},{2,3},{3,2},{4,5},{5,4},{6,7},{7,6},{8,9},{9,8},{10,11... | collective-permute-start | bytes 3145736 | tf_op jit(solution)/shard_map/ppermute | solution.py:196
  74.8 5.9 %collective-permute-start.2 = (bf16[1024,512]{1,0:T(8,128)(2,1)}, bf16[1024,512]{1,0:T(8,128)(2,1)}, u32[]{:S(2)}, u32[]{:S(2)}) collective-permute-start(bf16[1024,512]{1,0:T(8,128)(2,1)} %collective-permute-done), channel_id=1, source_target_pairs={{0,1},{1,0},{2,3},{3,2},{4,5},{5,4},{6,7},{7,6},{8,9},{9,8},{10,11... | collective-permute-start | bytes 3145736 | tf_op jit(solution)/shard_map/ppermute | solution.py:196
  82.8 37.7 %copy-start.1 = (f32[512,128]{1,0:T(8,128)S(1)}, f32[512,128]{1,0:T(8,128)}, u32[]{:S(2)}) copy-start(f32[512,128]{1,0:T(8,128)} %param.9) | copy-start | bytes 786436
  82.9 37.8 %copy-start.2 = (f32[512,128]{1,0:T(8,128)S(1)}, f32[512,128]{1,0:T(8,128)}, u32[]{:S(2)}) copy-start(f32[512,128]{1,0:T(8,128)} %param.10) | copy-start | bytes 786436
  82.9 37.9 %copy-start.3 = (f32[512,128]{1,0:T(8,128)S(1)}, f32[512,128]{1,0:T(8,128)}, u32[]{:S(2)}) copy-start(f32[512,128]{1,0:T(8,128)} %param.11) | copy-start | bytes 786436
  115.5 13.4 %collective-permute-start.3 = (bf16[512,128]{0,1:T(8,128)(2,1)S(1)}, bf16[512,128]{0,1:T(8,128)(2,1)S(1)}, u32[]{:S(2)}, u32[]{:S(2)}) collective-permute-start(bf16[512,128]{0,1:T(8,128)(2,1)S(1)} %reduce_sum.12), channel_id=1, source_target_pairs={{0,0},{1,20},{2,36},{3,48},{4,76},{5,88},{6,104},{7,124},{8,128},{... | collective-permute-start | bytes 393224 | tf_op jit(solution)/shard_map/ppermute | solution.py:215
  169.3 103.4 %all-to-all-start.5 = ((bf16[64,4,32,256]{3,2,1,0:T(8,128)(2,1)}), bf16[64,4,32,256]{3,2,1,0:T(8,128)(2,1)}, u32[]{:S(2)}, u32[]{:S(2)}) async-start(bf16[64,4,32,256]{3,2,1,0:T(8,128)(2,1)} %unpack.1), calls=%async_computation.5 | async-start | bytes 8388608 | tf_op jit(solution)/shard_map/all_to_all | solution.py:224
  180.0 55.1 %collective-permute-start.4 = (bf16[512,128]{0,1:T(8,128)(2,1)S(1)}, bf16[512,128]{0,1:T(8,128)(2,1)S(1)}, u32[]{:S(2)}, u32[]{:S(2)}) collective-permute-start(bf16[512,128]{0,1:T(8,128)(2,1)S(1)} %get-tuple-element.15), channel_id=1, source_target_pairs={{0,128},{128,0},{1,129},{129,1},{2,130},{130,2},{3,131},{131,3},{4... | collective-permute-start | bytes 393224 | tf_op jit(solution)/shard_map/ppermute | solution.py:164
  235.9 8.6 %collective-permute-start.5 = (bf16[2,512,128]{1,2,0:T(8,128)(2,1)}, bf16[2,512,128]{1,2,0:T(8,128)(2,1)}, u32[]{:S(2)}, u32[]{:S(2)}) collective-permute-start(bf16[2,512,128]{1,2,0:T(8,128)(2,1)} %pad_maximum_fusion), channel_id=1, source_target_pairs={{0,16},{16,32},{32,48},{48,64},{64,80},{80,96},{96,112},{112,0},{1... | collective-permute-start | bytes 786440 | tf_op jit(solution)/shard_map/ppermute | solution.py:174
  235.9 10.1 %collective-permute-start.6 = (bf16[2,512,128]{1,2,0:T(8,128)(2,1)}, bf16[2,512,128]{1,2,0:T(8,128)(2,1)S(1)}, u32[]{:S(2)}, u32[]{:S(2)}) collective-permute-start(bf16[2,512,128]{1,2,0:T(8,128)(2,1)} %pad_maximum_fusion), channel_id=1, source_target_pairs={{0,112},{16,0},{32,16},{48,32},{64,48},{80,64},{96,80},{112,96},{1... | collective-permute-start | bytes 786440 | tf_op jit(solution)/shard_map/ppermute | solution.py:175
  244.5 7.6 %collective-permute-start.7 = (bf16[2,512,128]{1,2,0:T(8,128)(2,1)}, bf16[2,512,128]{1,2,0:T(8,128)(2,1)S(1)}, u32[]{:S(2)}, u32[]{:S(2)}) collective-permute-start(bf16[2,512,128]{1,2,0:T(8,128)(2,1)} %collective-permute-done.5), channel_id=1, source_target_pairs={{0,16},{16,32},{32,48},{48,64},{64,80},{80,96},{96,112},{112,0},{1... | collective-permute-start | bytes 786440 | tf_op jit(solution)/shard_map/ppermute | solution.py:174
  246.0 9.1 %collective-permute-start.8 = (bf16[2,512,128]{1,2,0:T(8,128)(2,1)S(1)}, bf16[2,512,128]{1,2,0:T(8,128)(2,1)S(1)}, u32[]{:S(2)}, u32[]{:S(2)}) collective-permute-start(bf16[2,512,128]{1,2,0:T(8,128)(2,1)S(1)} %collective-permute-done.6), channel_id=1, source_target_pairs={{0,112},{16,0},{32,16},{48,32},{64,48},{80,64},{96,80},{112,96},{1... | collective-permute-start | bytes 786440 | tf_op jit(solution)/shard_map/ppermute | solution.py:175
  252.1 7.3 %collective-permute-start.9 = (bf16[2,512,128]{1,2,0:T(8,128)(2,1)S(1)}, bf16[2,512,128]{1,2,0:T(8,128)(2,1)S(1)}, u32[]{:S(2)}, u32[]{:S(2)}) collective-permute-start(bf16[2,512,128]{1,2,0:T(8,128)(2,1)S(1)} %collective-permute-done.7), channel_id=1, source_target_pairs={{0,16},{16,32},{32,48},{48,64},{64,80},{80,96},{96,112},{112,0},{1... | collective-permute-start | bytes 786440 | tf_op jit(solution)/shard_map/ppermute | solution.py:174
  255.1 8.1 %collective-permute-start.10 = (bf16[2,512,128]{1,2,0:T(8,128)(2,1)S(1)}, bf16[2,512,128]{1,2,0:T(8,128)(2,1)S(1)}, u32[]{:S(2)}, u32[]{:S(2)}) collective-permute-start(bf16[2,512,128]{1,2,0:T(8,128)(2,1)S(1)} %collective-permute-done.8), channel_id=1, source_target_pairs={{0,112},{16,0},{32,16},{48,32},{64,48},{80,64},{96,80},{112,96},{1... | collective-permute-start | bytes 786440 | tf_op jit(solution)/shard_map/ppermute | solution.py:175
  259.5 10.2 %collective-permute-start.11 = (bf16[1,512,128]{1,2,0:T(8,128)(2,1)S(1)}, bf16[1,512,128]{1,2,0:T(8,128)(2,1)S(1)}, u32[]{:S(2)}, u32[]{:S(2)}) collective-permute-start(bf16[1,512,128]{1,2,0:T(8,128)(2,1)S(1)} %slice.48), channel_id=1, source_target_pairs={{0,16},{16,32},{32,48},{48,64},{64,80},{80,96},{96,112},{112,0},{1... | collective-permute-start | bytes 393224 | tf_op jit(solution)/shard_map/ppermute | solution.py:178
  263.3 6.3 %collective-permute-start.12 = (bf16[1,512,128]{1,2,0:T(8,128)(2,1)S(1)}, bf16[1,512,128]{1,2,0:T(8,128)(2,1)S(1)}, u32[]{:S(2)}, u32[]{:S(2)}) collective-permute-start(bf16[1,512,128]{1,2,0:T(8,128)(2,1)S(1)} %slice.49), channel_id=1, source_target_pairs={{0,112},{16,0},{32,16},{48,32},{64,48},{80,64},{96,80},{112,96},{1... | collective-permute-start | bytes 393224 | tf_op jit(solution)/shard_map/ppermute | solution.py:179

commit v3 on v2

--- a/solution.py
+++ b/solution.py
@@ -112,14 +112,14 @@
 def unpack_kernel(place_ref, lengths_ref, weights_ref, out_ref, windows_ref):
     group = pl.program_id(0)
     replica = 8 * (group // 2) + 2 * place_ref[1] + group % 2
-    zh, blocks, rows, width = weights_ref.shape
-    lane = lax.broadcasted_iota(jnp.int32, (zh, rows, width), 2)
+    pieces, blocks, rows, width = weights_ref.shape
+    lane = lax.broadcasted_iota(jnp.int32, (pieces, rows, width), 2)
 
     @pl.when(group == 0)
     def _():
         def turned(t):
-            tile = weights_ref[:, t].reshape(zh * rows, width)
-            return pltpu.roll(tile.astype(jnp.float32), UNIT, 1).reshape(zh, rows, width)
+            tile = weights_ref[:, t].reshape(pieces * rows, width)
+            return pltpu.roll(tile.astype(jnp.float32), UNIT, 1).reshape(pieces, rows, width)
 
         def window(t, low):
             high = turned(jnp.minimum(t + 1, blocks - 1))
@@ -141,16 +141,16 @@
 
 
 def slot_columns(weights, lengths, place):
-    zh, blocks, rows, width = weights.shape
+    pieces, blocks, rows, width = weights.shape
     smem = pl.BlockSpec(memory_space=pltpu.SMEM)
     return pl.pallas_call(
         unpack_kernel,
-        out_shape=jax.ShapeDtypeStruct((64, zh, rows, 256), weights.dtype),
+        out_shape=jax.ShapeDtypeStruct((64, pieces, rows, 256), weights.dtype),
         grid=(4,),
-        in_specs=[smem, smem, pl.BlockSpec((zh, blocks, rows, width), lambda g: (0, 0, 0, 0))],
-        out_specs=pl.BlockSpec((16, zh, rows, 256), lambda g: (g, 0, 0, 0)),
-        scratch_shapes=[pltpu.VMEM((2 * blocks, zh, rows, width), weights.dtype)],
-        cost_estimate=pl.CostEstimate(flops=10_000_000, bytes_accessed=5_000_000, transcendentals=0),
+        in_specs=[smem, smem, pl.BlockSpec((pieces, blocks, rows, width), lambda g: (0, 0, 0, 0))],
+        out_specs=pl.BlockSpec((16, pieces, rows, 256), lambda g: (g, 0, 0, 0)),
+        scratch_shapes=[pltpu.VMEM((2 * blocks, pieces, rows, width), weights.dtype)],
+        cost_estimate=pl.CostEstimate(flops=3_000_000 * pieces, bytes_accessed=1_300_000 * pieces, transcendentals=0),
         name="unpack",
     )(place, lengths, weights)
 
@@ -218,11 +218,19 @@
     weights = new_master.astype(jnp.bfloat16)
 
     rows = lax.all_to_all(weights.reshape(16, 32, 128), TP, split_axis=0, concat_axis=0, tiled=True)
-    rows = jnp.broadcast_to(rows[None], (4, *rows.shape))
-    rows = lax.all_to_all(rows, "zh", split_axis=0, concat_axis=0, tiled=True)
-    outgoing = slot_columns(rows, lengths, place)
-    incoming = lax.all_to_all(outgoing, GROUP, split_axis=0, concat_axis=0, tiled=True)
-    slot_weights = incoming.reshape(2, 2, 16, 4, 32, slot_width).transpose(0, 3, 1, 2, 4, 5)
+    others = [lax.ppermute(rows, "zh", [(k, (k + step) % 4) for k in range(4)]) for step in (3, 2, 1)]
+    zh = lax.axis_index("zh")
+    slot_weights = jnp.zeros((2, 4, 2, 16, 32, slot_width), weights.dtype)
+    distance = 0
+    for pieces in (rows[None], jnp.stack(others)):
+        outgoing = slot_columns(pieces, lengths, place)
+        incoming = lax.all_to_all(outgoing, GROUP, split_axis=0, concat_axis=0, tiled=True)
+        incoming = incoming.reshape(2, 2, 16, -1, 32, slot_width).transpose(0, 3, 1, 2, 4, 5)
+        for piece in range(incoming.shape[1]):
+            slot_weights = lax.dynamic_update_slice(
+                slot_weights, incoming[:, piece : piece + 1], (0, (zh + distance) % 4, 0, 0, 0, 0)
+            )
+            distance += 1
     slot_weights = slot_weights.reshape(1, -1, slot_width)
     healthy = all_rows(weights)
     return (new_master, new_first, new_second, healthy, slot_weights)

time: 278 us -> 293 us (1.054)
  the two profiles are of different devices: /device:TPU:118 before, /device:TPU:22 now
where the time goes in v3:
time: 293 us; the launch traced here: 292 us
  waiting for transfers between devices  130 us (44%)
  starting transfers between devices  59.5 us (20%)
  blocking collectives  49 us (17%)
  local copies, waits for them, and re-layouts  27.6 us (9%)
  Pallas kernels  12.3 us (4%)
  matrix products  7.84 us (3%)
  other arithmetic  4.89 us (2%)
    ppermute x1, waiting for transfers between devices, on_device(): across = lax.ppermute(tokens, 'z0', SWAP)  46.3 us
    ppermute x1, waiting for transfers between devices, all_rows(): other = lax.ppermute(weights, 'yl', SWAP)  38.2 us
    all_to_all x1, blocking collectives, on_device(): lax.all_to_all(jnp.stack(blocks), SUM, split_axis=0, concat_axis=0, tiled...  37.8 us
    ppermute x3, waiting for transfers between devices, on_device(): lax.ppermute(rows, 'zh', [(k, (k + step) % 4) for k in range(4)])  19.9 us
    all_to_all x2, starting transfers between devices, on_device(): lax.all_to_all(outgoing, GROUP, split_axis=0, concat_axis=0, tiled=True)  17.3 us
    dynamic_update_slice x9, local copies, waits for them, and re-layouts, put(): lax.dynamic_update_slice(out, piece[:, None], (first, (z + distance) % 8,...  11.5 us
    ppermute x1, waiting for transfers between devices, on_device(): lax.ppermute(summed, AXES, home_permutation()).astype(jnp.float32)  11.3 us
    all_to_all x1, blocking collectives, on_device(): lax.all_to_all(weights.reshape(16, 32, 128), TP, split_axis=0, concat_axi...  11.2 us
  transfers between devices with their start and end apart: 20, of which 10 were waited for; matrix products, arithmetic and copies ran while one was open for 11% of the time, Pallas kernels for 2%

profile of v3, /device:TPU:22, one launch (start us, length us, event | category | flops | bytes accessed | tf_op | source)
XLA Modules:
  0.0 292.3 jit_solution(2911475495598073101)
XLA Ops:
  0.6 7.2 %all-to-all-start = ((bf16[16,64,256]{2,1,0:T(8,128)(2,1)}), bf16[16,64,256]{2,1,0:T(8,128)(2,1)S(1)}, u32[]{:S(2)}, u32[]{:S(2)}) async-start(bf16[16,64,256]{2,1,0:T(8,128)(2,1)} %bitcast.126), calls=%async_computation | async-start | bytes 1048576 | tf_op jit(solution)/shard_map/all_to_all | solution.py:199
  7.8 0.6 pad_add_fusion.place_ref
  8.4 6.7 %all-to-all-done.slots_ref = bf16[16,64,256]{2,1,0:T(8,128)(2,1)S(1)} async-done(((bf16[16,64,256]{2,1,0:T(8,128)(2,1)}), bf16[16,64,256]{2,1,0:T(8,128)(2,1)S(1)}, u32[]{:S(2)}, u32[]{:S(2)}) %all-to-all-start) | async-done | bytes 524320 | tf_op jit(solution)/shard_map/all_to_all | solution.py:199
  15.1 0.8 copy-done.2
  15.9 3.1 %pack.1 = bf16[2,8,2,64,512]{4,3,2,1,0:T(8,128)(2,1)} custom-call(s32[2]{0:T(128)} %pad_add_fusion.place_ref, s32[16,16]{1,0:T(8,128)} %lengths_ref.5, bf16[16,64,256]{2,1,0:T(8,128)(2,1)} %copy-done.2), custom_call_target="tpu_custom_call" | custom-call | flops 1000000 | bytes 5000000 | tf_op jit(solution)/shard_map/pack/pallas_call | solution.py:101
  19.0 9.1 %all-to-all-start.1 = ((bf16[32,64,512]{2,1,0:T(8,128)(2,1)}), bf16[32,64,512]{2,1,0:T(8,128)(2,1)S(1)}, u32[]{:S(2)}, u32[]{:S(2)}) async-start(bf16[32,64,512]{2,1,0:T(8,128)(2,1)} %bitcast.118), calls=%async_computation.1 | async-start | bytes 4194304 | tf_op jit(solution)/shard_map/all_to_all | solution.py:201
  28.1 1.6 collective-permute-start
  29.7 46.3 %collective-permute-done = bf16[1024,512]{1,0:T(8,128)(2,1)} collective-permute-done((bf16[1024,512]{1,0:T(8,128)(2,1)}, bf16[1024,512]{1,0:T(8,128)(2,1)}, u32[]{:S(2)}, u32[]{:S(2)}) %collective-permute-start) | collective-permute-done | bytes 1048608 | tf_op jit(solution)/shard_map/ppermute | solution.py:194
  76.0 2.0 fusion.11
  78.0 2.0 fusion.3
  80.0 2.0 fusion.9
  82.0 2.0 fusion.2
  84.1 37.8 %all_to_all.30 = bf16[8,512,128]{1,2,0:T(8,128)(2,1)S(1)} all-to-all(bf16[8,512,128]{1,2,0:T(8,128)(2,1)S(1)} %fusion.19), channel_id=1, replica_groups=mesh['yl'=2,'zh'=4,'z0'=2,'x'=4,'yh'=2,'co'=2] {'yl','zh'}, dimensions={0} | all-to-all | bytes 2097152 | tf_op jit(solution)/shard_map/all_to_all | solution.py:213
  121.9 0.1 reduce_sum.12
  122.0 1.9 collective-permute-start.3
  123.9 0.1 copy.22
  124.1 0.1 copy.23
  124.2 0.1 copy.25
  124.4 11.3 %collective-permute-done.3 = bf16[512,128]{0,1:T(8,128)(2,1)S(1)} collective-permute-done((bf16[512,128]{0,1:T(8,128)(2,1)S(1)}, bf16[512,128]{0,1:T(8,128)(2,1)S(1)}, u32[]{:S(2)}, u32[]{:S(2)}) %collective-permute-start.3) | collective-permute-done | bytes 131104 | tf_op jit(solution)/shard_map/ppermute | solution.py:215
  135.7 1.0 fusion.31
  136.8 11.2 %all_to_all.31 = bf16[16,32,128]{2,1,0:T(8,128)(2,1)} all-to-all(bf16[16,32,128]{2,1,0:T(8,128)(2,1)S(1)} %bitcast.127), channel_id=1, replica_groups=mesh['yl'=2,'zh'=4,'z0'=2,'x'=4,'yh'=2,'co'=2] {'x','yh','co'}, dimensions={0} | all-to-all | bytes 262144 | tf_op jit(solution)/shard_map/all_to_all | solution.py:220
  148.0 4.2 %unpack.2 = bf16[64,1,32,256]{3,2,1,0:T(8,128)(2,1)} custom-call(s32[2]{0:T(128)} %pad_add_fusion.place_ref, s32[16,16]{1,0:T(8,128)} %lengths_ref.5, bf16[1,16,32,128]{3,2,1,0:T(8,128)(2,1)} %bitcast.125), custom_call_target="tpu_custom_call" | custom-call | flops 3000000 | bytes 1300000 | tf_op jit(solution)/shard_map/unpack/pallas_call | solution.py:146
  152.2 8.8 %all-to-all-start.4 = ((bf16[64,1,32,256]{3,2,1,0:T(8,128)(2,1)}), bf16[64,1,32,256]{3,2,1,0:T(8,128)(2,1)S(1)}, u32[]{:S(2)}, u32[]{:S(2)}) async-start(bf16[64,1,32,256]{3,2,1,0:T(8,128)(2,1)} %unpack.2), calls=%async_computation.4 | async-start | bytes 2097152 | tf_op jit(solution)/shard_map/all_to_all | solution.py:227
  161.0 2.0 collective-permute-start.13
  162.9 3.3 %collective-permute-start.14 = (bf16[16,32,128]{2,1,0:T(8,128)(2,1)S(1)}, bf16[16,32,128]{2,1,0:T(8,128)(2,1)S(1)}, u32[]{:S(2)}, u32[]{:S(2)}) collective-permute-start(bf16[16,32,128]{2,1,0:T(8,128)(2,1)S(1)} %copy-done.3), channel_id=1, source_target_pairs={{0,64},{32,96},{64,0},{96,32},{1,65},{33,97},{65,1},{97,33},{2,66}... | collective-permute-start | bytes 393224 | tf_op jit(solution)/shard_map/ppermute | solution.py:221
  166.2 1.4 collective-permute-done.13
  167.6 14.9 %collective-permute-done.14 = bf16[16,32,128]{2,1,0:T(8,128)(2,1)S(1)} collective-permute-done((bf16[16,32,128]{2,1,0:T(8,128)(2,1)S(1)}, bf16[16,32,128]{2,1,0:T(8,128)(2,1)S(1)}, u32[]{:S(2)}, u32[]{:S(2)}) %collective-permute-start.14) | collective-permute-done | bytes 131104 | tf_op jit(solution)/shard_map/ppermute | solution.py:221
  182.5 3.7 %collective-permute-done.15 = bf16[16,32,128]{2,1,0:T(8,128)(2,1)S(1)} collective-permute-done((bf16[16,32,128]{2,1,0:T(8,128)(2,1)S(1)}, bf16[16,32,128]{2,1,0:T(8,128)(2,1)S(1)}, u32[]{:S(2)}, u32[]{:S(2)}) %collective-permute-start.15) | collective-permute-done | bytes 131104 | tf_op jit(solution)/shard_map/ppermute | solution.py:221
  186.1 0.8 pad_maximum_fusion.weights_ref
  186.9 5.0 %unpack.3 = bf16[64,3,32,256]{3,2,1,0:T(8,128)(2,1)} custom-call(s32[2]{0:T(128)} %pad_add_fusion.place_ref, s32[16,16]{1,0:T(8,128)} %lengths_ref.5, bf16[3,16,32,128]{3,2,1,0:T(8,128)(2,1)} %pad_maximum_fusion.weights_ref), custom_call_target="tpu_custom_call" | custom-call | flops 9000000 | bytes 3900000 | tf_op jit(solution)/shard_map/unpack/pallas_call | solution.py:146
  191.9 1.0 copy-done
  192.9 8.5 %all-to-all-start.5 = ((bf16[64,3,32,256]{3,2,1,0:T(8,128)(2,1)}), bf16[64,3,32,256]{3,2,1,0:T(8,128)(2,1)S(1)}, u32[]{:S(2)}, u32[]{:S(2)}) async-start(bf16[64,3,32,256]{3,2,1,0:T(8,128)(2,1)} %unpack.3), calls=%async_computation.5 | async-start | bytes 6291456 | tf_op jit(solution)/shard_map/all_to_all | solution.py:227
  201.4 1.4 collective-permute-start.4
  202.8 38.2 %collective-permute-done.4 = bf16[512,128]{0,1:T(8,128)(2,1)} collective-permute-done((bf16[512,128]{0,1:T(8,128)(2,1)S(1)}, bf16[512,128]{0,1:T(8,128)(2,1)}, u32[]{:S(2)}, u32[]{:S(2)}) %collective-permute-start.4) | collective-permute-done | bytes 131104 | tf_op jit(solution)/shard_map/ppermute | solution.py:164
  241.1 0.9 select_bitcast_fusion.1
  242.0 0.7 pad_maximum_fusion.1
  242.7 3.9 %collective-permute-start.5 = (bf16[2,512,128]{1,2,0:T(8,128)(2,1)}, bf16[2,512,128]{1,2,0:T(8,128)(2,1)}, u32[]{:S(2)}, u32[]{:S(2)}) collective-permute-start(bf16[2,512,128]{1,2,0:T(8,128)(2,1)} %pad_maximum_fusion.1), channel_id=1, source_target_pairs={{0,16},{16,32},{32,48},{48,64},{64,80},{80,96},{96,112},{112,0},{1... | collective-permute-start | bytes 786440 | tf_op jit(solution)/shard_map/ppermute | solution.py:174
  246.7 1.9 collective-permute-start.6
  248.6 1.8 copy.40
  250.3 1.8 copy.41
  252.1 1.8 copy.42
  253.9 1.5 broadcast_in_dim.36
  255.4 0.7 bitcast_dynamic-update-slice_fusion.6
  256.2 0.1 collective-permute-start.7
  256.3 3.1 %collective-permute-start.8 = (bf16[2,512,128]{1,2,0:T(8,128)(2,1)}, bf16[2,512,128]{1,2,0:T(8,128)(2,1)S(1)}, u32[]{:S(2)}, u32[]{:S(2)}) collective-permute-start(bf16[2,512,128]{1,2,0:T(8,128)(2,1)} %collective-permute-done.6), channel_id=1, source_target_pairs={{0,112},{16,0},{32,16},{48,32},{64,48},{80,64},{96,80},{112,96},{1... | collective-permute-start | bytes 786440 | tf_op jit(solution)/shard_map/ppermute | solution.py:175
  259.4 1.7 bitcast_dynamic-update-slice_fusion.5
  261.1 1.7 bitcast_dynamic-update-slice_fusion.4
  262.7 2.8 collective-permute-done.7
  265.6 3.2 %collective-permute-start.10 = (bf16[2,512,128]{1,2,0:T(8,128)(2,1)S(1)}, bf16[2,512,128]{1,2,0:T(8,128)(2,1)S(1)}, u32[]{:S(2)}, u32[]{:S(2)}) collective-permute-start(bf16[2,512,128]{1,2,0:T(8,128)(2,1)S(1)} %collective-permute-done.8), channel_id=1, source_target_pairs={{0,112},{16,0},{32,16},{48,32},{64,48},{80,64},{96,80},{112,96},{1... | collective-permute-start | bytes 786440 | tf_op jit(solution)/shard_map/ppermute | solution.py:175
  268.8 0.7 bitcast_dynamic-update-slice_fusion.3
  269.5 0.7 bitcast_dynamic-update-slice_fusion.2
  270.3 3.7 %collective-permute-done.9 = bf16[2,512,128]{1,2,0:T(8,128)(2,1)S(1)} collective-permute-done((bf16[2,512,128]{1,2,0:T(8,128)(2,1)S(1)}, bf16[2,512,128]{1,2,0:T(8,128)(2,1)S(1)}, u32[]{:S(2)}, u32[]{:S(2)}) %collective-permute-start.9) | collective-permute-done | bytes 262176 | tf_op jit(solution)/shard_map/ppermute | solution.py:174
  274.1 3.3 %collective-permute-start.12 = (bf16[1,512,128]{1,2,0:T(8,128)(2,1)S(1)}, bf16[1,512,128]{1,2,0:T(8,128)(2,1)S(1)}, u32[]{:S(2)}, u32[]{:S(2)}) collective-permute-start(bf16[1,512,128]{1,2,0:T(8,128)(2,1)S(1)} %slice.61), channel_id=1, source_target_pairs={{0,112},{16,0},{32,16},{48,32},{64,48},{80,64},{96,80},{112,96},{1... | collective-permute-start | bytes 393224 | tf_op jit(solution)/shard_map/ppermute | solution.py:179
  277.3 0.7 bitcast_dynamic-update-slice_fusion.1
  278.1 0.7 bitcast_dynamic-update-slice_fusion
  278.8 1.4 collective-permute-done.11
  280.2 0.7 bitcast_dynamic-update-slice_fusion.7
  280.9 3.9 %copy.33 = bf16[2,8,512,128]{3,2,1,0:T(8,128)(2,1)} copy(bf16[2,8,512,128]{2,3,1,0:T(8,128)(2,1)} %bitcast_dynamic-update-slice_fusion.7) | data formatting | bytes 4194304 | tf_op jit(solution)/shard_map/dynamic_update_slice | solution.py:169
  284.9 0.7 constant_dynamic-update-slice_fusion.1
  285.6 2.5 broadcast_in_dim.46
  288.1 1.0 constant_dynamic-update-slice_fusion
  289.2 1.0 fusion.6
  290.2 1.0 fusion.5
  291.3 1.0 fusion.4
  (39 shorter events, 0.5 us)
Async XLA Ops:
  0.6 14.5 %all-to-all-start = ((bf16[16,64,256]{2,1,0:T(8,128)(2,1)}), bf16[16,64,256]{2,1,0:T(8,128)(2,1)S(1)}, u32[]{:S(2)}, u32[]{:S(2)}) async-start(bf16[16,64,256]{2,1,0:T(8,128)(2,1)} %bitcast.126), calls=%async_computation | async-start | bytes 1048576 | tf_op jit(solution)/shard_map/all_to_all | solution.py:199
  15.1 0.8 copy-start.2
  19.0 57.0 %all-to-all-start.1 = ((bf16[32,64,512]{2,1,0:T(8,128)(2,1)}), bf16[32,64,512]{2,1,0:T(8,128)(2,1)S(1)}, u32[]{:S(2)}, u32[]{:S(2)}) async-start(bf16[32,64,512]{2,1,0:T(8,128)(2,1)} %bitcast.118), calls=%async_computation.1 | async-start | bytes 4194304 | tf_op jit(solution)/shard_map/all_to_all | solution.py:201
  28.1 47.9 %collective-permute-start = (bf16[1024,512]{1,0:T(8,128)(2,1)}, bf16[1024,512]{1,0:T(8,128)(2,1)}, u32[]{:S(2)}, u32[]{:S(2)}) collective-permute-start(bf16[1024,512]{1,0:T(8,128)(2,1)} %param.6), channel_id=1, source_target_pairs={{0,16},{16,0},{1,17},{17,1},{2,18},{18,2},{3,19},{19,3},{4,20},{20... | collective-permute-start | bytes 3145736 | tf_op jit(solution)/shard_map/ppermute | solution.py:194
  29.7 50.2 %collective-permute-start.1 = (bf16[1024,512]{1,0:T(8,128)(2,1)}, bf16[1024,512]{1,0:T(8,128)(2,1)}, u32[]{:S(2)}, u32[]{:S(2)}) collective-permute-start(bf16[1024,512]{1,0:T(8,128)(2,1)} %param.6), channel_id=1, source_target_pairs={{0,1},{1,0},{2,3},{3,2},{4,5},{5,4},{6,7},{7,6},{8,9},{9,8},{10,11... | collective-permute-start | bytes 3145736 | tf_op jit(solution)/shard_map/ppermute | solution.py:196
  76.0 6.0 %collective-permute-start.2 = (bf16[1024,512]{1,0:T(8,128)(2,1)}, bf16[1024,512]{1,0:T(8,128)(2,1)}, u32[]{:S(2)}, u32[]{:S(2)}) collective-permute-start(bf16[1024,512]{1,0:T(8,128)(2,1)} %collective-permute-done), channel_id=1, source_target_pairs={{0,1},{1,0},{2,3},{3,2},{4,5},{5,4},{6,7},{7,6},{8,9},{9,8},{10,11... | collective-permute-start | bytes 3145736 | tf_op jit(solution)/shard_map/ppermute | solution.py:196
  84.0 40.0 %copy-start.4 = (f32[512,128]{1,0:T(8,128)S(1)}, f32[512,128]{1,0:T(8,128)}, u32[]{:S(2)}) copy-start(f32[512,128]{1,0:T(8,128)} %param.10) | copy-start | bytes 786436
  84.0 40.1 %copy-start.5 = (f32[512,128]{1,0:T(8,128)S(1)}, f32[512,128]{1,0:T(8,128)}, u32[]{:S(2)}) copy-start(f32[512,128]{1,0:T(8,128)} %param.11) | copy-start | bytes 786436
  84.1 40.2 %copy-start.6 = (f32[512,128]{1,0:T(8,128)S(1)}, f32[512,128]{1,0:T(8,128)}, u32[]{:S(2)}) copy-start(f32[512,128]{1,0:T(8,128)} %param.9) | copy-start | bytes 786436
  122.0 13.7 %collective-permute-start.3 = (bf16[512,128]{0,1:T(8,128)(2,1)S(1)}, bf16[512,128]{0,1:T(8,128)(2,1)S(1)}, u32[]{:S(2)}, u32[]{:S(2)}) collective-permute-start(bf16[512,128]{0,1:T(8,128)(2,1)S(1)} %reduce_sum.12), channel_id=1, source_target_pairs={{0,0},{1,20},{2,36},{3,48},{4,76},{5,88},{6,104},{7,124},{8,128},{... | collective-permute-start | bytes 393224 | tf_op jit(solution)/shard_map/ppermute | solution.py:215
  148.0 13.0 %copy-start.3 = (bf16[16,32,128]{2,1,0:T(8,128)(2,1)S(1)}, bf16[16,32,128]{2,1,0:T(8,128)(2,1)}, u32[]{:S(2)}) copy-start(bf16[16,32,128]{2,1,0:T(8,128)(2,1)} %all_to_all.31) | copy-start | bytes 393220
  152.2 39.7 %all-to-all-start.4 = ((bf16[64,1,32,256]{3,2,1,0:T(8,128)(2,1)}), bf16[64,1,32,256]{3,2,1,0:T(8,128)(2,1)S(1)}, u32[]{:S(2)}, u32[]{:S(2)}) async-start(bf16[64,1,32,256]{3,2,1,0:T(8,128)(2,1)} %unpack.2), calls=%async_computation.4 | async-start | bytes 2097152 | tf_op jit(solution)/shard_map/all_to_all | solution.py:227
  161.0 6.6 %collective-permute-start.13 = (bf16[16,32,128]{2,1,0:T(8,128)(2,1)S(1)}, bf16[16,32,128]{2,1,0:T(8,128)(2,1)S(1)}, u32[]{:S(2)}, u32[]{:S(2)}) collective-permute-start(bf16[16,32,128]{2,1,0:T(8,128)(2,1)S(1)} %copy-done.3), channel_id=1, source_target_pairs={{0,96},{32,0},{64,32},{96,64},{1,97},{33,1},{65,33},{97,65},{2,98}... | collective-permute-start | bytes 393224 | tf_op jit(solution)/shard_map/ppermute | solution.py:221
  162.9 19.5 %collective-permute-start.14 = (bf16[16,32,128]{2,1,0:T(8,128)(2,1)S(1)}, bf16[16,32,128]{2,1,0:T(8,128)(2,1)S(1)}, u32[]{:S(2)}, u32[]{:S(2)}) collective-permute-start(bf16[16,32,128]{2,1,0:T(8,128)(2,1)S(1)} %copy-done.3), channel_id=1, source_target_pairs={{0,64},{32,96},{64,0},{96,32},{1,65},{33,97},{65,1},{97,33},{2,66}... | collective-permute-start | bytes 393224 | tf_op jit(solution)/shard_map/ppermute | solution.py:221
  166.2 19.9 %collective-permute-start.15 = (bf16[16,32,128]{2,1,0:T(8,128)(2,1)S(1)}, bf16[16,32,128]{2,1,0:T(8,128)(2,1)S(1)}, u32[]{:S(2)}, u32[]{:S(2)}) collective-permute-start(bf16[16,32,128]{2,1,0:T(8,128)(2,1)S(1)} %copy-done.3), channel_id=1, source_target_pairs={{0,32},{32,64},{64,96},{96,0},{1,33},{33,65},{65,97},{97,1},{2,34}... | collective-permute-start | bytes 393224 | tf_op jit(solution)/shard_map/ppermute | solution.py:221
  191.9 1.0 copy-start
  192.9 96.3 %all-to-all-start.5 = ((bf16[64,3,32,256]{3,2,1,0:T(8,128)(2,1)}), bf16[64,3,32,256]{3,2,1,0:T(8,128)(2,1)S(1)}, u32[]{:S(2)}, u32[]{:S(2)}) async-start(bf16[64,3,32,256]{3,2,1,0:T(8,128)(2,1)} %unpack.3), calls=%async_computation.5 | async-start | bytes 6291456 | tf_op jit(solution)/shard_map/all_to_all | solution.py:227
  201.4 39.7 %collective-permute-start.4 = (bf16[512,128]{0,1:T(8,128)(2,1)S(1)}, bf16[512,128]{0,1:T(8,128)(2,1)}, u32[]{:S(2)}, u32[]{:S(2)}) collective-permute-start(bf16[512,128]{0,1:T(8,128)(2,1)S(1)} %get-tuple-element.10), channel_id=1, source_target_pairs={{0,128},{128,0},{1,129},{129,1},{2,130},{130,2},{3,131},{131,3},{4... | collective-permute-start | bytes 393224 | tf_op jit(solution)/shard_map/ppermute | solution.py:164
  242.7 13.4 %collective-permute-start.5 = (bf16[2,512,128]{1,2,0:T(8,128)(2,1)}, bf16[2,512,128]{1,2,0:T(8,128)(2,1)}, u32[]{:S(2)}, u32[]{:S(2)}) collective-permute-start(bf16[2,512,128]{1,2,0:T(8,128)(2,1)} %pad_maximum_fusion.1), channel_id=1, source_target_pairs={{0,16},{16,32},{32,48},{48,64},{64,80},{80,96},{96,112},{112,0},{1... | collective-permute-start | bytes 786440 | tf_op jit(solution)/shard_map/ppermute | solution.py:174
  246.7 9.6 %collective-permute-start.6 = (bf16[2,512,128]{1,2,0:T(8,128)(2,1)}, bf16[2,512,128]{1,2,0:T(8,128)(2,1)}, u32[]{:S(2)}, u32[]{:S(2)}) collective-permute-start(bf16[2,512,128]{1,2,0:T(8,128)(2,1)} %pad_maximum_fusion.1), channel_id=1, source_target_pairs={{0,112},{16,0},{32,16},{48,32},{64,48},{80,64},{96,80},{112,96},{1... | collective-permute-start | bytes 786440 | tf_op jit(solution)/shard_map/ppermute | solution.py:175
  256.2 9.4 %collective-permute-start.7 = (bf16[2,512,128]{1,2,0:T(8,128)(2,1)}, bf16[2,512,128]{1,2,0:T(8,128)(2,1)S(1)}, u32[]{:S(2)}, u32[]{:S(2)}) collective-permute-start(bf16[2,512,128]{1,2,0:T(8,128)(2,1)} %collective-permute-done.5), channel_id=1, source_target_pairs={{0,16},{16,32},{32,48},{48,64},{64,80},{80,96},{96,112},{112,0},{1... | collective-permute-start | bytes 786440 | tf_op jit(solution)/shard_map/ppermute | solution.py:174
  256.3 9.3 %collective-permute-start.8 = (bf16[2,512,128]{1,2,0:T(8,128)(2,1)}, bf16[2,512,128]{1,2,0:T(8,128)(2,1)S(1)}, u32[]{:S(2)}, u32[]{:S(2)}) collective-permute-start(bf16[2,512,128]{1,2,0:T(8,128)(2,1)} %collective-permute-done.6), channel_id=1, source_target_pairs={{0,112},{16,0},{32,16},{48,32},{64,48},{80,64},{96,80},{112,96},{1... | collective-permute-start | bytes 786440 | tf_op jit(solution)/shard_map/ppermute | solution.py:175
  265.6 8.3 %collective-permute-start.9 = (bf16[2,512,128]{1,2,0:T(8,128)(2,1)S(1)}, bf16[2,512,128]{1,2,0:T(8,128)(2,1)S(1)}, u32[]{:S(2)}, u32[]{:S(2)}) collective-permute-start(bf16[2,512,128]{1,2,0:T(8,128)(2,1)S(1)} %collective-permute-done.7), channel_id=1, source_target_pairs={{0,16},{16,32},{32,48},{48,64},{64,80},{80,96},{96,112},{112,0},{1... | collective-permute-start | bytes 786440 | tf_op jit(solution)/shard_map/ppermute | solution.py:174
  265.6 8.4 %collective-permute-start.10 = (bf16[2,512,128]{1,2,0:T(8,128)(2,1)S(1)}, bf16[2,512,128]{1,2,0:T(8,128)(2,1)S(1)}, u32[]{:S(2)}, u32[]{:S(2)}) collective-permute-start(bf16[2,512,128]{1,2,0:T(8,128)(2,1)S(1)} %collective-permute-done.8), channel_id=1, source_target_pairs={{0,112},{16,0},{32,16},{48,32},{64,48},{80,64},{96,80},{112,96},{1... | collective-permute-start | bytes 786440 | tf_op jit(solution)/shard_map/ppermute | solution.py:175
  273.9 6.3 %collective-permute-start.11 = (bf16[1,512,128]{1,2,0:T(8,128)(2,1)S(1)}, bf16[1,512,128]{1,2,0:T(8,128)(2,1)S(1)}, u32[]{:S(2)}, u32[]{:S(2)}) collective-permute-start(bf16[1,512,128]{1,2,0:T(8,128)(2,1)S(1)} %slice.60), channel_id=1, source_target_pairs={{0,16},{16,32},{32,48},{48,64},{64,80},{80,96},{96,112},{112,0},{1... | collective-permute-start | bytes 393224 | tf_op jit(solution)/shard_map/ppermute | solution.py:178
  274.1 10.7 %collective-permute-start.12 = (bf16[1,512,128]{1,2,0:T(8,128)(2,1)S(1)}, bf16[1,512,128]{1,2,0:T(8,128)(2,1)S(1)}, u32[]{:S(2)}, u32[]{:S(2)}) collective-permute-start(bf16[1,512,128]{1,2,0:T(8,128)(2,1)S(1)} %slice.61), channel_id=1, source_target_pairs={{0,112},{16,0},{32,16},{48,32},{64,48},{80,64},{96,80},{112,96},{1... | collective-permute-start | bytes 393224 | tf_op jit(solution)/shard_map/ppermute | solution.py:179
  285.6 2.6 copy-start.1

commit v4 on v3

--- a/solution.py
+++ b/solution.py
@@ -3,6 +3,7 @@
 from jax import lax
 from jax.experimental import pallas as pl
 from jax.experimental.pallas import tpu as pltpu
+from jax.experimental.layout import Layout, with_layout_constraint
 from jax.sharding import Mesh
 from jax.sharding import PartitionSpec as P
 
@@ -127,7 +128,7 @@
             windows_ref[2 * t + 1] = jnp.where(lane < UNIT, low, high).astype(windows_ref.dtype)
             return high
 
-        lax.fori_loop(0, blocks, window, turned(0))
+        lax.fori_loop(0, blocks, window, turned(0), unroll=True)
 
     def slot(j, begin):
         count = lengths_ref[replica, j] // UNIT
@@ -212,7 +213,8 @@
             blocks.append(totals[half][:, 128 * part : 128 * (part + 1)])
     arrived = lax.all_to_all(jnp.stack(blocks), SUM, split_axis=0, concat_axis=0, tiled=True)
     summed = jnp.sum(arrived.astype(jnp.float32), axis=0).astype(jnp.bfloat16)
-    gradient = lax.ppermute(summed, AXES, home_permutation()).astype(jnp.float32)
+    gradient = lax.ppermute(summed, AXES, home_permutation())
+    gradient = with_layout_constraint(gradient, Layout(major_to_minor=(0, 1))).astype(jnp.float32)
 
     new_master, new_first, new_second = adam_update(master, first, second, gradient)
     weights = new_master.astype(jnp.bfloat16)

time: 293 us -> 285 us (0.973)
  local copies, waits for them, and re-layouts: 27.6 us -> 12.6 us
  waiting for transfers between devices: 130 us -> 141 us
    dynamic_update_slice x9 -> x8, local copies, waits for them, and re-layouts: 11.5 us -> 2.17 us  [put(): lax.dynamic_update_slice(out, piece[:, None], (first, (z + distance) % 8,...]
    ppermute x3, waiting for transfers between devices: 6.5 us -> 15 us  [all_rows(): up = lax.ppermute(up, Z, ring(1))]
    unnamed x27 -> x23, local copies, waits for them, and re-layouts: 7.6 us -> 3.17 us
  transfers between devices with their start and end apart: 20 -> 20, of which waited for: 10 -> 11; matrix products, arithmetic and copies ran while one was open for 11% -> 5% of each run, Pallas kernels for 2% -> 1%
where the time goes in v4:
time: 285 us
  waiting for transfers between devices  141 us (49%)
  starting transfers between devices  59.5 us (21%)
  blocking collectives  48.9 us (17%)
  local copies, waits for them, and re-layouts  12.6 us (4%)
  Pallas kernels  9.9 us (3%)
  matrix products  7.84 us (3%)
  other arithmetic  4.22 us (1%)
    ppermute x1, waiting for transfers between devices, on_device(): across = lax.ppermute(tokens, 'z0', SWAP)  46.3 us
    ppermute x1, waiting for transfers between devices, all_rows(): other = lax.ppermute(weights, 'yl', SWAP)  38.2 us
    all_to_all x1, blocking collectives, on_device(): lax.all_to_all(jnp.stack(blocks), SUM, split_axis=0, concat_axis=0, tiled...  37.8 us
    ppermute x3, waiting for transfers between devices, on_device(): lax.ppermute(rows, 'zh', [(k, (k + step) % 4) for k in range(4)])  19.9 us
    all_to_all x2, starting transfers between devices, on_device(): lax.all_to_all(outgoing, GROUP, split_axis=0, concat_axis=0, tiled=True)  17.3 us
    ppermute x3, waiting for transfers between devices, all_rows(): up = lax.ppermute(up, Z, ring(1))  15 us
    ppermute x1, waiting for transfers between devices, on_device(): gradient = lax.ppermute(summed, AXES, home_permutation())  11.8 us
    all_to_all x1, blocking collectives, on_device(): lax.all_to_all(weights.reshape(16, 32, 128), TP, split_axis=0, concat_axi...  11.2 us
  transfers between devices with their start and end apart: 20, of which 11 were waited for; matrix products, arithmetic and copies ran while one was open for 5% of the time, Pallas kernels for 1%

profile of v4, /device:TPU:22, one launch (start us, length us, event | category | flops | bytes accessed | tf_op | source)
XLA Modules:
  0.0 284.5 jit_solution(977149743766577962)
XLA Ops:
  0.6 7.2 %all-to-all-start = ((bf16[16,64,256]{2,1,0:T(8,128)(2,1)}), bf16[16,64,256]{2,1,0:T(8,128)(2,1)S(1)}, u32[]{:S(2)}, u32[]{:S(2)}) async-start(bf16[16,64,256]{2,1,0:T(8,128)(2,1)} %bitcast.128), calls=%async_computation | async-start | bytes 1048576 | tf_op jit(solution)/shard_map/all_to_all | solution.py:200
  7.8 0.6 pad_add_fusion.place_ref
  8.4 6.7 %all-to-all-done.slots_ref = bf16[16,64,256]{2,1,0:T(8,128)(2,1)S(1)} async-done(((bf16[16,64,256]{2,1,0:T(8,128)(2,1)}), bf16[16,64,256]{2,1,0:T(8,128)(2,1)S(1)}, u32[]{:S(2)}, u32[]{:S(2)}) %all-to-all-start) | async-done | bytes 524320 | tf_op jit(solution)/shard_map/all_to_all | solution.py:200
  15.1 0.8 copy-done.3
  15.9 3.1 %pack.1 = bf16[2,8,2,64,512]{4,3,2,1,0:T(8,128)(2,1)} custom-call(s32[2]{0:T(128)} %pad_add_fusion.place_ref, s32[16,16]{1,0:T(8,128)} %lengths_ref.5, bf16[16,64,256]{2,1,0:T(8,128)(2,1)} %copy-done.3), custom_call_target="tpu_custom_call" | custom-call | flops 1000000 | bytes 5000000 | tf_op jit(solution)/shard_map/pack/pallas_call | solution.py:102
  19.0 9.1 %all-to-all-start.1 = ((bf16[32,64,512]{2,1,0:T(8,128)(2,1)}), bf16[32,64,512]{2,1,0:T(8,128)(2,1)S(1)}, u32[]{:S(2)}, u32[]{:S(2)}) async-start(bf16[32,64,512]{2,1,0:T(8,128)(2,1)} %bitcast.119), calls=%async_computation.1 | async-start | bytes 4194304 | tf_op jit(solution)/shard_map/all_to_all | solution.py:202
  28.1 1.6 collective-permute-start
  29.7 0.0 collective-permute-start.1
  29.7 46.3 %collective-permute-done = bf16[1024,512]{1,0:T(8,128)(2,1)} collective-permute-done((bf16[1024,512]{1,0:T(8,128)(2,1)}, bf16[1024,512]{1,0:T(8,128)(2,1)}, u32[]{:S(2)}, u32[]{:S(2)}) %collective-permute-start) | collective-permute-done | bytes 1048608 | tf_op jit(solution)/shard_map/ppermute | solution.py:195
  76.0 0.0 collective-permute-start.2
  76.0 0.0 all-to-all-done.1
  76.0 2.0 fusion.11
  78.0 2.0 fusion.3
  80.0 0.0 collective-permute-done.1
  80.0 2.0 fusion.9
  81.9 0.0 collective-permute-done.2
  82.0 2.0 fusion.2
  84.0 0.0 copy-start.5
  84.0 0.0 copy-start.6
  84.0 0.0 copy-start.7
  84.1 37.8 %all_to_all.30 = bf16[8,512,128]{1,2,0:T(8,128)(2,1)S(1)} all-to-all(bf16[8,512,128]{1,2,0:T(8,128)(2,1)S(1)} %fusion.19), channel_id=1, replica_groups=mesh['yl'=2,'zh'=4,'z0'=2,'x'=4,'yh'=2,'co'=2] {'yl','zh'}, dimensions={0} | all-to-all | bytes 2097152 | tf_op jit(solution)/shard_map/all_to_all | solution.py:214
  121.9 0.1 reduce_sum.12
  122.0 0.1 copy.22
  122.1 1.9 collective-permute-start.3
  124.1 11.8 %collective-permute-done.3 = bf16[512,128]{1,0:T(8,128)(2,1)S(1)} collective-permute-done((bf16[512,128]{1,0:T(8,128)(2,1)S(1)}, bf16[512,128]{1,0:T(8,128)(2,1)S(1)}, u32[]{:S(2)}, u32[]{:S(2)}) %collective-permute-start.3) | collective-permute-done | bytes 131104 | tf_op jit(solution)/shard_map/ppermute | solution.py:216
  135.9 1.0 fusion.31
  136.9 11.2 %all_to_all.31 = bf16[16,32,128]{2,1,0:T(8,128)(2,1)} all-to-all(bf16[16,32,128]{2,1,0:T(8,128)(2,1)S(1)} %bitcast.126), channel_id=1, replica_groups=mesh['yl'=2,'zh'=4,'z0'=2,'x'=4,'yh'=2,'co'=2] {'x','yh','co'}, dimensions={0} | all-to-all | bytes 262144 | tf_op jit(solution)/shard_map/all_to_all | solution.py:222
  148.0 3.0 %unpack.2 = bf16[64,1,32,256]{3,2,1,0:T(8,128)(2,1)} custom-call(s32[2]{0:T(128)} %pad_add_fusion.place_ref, s32[16,16]{1,0:T(8,128)} %lengths_ref.5, bf16[1,16,32,128]{3,2,1,0:T(8,128)(2,1)} %bitcast.127), custom_call_target="tpu_custom_call" | custom-call | flops 3000000 | bytes 1300000 | tf_op jit(solution)/shard_map/unpack/pallas_call | solution.py:147
  151.0 8.8 %all-to-all-start.4 = ((bf16[64,1,32,256]{3,2,1,0:T(8,128)(2,1)}), bf16[64,1,32,256]{3,2,1,0:T(8,128)(2,1)S(1)}, u32[]{:S(2)}, u32[]{:S(2)}) async-start(bf16[64,1,32,256]{3,2,1,0:T(8,128)(2,1)} %unpack.2), calls=%async_computation.4 | async-start | bytes 2097152 | tf_op jit(solution)/shard_map/all_to_all | solution.py:229
  159.8 2.0 collective-permute-start.13
  161.8 3.3 %collective-permute-start.14 = (bf16[16,32,128]{2,1,0:T(8,128)(2,1)S(1)}, bf16[16,32,128]{2,1,0:T(8,128)(2,1)S(1)}, u32[]{:S(2)}, u32[]{:S(2)}) collective-permute-start(bf16[16,32,128]{2,1,0:T(8,128)(2,1)S(1)} %copy-done.4), channel_id=1, source_target_pairs={{0,64},{32,96},{64,0},{96,32},{1,65},{33,97},{65,1},{97,33},{2,66}... | collective-permute-start | bytes 393224 | tf_op jit(solution)/shard_map/ppermute | solution.py:223
  165.0 0.0 collective-permute-start.15
  165.0 1.4 collective-permute-done.13
  166.4 14.9 %collective-permute-done.14 = bf16[16,32,128]{2,1,0:T(8,128)(2,1)S(1)} collective-permute-done((bf16[16,32,128]{2,1,0:T(8,128)(2,1)S(1)}, bf16[16,32,128]{2,1,0:T(8,128)(2,1)S(1)}, u32[]{:S(2)}, u32[]{:S(2)}) %collective-permute-start.14) | collective-permute-done | bytes 131104 | tf_op jit(solution)/shard_map/ppermute | solution.py:223
  181.3 3.7 %collective-permute-done.15 = bf16[16,32,128]{2,1,0:T(8,128)(2,1)S(1)} collective-permute-done((bf16[16,32,128]{2,1,0:T(8,128)(2,1)S(1)}, bf16[16,32,128]{2,1,0:T(8,128)(2,1)S(1)}, u32[]{:S(2)}, u32[]{:S(2)}) %collective-permute-start.15) | collective-permute-done | bytes 131104 | tf_op jit(solution)/shard_map/ppermute | solution.py:223
  184.9 0.8 pad_maximum_fusion.weights_ref
  185.7 3.8 %unpack.3 = bf16[64,3,32,256]{3,2,1,0:T(8,128)(2,1)} custom-call(s32[2]{0:T(128)} %pad_add_fusion.place_ref, s32[16,16]{1,0:T(8,128)} %lengths_ref.5, bf16[3,16,32,128]{3,2,1,0:T(8,128)(2,1)} %pad_maximum_fusion.weights_ref), custom_call_target="tpu_custom_call" | custom-call | flops 9000000 | bytes 3900000 | tf_op jit(solution)/shard_map/unpack/pallas_call | solution.py:147
  189.5 1.0 copy-done
  190.5 8.5 %all-to-all-start.5 = ((bf16[64,3,32,256]{3,2,1,0:T(8,128)(2,1)}), bf16[64,3,32,256]{3,2,1,0:T(8,128)(2,1)S(1)}, u32[]{:S(2)}, u32[]{:S(2)}) async-start(bf16[64,3,32,256]{3,2,1,0:T(8,128)(2,1)} %unpack.3), calls=%async_computation.5 | async-start | bytes 6291456 | tf_op jit(solution)/shard_map/all_to_all | solution.py:229
  199.0 1.4 collective-permute-start.4
  200.5 38.2 %collective-permute-done.4 = bf16[512,128]{1,0:T(8,128)(2,1)} collective-permute-done((bf16[512,128]{1,0:T(8,128)(2,1)S(1)}, bf16[512,128]{1,0:T(8,128)(2,1)}, u32[]{:S(2)}, u32[]{:S(2)}) %collective-permute-start.4) | collective-permute-done | bytes 131104 | tf_op jit(solution)/shard_map/ppermute | solution.py:165
  238.7 0.9 select_bitcast_fusion.1
  239.6 0.7 pad_maximum_fusion.1
  240.3 3.9 %collective-permute-start.5 = (bf16[2,512,128]{2,1,0:T(8,128)(2,1)}, bf16[2,512,128]{2,1,0:T(8,128)(2,1)}, u32[]{:S(2)}, u32[]{:S(2)}) collective-permute-start(bf16[2,512,128]{2,1,0:T(8,128)(2,1)} %pad_maximum_fusion.1), channel_id=1, source_target_pairs={{0,16},{16,32},{32,48},{48,64},{64,80},{80,96},{96,112},{112,0},{1... | collective-permute-start | bytes 786440 | tf_op jit(solution)/shard_map/ppermute | solution.py:175
  244.3 1.9 collective-permute-start.6
  246.2 0.4 broadcast_in_dim.36
  246.6 6.4 %collective-permute-done.5 = bf16[2,512,128]{2,1,0:T(8,128)(2,1)} collective-permute-done((bf16[2,512,128]{2,1,0:T(8,128)(2,1)}, bf16[2,512,128]{2,1,0:T(8,128)(2,1)}, u32[]{:S(2)}, u32[]{:S(2)}) %collective-permute-start.5) | collective-permute-done | bytes 262176 | tf_op jit(solution)/shard_map/ppermute | solution.py:175
  253.0 3.2 %collective-permute-start.8 = (bf16[2,512,128]{2,1,0:T(8,128)(2,1)}, bf16[2,512,128]{2,1,0:T(8,128)(2,1)S(1)}, u32[]{:S(2)}, u32[]{:S(2)}) collective-permute-start(bf16[2,512,128]{2,1,0:T(8,128)(2,1)} %collective-permute-done.6), channel_id=1, source_target_pairs={{0,112},{16,0},{32,16},{48,32},{64,48},{80,64},{96,80},{112,96},{1... | collective-permute-start | bytes 786440 | tf_op jit(solution)/shard_map/ppermute | solution.py:176
  256.3 1.0 bitcast_dynamic-update-slice_fusion.5
  257.2 1.0 bitcast_dynamic-update-slice_fusion.4
  258.2 3.9 %collective-permute-done.7 = bf16[2,512,128]{2,1,0:T(8,128)(2,1)S(1)} collective-permute-done((bf16[2,512,128]{2,1,0:T(8,128)(2,1)}, bf16[2,512,128]{2,1,0:T(8,128)(2,1)S(1)}, u32[]{:S(2)}, u32[]{:S(2)}) %collective-permute-start.7) | collective-permute-done | bytes 262176 | tf_op jit(solution)/shard_map/ppermute | solution.py:175
  262.1 3.2 %collective-permute-start.10 = (bf16[2,512,128]{2,1,0:T(8,128)(2,1)S(1)}, bf16[2,512,128]{2,1,0:T(8,128)(2,1)S(1)}, u32[]{:S(2)}, u32[]{:S(2)}) collective-permute-start(bf16[2,512,128]{2,1,0:T(8,128)(2,1)S(1)} %collective-permute-done.8), channel_id=1, source_target_pairs={{0,112},{16,0},{32,16},{48,32},{64,48},{80,64},{96,80},{112,96},{1... | collective-permute-start | bytes 786440 | tf_op jit(solution)/shard_map/ppermute | solution.py:176
  265.5 4.7 %collective-permute-done.9 = bf16[2,512,128]{2,1,0:T(8,128)(2,1)S(1)} collective-permute-done((bf16[2,512,128]{2,1,0:T(8,128)(2,1)S(1)}, bf16[2,512,128]{2,1,0:T(8,128)(2,1)S(1)}, u32[]{:S(2)}, u32[]{:S(2)}) %collective-permute-start.9) | collective-permute-done | bytes 262176 | tf_op jit(solution)/shard_map/ppermute | solution.py:175
  270.2 0.1 collective-permute-start.11
  270.3 3.3 %collective-permute-start.12 = (bf16[1,512,128]{2,1,0:T(8,128)(2,1)S(1)}, bf16[1,512,128]{2,1,0:T(8,128)(2,1)S(1)}, u32[]{:S(2)}, u32[]{:S(2)}) collective-permute-start(bf16[1,512,128]{2,1,0:T(8,128)(2,1)S(1)} %slice.61), channel_id=1, source_target_pairs={{0,112},{16,0},{32,16},{48,32},{64,48},{80,64},{96,80},{112,96},{1... | collective-permute-start | bytes 393224 | tf_op jit(solution)/shard_map/ppermute | solution.py:180
  273.7 2.8 collective-permute-done.11
  276.5 0.0 copy-start.2
  276.5 1.3 copy-done.2
  277.8 2.5 broadcast_in_dim.46
  280.4 1.0 constant_dynamic-update-slice_fusion
  281.4 0.0 all-to-all-done.5
  281.4 1.0 fusion.6
  282.5 1.0 fusion.5
  283.5 1.0 fusion.4
  (33 shorter events, 0.4 us)
Async XLA Ops:
  0.6 14.5 %all-to-all-start = ((bf16[16,64,256]{2,1,0:T(8,128)(2,1)}), bf16[16,64,256]{2,1,0:T(8,128)(2,1)S(1)}, u32[]{:S(2)}, u32[]{:S(2)}) async-start(bf16[16,64,256]{2,1,0:T(8,128)(2,1)} %bitcast.128), calls=%async_computation | async-start | bytes 1048576 | tf_op jit(solution)/shard_map/all_to_all | solution.py:200
  15.1 0.8 copy-start.3
  19.0 57.0 %all-to-all-start.1 = ((bf16[32,64,512]{2,1,0:T(8,128)(2,1)}), bf16[32,64,512]{2,1,0:T(8,128)(2,1)S(1)}, u32[]{:S(2)}, u32[]{:S(2)}) async-start(bf16[32,64,512]{2,1,0:T(8,128)(2,1)} %bitcast.119), calls=%async_computation.1 | async-start | bytes 4194304 | tf_op jit(solution)/shard_map/all_to_all | solution.py:202
  28.1 47.9 %collective-permute-start = (bf16[1024,512]{1,0:T(8,128)(2,1)}, bf16[1024,512]{1,0:T(8,128)(2,1)}, u32[]{:S(2)}, u32[]{:S(2)}) collective-permute-start(bf16[1024,512]{1,0:T(8,128)(2,1)} %param.6), channel_id=1, source_target_pairs={{0,16},{16,0},{1,17},{17,1},{2,18},{18,2},{3,19},{19,3},{4,20},{20... | collective-permute-start | bytes 3145736 | tf_op jit(solution)/shard_map/ppermute | solution.py:195
  29.7 50.2 %collective-permute-start.1 = (bf16[1024,512]{1,0:T(8,128)(2,1)}, bf16[1024,512]{1,0:T(8,128)(2,1)}, u32[]{:S(2)}, u32[]{:S(2)}) collective-permute-start(bf16[1024,512]{1,0:T(8,128)(2,1)} %param.6), channel_id=1, source_target_pairs={{0,1},{1,0},{2,3},{3,2},{4,5},{5,4},{6,7},{7,6},{8,9},{9,8},{10,11... | collective-permute-start | bytes 3145736 | tf_op jit(solution)/shard_map/ppermute | solution.py:197
  76.0 6.0 %collective-permute-start.2 = (bf16[1024,512]{1,0:T(8,128)(2,1)}, bf16[1024,512]{1,0:T(8,128)(2,1)}, u32[]{:S(2)}, u32[]{:S(2)}) collective-permute-start(bf16[1024,512]{1,0:T(8,128)(2,1)} %collective-permute-done), channel_id=1, source_target_pairs={{0,1},{1,0},{2,3},{3,2},{4,5},{5,4},{6,7},{7,6},{8,9},{9,8},{10,11... | collective-permute-start | bytes 3145736 | tf_op jit(solution)/shard_map/ppermute | solution.py:197
  84.0 51.8 %copy-start.5 = (f32[512,128]{1,0:T(8,128)S(1)}, f32[512,128]{1,0:T(8,128)}, u32[]{:S(2)}) copy-start(f32[512,128]{1,0:T(8,128)} %param.9) | copy-start | bytes 786436
  84.0 51.8 %copy-start.6 = (f32[512,128]{1,0:T(8,128)S(1)}, f32[512,128]{1,0:T(8,128)}, u32[]{:S(2)}) copy-start(f32[512,128]{1,0:T(8,128)} %param.11) | copy-start | bytes 786436
  84.0 51.8 %copy-start.7 = (f32[512,128]{1,0:T(8,128)S(1)}, f32[512,128]{1,0:T(8,128)}, u32[]{:S(2)}) copy-start(f32[512,128]{1,0:T(8,128)} %param.10) | copy-start | bytes 786436
  122.1 13.7 %collective-permute-start.3 = (bf16[512,128]{1,0:T(8,128)(2,1)S(1)}, bf16[512,128]{1,0:T(8,128)(2,1)S(1)}, u32[]{:S(2)}, u32[]{:S(2)}) collective-permute-start(bf16[512,128]{1,0:T(8,128)(2,1)S(1)} %copy.22), channel_id=1, source_target_pairs={{0,0},{1,20},{2,36},{3,48},{4,76},{5,88},{6,104},{7,124},{8,128},{... | collective-permute-start | bytes 393224 | tf_op jit(solution)/shard_map/ppermute | solution.py:216
  148.0 11.8 %copy-start.4 = (bf16[16,32,128]{2,1,0:T(8,128)(2,1)S(1)}, bf16[16,32,128]{2,1,0:T(8,128)(2,1)}, u32[]{:S(2)}) copy-start(bf16[16,32,128]{2,1,0:T(8,128)(2,1)} %all_to_all.31) | copy-start | bytes 393220
  151.0 38.5 %all-to-all-start.4 = ((bf16[64,1,32,256]{3,2,1,0:T(8,128)(2,1)}), bf16[64,1,32,256]{3,2,1,0:T(8,128)(2,1)S(1)}, u32[]{:S(2)}, u32[]{:S(2)}) async-start(bf16[64,1,32,256]{3,2,1,0:T(8,128)(2,1)} %unpack.2), calls=%async_computation.4 | async-start | bytes 2097152 | tf_op jit(solution)/shard_map/all_to_all | solution.py:229
  159.8 6.6 %collective-permute-start.13 = (bf16[16,32,128]{2,1,0:T(8,128)(2,1)S(1)}, bf16[16,32,128]{2,1,0:T(8,128)(2,1)S(1)}, u32[]{:S(2)}, u32[]{:S(2)}) collective-permute-start(bf16[16,32,128]{2,1,0:T(8,128)(2,1)S(1)} %copy-done.4), channel_id=1, source_target_pairs={{0,96},{32,0},{64,32},{96,64},{1,97},{33,1},{65,33},{97,65},{2,98}... | collective-permute-start | bytes 393224 | tf_op jit(solution)/shard_map/ppermute | solution.py:223
  161.8 19.5 %collective-permute-start.14 = (bf16[16,32,128]{2,1,0:T(8,128)(2,1)S(1)}, bf16[16,32,128]{2,1,0:T(8,128)(2,1)S(1)}, u32[]{:S(2)}, u32[]{:S(2)}) collective-permute-start(bf16[16,32,128]{2,1,0:T(8,128)(2,1)S(1)} %copy-done.4), channel_id=1, source_target_pairs={{0,64},{32,96},{64,0},{96,32},{1,65},{33,97},{65,1},{97,33},{2,66}... | collective-permute-start | bytes 393224 | tf_op jit(solution)/shard_map/ppermute | solution.py:223
  165.0 19.9 %collective-permute-start.15 = (bf16[16,32,128]{2,1,0:T(8,128)(2,1)S(1)}, bf16[16,32,128]{2,1,0:T(8,128)(2,1)S(1)}, u32[]{:S(2)}, u32[]{:S(2)}) collective-permute-start(bf16[16,32,128]{2,1,0:T(8,128)(2,1)S(1)} %copy-done.4), channel_id=1, source_target_pairs={{0,32},{32,64},{64,96},{96,0},{1,33},{33,65},{65,97},{97,1},{2,34}... | collective-permute-start | bytes 393224 | tf_op jit(solution)/shard_map/ppermute | solution.py:223
  189.5 1.0 copy-start
  190.5 90.9 %all-to-all-start.5 = ((bf16[64,3,32,256]{3,2,1,0:T(8,128)(2,1)}), bf16[64,3,32,256]{3,2,1,0:T(8,128)(2,1)S(1)}, u32[]{:S(2)}, u32[]{:S(2)}) async-start(bf16[64,3,32,256]{3,2,1,0:T(8,128)(2,1)} %unpack.3), calls=%async_computation.5 | async-start | bytes 6291456 | tf_op jit(solution)/shard_map/all_to_all | solution.py:229
  199.0 39.7 %collective-permute-start.4 = (bf16[512,128]{1,0:T(8,128)(2,1)S(1)}, bf16[512,128]{1,0:T(8,128)(2,1)}, u32[]{:S(2)}, u32[]{:S(2)}) collective-permute-start(bf16[512,128]{1,0:T(8,128)(2,1)S(1)} %get-tuple-element.5), channel_id=1, source_target_pairs={{0,128},{128,0},{1,129},{129,1},{2,130},{130,2},{3,131},{131,3},{4... | collective-permute-start | bytes 393224 | tf_op jit(solution)/shard_map/ppermute | solution.py:165
  240.3 12.7 %collective-permute-start.5 = (bf16[2,512,128]{2,1,0:T(8,128)(2,1)}, bf16[2,512,128]{2,1,0:T(8,128)(2,1)}, u32[]{:S(2)}, u32[]{:S(2)}) collective-permute-start(bf16[2,512,128]{2,1,0:T(8,128)(2,1)} %pad_maximum_fusion.1), channel_id=1, source_target_pairs={{0,16},{16,32},{32,48},{48,64},{64,80},{80,96},{96,112},{112,0},{1... | collective-permute-start | bytes 786440 | tf_op jit(solution)/shard_map/ppermute | solution.py:175
  244.3 8.8 %collective-permute-start.6 = (bf16[2,512,128]{2,1,0:T(8,128)(2,1)}, bf16[2,512,128]{2,1,0:T(8,128)(2,1)}, u32[]{:S(2)}, u32[]{:S(2)}) collective-permute-start(bf16[2,512,128]{2,1,0:T(8,128)(2,1)} %pad_maximum_fusion.1), channel_id=1, source_target_pairs={{0,112},{16,0},{32,16},{48,32},{64,48},{80,64},{96,80},{112,96},{1... | collective-permute-start | bytes 786440 | tf_op jit(solution)/shard_map/ppermute | solution.py:176
  253.0 9.1 %collective-permute-start.7 = (bf16[2,512,128]{2,1,0:T(8,128)(2,1)}, bf16[2,512,128]{2,1,0:T(8,128)(2,1)S(1)}, u32[]{:S(2)}, u32[]{:S(2)}) collective-permute-start(bf16[2,512,128]{2,1,0:T(8,128)(2,1)} %collective-permute-done.5), channel_id=1, source_target_pairs={{0,16},{16,32},{32,48},{48,64},{64,80},{80,96},{96,112},{112,0},{1... | collective-permute-start | bytes 786440 | tf_op jit(solution)/shard_map/ppermute | solution.py:175
  253.0 9.1 %collective-permute-start.8 = (bf16[2,512,128]{2,1,0:T(8,128)(2,1)}, bf16[2,512,128]{2,1,0:T(8,128)(2,1)S(1)}, u32[]{:S(2)}, u32[]{:S(2)}) collective-permute-start(bf16[2,512,128]{2,1,0:T(8,128)(2,1)} %collective-permute-done.6), channel_id=1, source_target_pairs={{0,112},{16,0},{32,16},{48,32},{64,48},{80,64},{96,80},{112,96},{1... | collective-permute-start | bytes 786440 | tf_op jit(solution)/shard_map/ppermute | solution.py:176
  262.1 8.1 %collective-permute-start.9 = (bf16[2,512,128]{2,1,0:T(8,128)(2,1)S(1)}, bf16[2,512,128]{2,1,0:T(8,128)(2,1)S(1)}, u32[]{:S(2)}, u32[]{:S(2)}) collective-permute-start(bf16[2,512,128]{2,1,0:T(8,128)(2,1)S(1)} %collective-permute-done.7), channel_id=1, source_target_pairs={{0,16},{16,32},{32,48},{48,64},{64,80},{80,96},{96,112},{112,0},{1... | collective-permute-start | bytes 786440 | tf_op jit(solution)/shard_map/ppermute | solution.py:175
  262.1 8.2 %collective-permute-start.10 = (bf16[2,512,128]{2,1,0:T(8,128)(2,1)S(1)}, bf16[2,512,128]{2,1,0:T(8,128)(2,1)S(1)}, u32[]{:S(2)}, u32[]{:S(2)}) collective-permute-start(bf16[2,512,128]{2,1,0:T(8,128)(2,1)S(1)} %collective-permute-done.8), channel_id=1, source_target_pairs={{0,112},{16,0},{32,16},{48,32},{64,48},{80,64},{96,80},{112,96},{1... | collective-permute-start | bytes 786440 | tf_op jit(solution)/shard_map/ppermute | solution.py:176
  270.2 6.3 %collective-permute-start.11 = (bf16[1,512,128]{2,1,0:T(8,128)(2,1)S(1)}, bf16[1,512,128]{2,1,0:T(8,128)(2,1)S(1)}, u32[]{:S(2)}, u32[]{:S(2)}) collective-permute-start(bf16[1,512,128]{2,1,0:T(8,128)(2,1)S(1)} %slice.60), channel_id=1, source_target_pairs={{0,16},{16,32},{32,48},{48,64},{64,80},{80,96},{96,112},{112,0},{1... | collective-permute-start | bytes 393224 | tf_op jit(solution)/shard_map/ppermute | solution.py:179
  270.3 6.2 %collective-permute-start.12 = (bf16[1,512,128]{2,1,0:T(8,128)(2,1)S(1)}, bf16[1,512,128]{2,1,0:T(8,128)(2,1)S(1)}, u32[]{:S(2)}, u32[]{:S(2)}) collective-permute-start(bf16[1,512,128]{2,1,0:T(8,128)(2,1)S(1)} %slice.61), channel_id=1, source_target_pairs={{0,112},{16,0},{32,16},{48,32},{64,48},{80,64},{96,80},{112,96},{1... | collective-permute-start | bytes 393224 | tf_op jit(solution)/shard_map/ppermute | solution.py:180
  276.5 1.3 copy-start.2
  277.8 2.6 copy-start.1

commit v5 on v4

--- a/solution.py
+++ b/solution.py
@@ -160,7 +160,7 @@
     return [(k, (k + step) % 8) for k in range(8)]
 
 
-def all_rows(weights):
+def all_rows(weights, ahead):
     yl, z = lax.axis_index("yl"), lax.axis_index(Z)
     other = lax.ppermute(weights, "yl", SWAP)
     pair = jnp.stack([jnp.where(yl == 0, weights, other), jnp.where(yl == 0, other, weights)])
@@ -176,11 +176,12 @@
         down = lax.ppermute(down, Z, ring(-1))
         out = put(out, up, 0, 8 - k)
         out = put(out, down, 0, k)
+    up, down, ahead = lax.optimization_barrier((up, down, ahead))
     up = lax.ppermute(up[:1], Z, ring(1))
     down = lax.ppermute(down[1:], Z, ring(-1))
     out = put(out, up, 0, 4)
     out = put(out, down, 1, 4)
-    return out.reshape(-1, weights.shape[1])
+    return out.reshape(-1, weights.shape[1]), ahead
 
 
 def product(tokens, dense):
@@ -220,9 +221,12 @@
     weights = new_master.astype(jnp.bfloat16)
 
     rows = lax.all_to_all(weights.reshape(16, 32, 128), TP, split_axis=0, concat_axis=0, tiled=True)
-    others = [lax.ppermute(rows, "zh", [(k, (k + step) % 4) for k in range(4)]) for step in (3, 2, 1)]
+    others = []
+    for step in (3, 2, 1):
+        others.append(lax.ppermute(rows, "zh", [(k, (k + step) % 4) for k in range(4)]))
     zh = lax.axis_index("zh")
     slot_weights = jnp.zeros((2, 4, 2, 16, 32, slot_width), weights.dtype)
+    healthy = None
     distance = 0
     for pieces in (rows[None], jnp.stack(others)):
         outgoing = slot_columns(pieces, lengths, place)
@@ -233,8 +237,9 @@
                 slot_weights, incoming[:, piece : piece + 1], (0, (zh + distance) % 4, 0, 0, 0, 0)
             )
             distance += 1
+        if healthy is None:
+            healthy, slot_weights = all_rows(weights, slot_weights)
     slot_weights = slot_weights.reshape(1, -1, slot_width)
-    healthy = all_rows(weights)
     return (new_master, new_first, new_second, healthy, slot_weights)
 
 

time: 285 us -> 286 us (level)
  waiting for transfers between devices: 141 us -> 137 us
  local copies, waits for them, and re-layouts: 12.6 us -> 16 us
    ppermute x3, waiting for transfers between devices: 15 us -> 6.14 us  [all_rows(): up = lax.ppermute(up, Z, ring(1))]
    dynamic_update_slice x8, local copies, waits for them, and re-layouts: 2.17 us -> 7.81 us  [put(): lax.dynamic_update_slice(out, piece[:, None], (first, (z + distance) % 8,...]
    ppermute x3, waiting for transfers between devices: 0.01 us -> 5.47 us  [all_rows(): down = lax.ppermute(down, Z, ring(-1))]
    ppermute x3, starting transfers between devices: 8.38 us -> 13.1 us  [all_rows(): down = lax.ppermute(down, Z, ring(-1))]
    ppermute x3, starting transfers between devices: 3.93 us -> 0.01 us  [all_rows(): up = lax.ppermute(up, Z, ring(1))]
  transfers between devices with their start and end apart: 20 -> 20, of which waited for: 11 -> 11; matrix products, arithmetic and copies ran while one was open for 5% -> 7% of each run, Pallas kernels for 1% -> 1%
where the time goes in v5:
time: 286 us; the launch traced here: 285 us
  waiting for transfers between devices  137 us (48%)
  starting transfers between devices  60.1 us (21%)
  blocking collectives  48.9 us (17%)
  local copies, waits for them, and re-layouts  16 us (6%)
  Pallas kernels  9.9 us (3%)
  matrix products  7.84 us (3%)
  other arithmetic  4.89 us (2%)
    ppermute x1, waiting for transfers between devices, on_device(): across = lax.ppermute(tokens, 'z0', SWAP)  46.3 us
    ppermute x1, waiting for transfers between devices, all_rows(): other = lax.ppermute(weights, 'yl', SWAP)  38.2 us
    all_to_all x1, blocking collectives, on_device(): lax.all_to_all(jnp.stack(blocks), SUM, split_axis=0, concat_axis=0, tiled...  37.8 us
    ppermute x3, waiting for transfers between devices, on_device(): lax.ppermute(rows, 'zh', [(k, (k + step) % 4) for k in range(4)])  19.9 us
    all_to_all x2, starting transfers between devices, on_device(): lax.all_to_all(outgoing, GROUP, split_axis=0, concat_axis=0, tiled=True)  17.3 us
    ppermute x3, starting transfers between devices, all_rows(): down = lax.ppermute(down, Z, ring(-1))  13.1 us
    ppermute x1, waiting for transfers between devices, on_device(): gradient = lax.ppermute(summed, AXES, home_permutation())  11.8 us
    all_to_all x1, blocking collectives, on_device(): lax.all_to_all(weights.reshape(16, 32, 128), TP, split_axis=0, concat_axi...  11.2 us
  transfers between devices with their start and end apart: 20, of which 11 were waited for; matrix products, arithmetic and copies ran while one was open for 7% of the time, Pallas kernels for 1%

profile of v5, /device:TPU:22, one launch (start us, length us, event | category | flops | bytes accessed | tf_op | source)
XLA Modules:
  0.0 285.2 jit_solution(3749022703238438710)
XLA Ops:
  0.6 7.2 %all-to-all-start = ((bf16[16,64,256]{2,1,0:T(8,128)(2,1)}), bf16[16,64,256]{2,1,0:T(8,128)(2,1)S(1)}, u32[]{:S(2)}, u32[]{:S(2)}) async-start(bf16[16,64,256]{2,1,0:T(8,128)(2,1)} %bitcast.128), calls=%async_computation | async-start | bytes 1048576 | tf_op jit(solution)/shard_map/all_to_all | solution.py:201
  7.8 0.6 pad_add_fusion.place_ref
  8.4 6.7 %all-to-all-done.slots_ref = bf16[16,64,256]{2,1,0:T(8,128)(2,1)S(1)} async-done(((bf16[16,64,256]{2,1,0:T(8,128)(2,1)}), bf16[16,64,256]{2,1,0:T(8,128)(2,1)S(1)}, u32[]{:S(2)}, u32[]{:S(2)}) %all-to-all-start) | async-done | bytes 524320 | tf_op jit(solution)/shard_map/all_to_all | solution.py:201
  15.1 0.8 copy-done.3
  15.9 3.1 %pack.1 = bf16[2,8,2,64,512]{4,3,2,1,0:T(8,128)(2,1)} custom-call(s32[2]{0:T(128)} %pad_add_fusion.place_ref, s32[16,16]{1,0:T(8,128)} %lengths_ref.5, bf16[16,64,256]{2,1,0:T(8,128)(2,1)} %copy-done.3), custom_call_target="tpu_custom_call" | custom-call | flops 1000000 | bytes 5000000 | tf_op jit(solution)/shard_map/pack/pallas_call | solution.py:102
  19.0 9.1 %all-to-all-start.1 = ((bf16[32,64,512]{2,1,0:T(8,128)(2,1)}), bf16[32,64,512]{2,1,0:T(8,128)(2,1)S(1)}, u32[]{:S(2)}, u32[]{:S(2)}) async-start(bf16[32,64,512]{2,1,0:T(8,128)(2,1)} %bitcast.119), calls=%async_computation.1 | async-start | bytes 4194304 | tf_op jit(solution)/shard_map/all_to_all | solution.py:203
  28.1 1.6 collective-permute-start
  29.7 46.3 %collective-permute-done = bf16[1024,512]{1,0:T(8,128)(2,1)} collective-permute-done((bf16[1024,512]{1,0:T(8,128)(2,1)}, bf16[1024,512]{1,0:T(8,128)(2,1)}, u32[]{:S(2)}, u32[]{:S(2)}) %collective-permute-start) | collective-permute-done | bytes 1048608 | tf_op jit(solution)/shard_map/ppermute | solution.py:196
  76.0 2.0 fusion.11
  78.0 2.0 fusion.3
  80.0 2.0 fusion.9
  81.9 0.0 collective-permute-done.2
  82.0 2.0 fusion.2
  84.0 0.0 copy-start.5
  84.0 0.0 copy-start.6
  84.0 0.0 copy-start.7
  84.1 37.8 %all_to_all.30 = bf16[8,512,128]{1,2,0:T(8,128)(2,1)S(1)} all-to-all(bf16[8,512,128]{1,2,0:T(8,128)(2,1)S(1)} %fusion.19), channel_id=1, replica_groups=mesh['yl'=2,'zh'=4,'z0'=2,'x'=4,'yh'=2,'co'=2] {'yl','zh'}, dimensions={0} | all-to-all | bytes 2097152 | tf_op jit(solution)/shard_map/all_to_all | solution.py:215
  121.9 0.1 reduce_sum.12
  122.0 0.1 copy.22
  122.1 1.9 collective-permute-start.3
  124.1 11.8 %collective-permute-done.3 = bf16[512,128]{1,0:T(8,128)(2,1)S(1)} collective-permute-done((bf16[512,128]{1,0:T(8,128)(2,1)S(1)}, bf16[512,128]{1,0:T(8,128)(2,1)S(1)}, u32[]{:S(2)}, u32[]{:S(2)}) %collective-permute-start.3) | collective-permute-done | bytes 131104 | tf_op jit(solution)/shard_map/ppermute | solution.py:217
  135.9 1.0 fusion.31
  136.9 11.2 %all_to_all.31 = bf16[16,32,128]{2,1,0:T(8,128)(2,1)} all-to-all(bf16[16,32,128]{2,1,0:T(8,128)(2,1)S(1)} %bitcast.126), channel_id=1, replica_groups=mesh['yl'=2,'zh'=4,'z0'=2,'x'=4,'yh'=2,'co'=2] {'x','yh','co'}, dimensions={0} | all-to-all | bytes 262144 | tf_op jit(solution)/shard_map/all_to_all | solution.py:223
  148.0 3.0 %unpack.2 = bf16[64,1,32,256]{3,2,1,0:T(8,128)(2,1)} custom-call(s32[2]{0:T(128)} %pad_add_fusion.place_ref, s32[16,16]{1,0:T(8,128)} %lengths_ref.5, bf16[1,16,32,128]{3,2,1,0:T(8,128)(2,1)} %bitcast.127), custom_call_target="tpu_custom_call" | custom-call | flops 3000000 | bytes 1300000 | tf_op jit(solution)/shard_map/unpack/pallas_call | solution.py:147
  151.0 8.8 %all-to-all-start.4 = ((bf16[64,1,32,256]{3,2,1,0:T(8,128)(2,1)}), bf16[64,1,32,256]{3,2,1,0:T(8,128)(2,1)S(1)}, u32[]{:S(2)}, u32[]{:S(2)}) async-start(bf16[64,1,32,256]{3,2,1,0:T(8,128)(2,1)} %unpack.2), calls=%async_computation.4 | async-start | bytes 2097152 | tf_op jit(solution)/shard_map/all_to_all | solution.py:233
  159.8 2.0 collective-permute-start.13
  161.8 3.3 %collective-permute-start.14 = (bf16[16,32,128]{2,1,0:T(8,128)(2,1)S(1)}, bf16[16,32,128]{2,1,0:T(8,128)(2,1)S(1)}, u32[]{:S(2)}, u32[]{:S(2)}) collective-permute-start(bf16[16,32,128]{2,1,0:T(8,128)(2,1)S(1)} %copy-done.4), channel_id=1, source_target_pairs={{0,64},{32,96},{64,0},{96,32},{1,65},{33,97},{65,1},{97,33},{2,66}... | collective-permute-start | bytes 393224 | tf_op jit(solution)/shard_map/ppermute | solution.py:226
  165.0 1.4 collective-permute-done.13
  166.4 14.9 %collective-permute-done.14 = bf16[16,32,128]{2,1,0:T(8,128)(2,1)S(1)} collective-permute-done((bf16[16,32,128]{2,1,0:T(8,128)(2,1)S(1)}, bf16[16,32,128]{2,1,0:T(8,128)(2,1)S(1)}, u32[]{:S(2)}, u32[]{:S(2)}) %collective-permute-start.14) | collective-permute-done | bytes 131104 | tf_op jit(solution)/shard_map/ppermute | solution.py:226
  181.3 3.7 %collective-permute-done.15 = bf16[16,32,128]{2,1,0:T(8,128)(2,1)S(1)} collective-permute-done((bf16[16,32,128]{2,1,0:T(8,128)(2,1)S(1)}, bf16[16,32,128]{2,1,0:T(8,128)(2,1)S(1)}, u32[]{:S(2)}, u32[]{:S(2)}) %collective-permute-start.15) | collective-permute-done | bytes 131104 | tf_op jit(solution)/shard_map/ppermute | solution.py:226
  184.9 0.8 pad_maximum_fusion.weights_ref
  185.7 3.8 %unpack.3 = bf16[64,3,32,256]{3,2,1,0:T(8,128)(2,1)} custom-call(s32[2]{0:T(128)} %pad_add_fusion.place_ref, s32[16,16]{1,0:T(8,128)} %lengths_ref.5, bf16[3,16,32,128]{3,2,1,0:T(8,128)(2,1)} %pad_maximum_fusion.weights_ref), custom_call_target="tpu_custom_call" | custom-call | flops 9000000 | bytes 3900000 | tf_op jit(solution)/shard_map/unpack/pallas_call | solution.py:147
  189.5 1.0 copy-done
  190.5 8.5 %all-to-all-start.5 = ((bf16[64,3,32,256]{3,2,1,0:T(8,128)(2,1)}), bf16[64,3,32,256]{3,2,1,0:T(8,128)(2,1)S(1)}, u32[]{:S(2)}, u32[]{:S(2)}) async-start(bf16[64,3,32,256]{3,2,1,0:T(8,128)(2,1)} %unpack.3), calls=%async_computation.5 | async-start | bytes 6291456 | tf_op jit(solution)/shard_map/all_to_all | solution.py:233
  199.0 1.4 collective-permute-start.4
  200.5 38.2 %collective-permute-done.4 = bf16[512,128]{1,0:T(8,128)(2,1)} collective-permute-done((bf16[512,128]{1,0:T(8,128)(2,1)S(1)}, bf16[512,128]{1,0:T(8,128)(2,1)}, u32[]{:S(2)}, u32[]{:S(2)}) %collective-permute-start.4) | collective-permute-done | bytes 131104 | tf_op jit(solution)/shard_map/ppermute | solution.py:165
  238.7 0.9 select_bitcast_fusion.1
  239.6 0.7 pad_maximum_fusion.1
  240.3 5.8 %collective-permute-start.6 = (bf16[2,512,128]{2,1,0:T(8,128)(2,1)}, bf16[2,512,128]{2,1,0:T(8,128)(2,1)}, u32[]{:S(2)}, u32[]{:S(2)}) collective-permute-start(bf16[2,512,128]{2,1,0:T(8,128)(2,1)} %pad_maximum_fusion.1), channel_id=1, source_target_pairs={{0,112},{16,0},{32,16},{48,32},{64,48},{80,64},{96,80},{112,96},{1... | collective-permute-start | bytes 786440 | tf_op jit(solution)/shard_map/ppermute | solution.py:176
  246.2 1.7 broadcast_in_dim.36
  247.9 0.7 bitcast_dynamic-update-slice_fusion.6
  248.6 3.7 %collective-permute-done.6 = bf16[2,512,128]{2,1,0:T(8,128)(2,1)} collective-permute-done((bf16[2,512,128]{2,1,0:T(8,128)(2,1)}, bf16[2,512,128]{2,1,0:T(8,128)(2,1)}, u32[]{:S(2)}, u32[]{:S(2)}) %collective-permute-start.6) | collective-permute-done | bytes 262176 | tf_op jit(solution)/shard_map/ppermute | solution.py:176
  252.3 3.7 %collective-permute-start.8 = (bf16[2,512,128]{2,1,0:T(8,128)(2,1)}, bf16[2,512,128]{2,1,0:T(8,128)(2,1)S(1)}, u32[]{:S(2)}, u32[]{:S(2)}) collective-permute-start(bf16[2,512,128]{2,1,0:T(8,128)(2,1)} %collective-permute-done.6), channel_id=1, source_target_pairs={{0,112},{16,0},{32,16},{48,32},{64,48},{80,64},{96,80},{112,96},{1... | collective-permute-start | bytes 786440 | tf_op jit(solution)/shard_map/ppermute | solution.py:176
  256.0 1.7 bitcast_dynamic-update-slice_fusion.5
  257.7 1.7 bitcast_dynamic-update-slice_fusion.4
  259.4 1.8 collective-permute-done.8
  261.2 3.6 %collective-permute-start.10 = (bf16[2,512,128]{2,1,0:T(8,128)(2,1)S(1)}, bf16[2,512,128]{2,1,0:T(8,128)(2,1)S(1)}, u32[]{:S(2)}, u32[]{:S(2)}) collective-permute-start(bf16[2,512,128]{2,1,0:T(8,128)(2,1)S(1)} %collective-permute-done.8), channel_id=1, source_target_pairs={{0,112},{16,0},{32,16},{48,32},{64,48},{80,64},{96,80},{112,96},{1... | collective-permute-start | bytes 786440 | tf_op jit(solution)/shard_map/ppermute | solution.py:176
  264.8 0.7 bitcast_dynamic-update-slice_fusion.3
  265.5 0.7 bitcast_dynamic-update-slice_fusion.2
  266.3 6.1 %collective-permute-done.9 = bf16[2,512,128]{2,1,0:T(8,128)(2,1)S(1)} collective-permute-done((bf16[2,512,128]{2,1,0:T(8,128)(2,1)S(1)}, bf16[2,512,128]{2,1,0:T(8,128)(2,1)S(1)}, u32[]{:S(2)}, u32[]{:S(2)}) %collective-permute-start.9) | collective-permute-done | bytes 262176 | tf_op jit(solution)/shard_map/ppermute | solution.py:175
  272.4 0.7 bitcast_dynamic-update-slice_fusion.1
  273.1 0.5 broadcast_in_dim.44
  273.6 0.7 copy-done.1
  274.3 0.1 constant_dynamic-update-slice_fusion
  274.4 0.0 copy-start.2
  274.5 0.1 collective-permute-start.11
  274.6 0.9 bitcast_dynamic-update-slice_fusion
  275.5 3.1 %collective-permute-start.12 = (bf16[1,512,128]{2,1,0:T(8,128)(2,1)S(1)}, bf16[1,512,128]{2,1,0:T(8,128)(2,1)S(1)}, u32[]{:S(2)}, u32[]{:S(2)}) collective-permute-start(bf16[1,512,128]{2,1,0:T(8,128)(2,1)S(1)} %slice.48), channel_id=1, source_target_pairs={{0,112},{16,0},{32,16},{48,32},{64,48},{80,64},{96,80},{112,96},{1... | collective-permute-start | bytes 393224 | tf_op jit(solution)/shard_map/ppermute | solution.py:181
  278.6 2.1 collective-permute-done.11
  280.7 0.7 bitcast_dynamic-update-slice_fusion.8
  281.4 0.7 bitcast_dynamic-update-slice_fusion.7
  282.1 1.0 fusion.6
  283.1 1.0 fusion.5
  284.1 1.0 fusion.4
  (33 shorter events, 0.2 us)
Async XLA Ops:
  0.6 14.5 %all-to-all-start = ((bf16[16,64,256]{2,1,0:T(8,128)(2,1)}), bf16[16,64,256]{2,1,0:T(8,128)(2,1)S(1)}, u32[]{:S(2)}, u32[]{:S(2)}) async-start(bf16[16,64,256]{2,1,0:T(8,128)(2,1)} %bitcast.128), calls=%async_computation | async-start | bytes 1048576 | tf_op jit(solution)/shard_map/all_to_all | solution.py:201
  15.1 0.8 copy-start.3
  19.0 57.0 %all-to-all-start.1 = ((bf16[32,64,512]{2,1,0:T(8,128)(2,1)}), bf16[32,64,512]{2,1,0:T(8,128)(2,1)S(1)}, u32[]{:S(2)}, u32[]{:S(2)}) async-start(bf16[32,64,512]{2,1,0:T(8,128)(2,1)} %bitcast.119), calls=%async_computation.1 | async-start | bytes 4194304 | tf_op jit(solution)/shard_map/all_to_all | solution.py:203
  28.1 47.9 %collective-permute-start = (bf16[1024,512]{1,0:T(8,128)(2,1)}, bf16[1024,512]{1,0:T(8,128)(2,1)}, u32[]{:S(2)}, u32[]{:S(2)}) collective-permute-start(bf16[1024,512]{1,0:T(8,128)(2,1)} %param.6), channel_id=1, source_target_pairs={{0,16},{16,0},{1,17},{17,1},{2,18},{18,2},{3,19},{19,3},{4,20},{20... | collective-permute-start | bytes 3145736 | tf_op jit(solution)/shard_map/ppermute | solution.py:196
  29.7 50.2 %collective-permute-start.1 = (bf16[1024,512]{1,0:T(8,128)(2,1)}, bf16[1024,512]{1,0:T(8,128)(2,1)}, u32[]{:S(2)}, u32[]{:S(2)}) collective-permute-start(bf16[1024,512]{1,0:T(8,128)(2,1)} %param.6), channel_id=1, source_target_pairs={{0,1},{1,0},{2,3},{3,2},{4,5},{5,4},{6,7},{7,6},{8,9},{9,8},{10,11... | collective-permute-start | bytes 3145736 | tf_op jit(solution)/shard_map/ppermute | solution.py:198
  76.0 6.0 %collective-permute-start.2 = (bf16[1024,512]{1,0:T(8,128)(2,1)}, bf16[1024,512]{1,0:T(8,128)(2,1)}, u32[]{:S(2)}, u32[]{:S(2)}) collective-permute-start(bf16[1024,512]{1,0:T(8,128)(2,1)} %collective-permute-done), channel_id=1, source_target_pairs={{0,1},{1,0},{2,3},{3,2},{4,5},{5,4},{6,7},{7,6},{8,9},{9,8},{10,11... | collective-permute-start | bytes 3145736 | tf_op jit(solution)/shard_map/ppermute | solution.py:198
  84.0 51.8 %copy-start.5 = (f32[512,128]{1,0:T(8,128)S(1)}, f32[512,128]{1,0:T(8,128)}, u32[]{:S(2)}) copy-start(f32[512,128]{1,0:T(8,128)} %param.9) | copy-start | bytes 786436
  84.0 51.8 %copy-start.6 = (f32[512,128]{1,0:T(8,128)S(1)}, f32[512,128]{1,0:T(8,128)}, u32[]{:S(2)}) copy-start(f32[512,128]{1,0:T(8,128)} %param.11) | copy-start | bytes 786436
  84.0 51.8 %copy-start.7 = (f32[512,128]{1,0:T(8,128)S(1)}, f32[512,128]{1,0:T(8,128)}, u32[]{:S(2)}) copy-start(f32[512,128]{1,0:T(8,128)} %param.10) | copy-start | bytes 786436
  122.1 13.7 %collective-permute-start.3 = (bf16[512,128]{1,0:T(8,128)(2,1)S(1)}, bf16[512,128]{1,0:T(8,128)(2,1)S(1)}, u32[]{:S(2)}, u32[]{:S(2)}) collective-permute-start(bf16[512,128]{1,0:T(8,128)(2,1)S(1)} %copy.22), channel_id=1, source_target_pairs={{0,0},{1,20},{2,36},{3,48},{4,76},{5,88},{6,104},{7,124},{8,128},{... | collective-permute-start | bytes 393224 | tf_op jit(solution)/shard_map/ppermute | solution.py:217
  148.0 11.8 %copy-start.4 = (bf16[16,32,128]{2,1,0:T(8,128)(2,1)S(1)}, bf16[16,32,128]{2,1,0:T(8,128)(2,1)}, u32[]{:S(2)}) copy-start(bf16[16,32,128]{2,1,0:T(8,128)(2,1)} %all_to_all.31) | copy-start | bytes 393220
  151.0 38.5 %all-to-all-start.4 = ((bf16[64,1,32,256]{3,2,1,0:T(8,128)(2,1)}), bf16[64,1,32,256]{3,2,1,0:T(8,128)(2,1)S(1)}, u32[]{:S(2)}, u32[]{:S(2)}) async-start(bf16[64,1,32,256]{3,2,1,0:T(8,128)(2,1)} %unpack.2), calls=%async_computation.4 | async-start | bytes 2097152 | tf_op jit(solution)/shard_map/all_to_all | solution.py:233
  159.8 6.6 %collective-permute-start.13 = (bf16[16,32,128]{2,1,0:T(8,128)(2,1)S(1)}, bf16[16,32,128]{2,1,0:T(8,128)(2,1)S(1)}, u32[]{:S(2)}, u32[]{:S(2)}) collective-permute-start(bf16[16,32,128]{2,1,0:T(8,128)(2,1)S(1)} %copy-done.4), channel_id=1, source_target_pairs={{0,96},{32,0},{64,32},{96,64},{1,97},{33,1},{65,33},{97,65},{2,98}... | collective-permute-start | bytes 393224 | tf_op jit(solution)/shard_map/ppermute | solution.py:226
  161.8 19.5 %collective-permute-start.14 = (bf16[16,32,128]{2,1,0:T(8,128)(2,1)S(1)}, bf16[16,32,128]{2,1,0:T(8,128)(2,1)S(1)}, u32[]{:S(2)}, u32[]{:S(2)}) collective-permute-start(bf16[16,32,128]{2,1,0:T(8,128)(2,1)S(1)} %copy-done.4), channel_id=1, source_target_pairs={{0,64},{32,96},{64,0},{96,32},{1,65},{33,97},{65,1},{97,33},{2,66}... | collective-permute-start | bytes 393224 | tf_op jit(solution)/shard_map/ppermute | solution.py:226
  165.0 19.9 %collective-permute-start.15 = (bf16[16,32,128]{2,1,0:T(8,128)(2,1)S(1)}, bf16[16,32,128]{2,1,0:T(8,128)(2,1)S(1)}, u32[]{:S(2)}, u32[]{:S(2)}) collective-permute-start(bf16[16,32,128]{2,1,0:T(8,128)(2,1)S(1)} %copy-done.4), channel_id=1, source_target_pairs={{0,32},{32,64},{64,96},{96,0},{1,33},{33,65},{65,97},{97,1},{2,34}... | collective-permute-start | bytes 393224 | tf_op jit(solution)/shard_map/ppermute | solution.py:226
  189.5 1.0 copy-start
  190.5 91.6 %all-to-all-start.5 = ((bf16[64,3,32,256]{3,2,1,0:T(8,128)(2,1)}), bf16[64,3,32,256]{3,2,1,0:T(8,128)(2,1)S(1)}, u32[]{:S(2)}, u32[]{:S(2)}) async-start(bf16[64,3,32,256]{3,2,1,0:T(8,128)(2,1)} %unpack.3), calls=%async_computation.5 | async-start | bytes 6291456 | tf_op jit(solution)/shard_map/all_to_all | solution.py:233
  199.0 39.7 %collective-permute-start.4 = (bf16[512,128]{1,0:T(8,128)(2,1)S(1)}, bf16[512,128]{1,0:T(8,128)(2,1)}, u32[]{:S(2)}, u32[]{:S(2)}) collective-permute-start(bf16[512,128]{1,0:T(8,128)(2,1)S(1)} %get-tuple-element.11), channel_id=1, source_target_pairs={{0,128},{128,0},{1,129},{129,1},{2,130},{130,2},{3,131},{131,3},{4... | collective-permute-start | bytes 393224 | tf_op jit(solution)/shard_map/ppermute | solution.py:165
  240.3 11.9 %collective-permute-start.6 = (bf16[2,512,128]{2,1,0:T(8,128)(2,1)}, bf16[2,512,128]{2,1,0:T(8,128)(2,1)}, u32[]{:S(2)}, u32[]{:S(2)}) collective-permute-start(bf16[2,512,128]{2,1,0:T(8,128)(2,1)} %pad_maximum_fusion.1), channel_id=1, source_target_pairs={{0,112},{16,0},{32,16},{48,32},{64,48},{80,64},{96,80},{112,96},{1... | collective-permute-start | bytes 786440 | tf_op jit(solution)/shard_map/ppermute | solution.py:176
  246.2 9.8 %collective-permute-start.5 = (bf16[2,512,128]{2,1,0:T(8,128)(2,1)}, bf16[2,512,128]{2,1,0:T(8,128)(2,1)}, u32[]{:S(2)}, u32[]{:S(2)}) collective-permute-start(bf16[2,512,128]{2,1,0:T(8,128)(2,1)} %pad_maximum_fusion.1), channel_id=1, source_target_pairs={{0,16},{16,32},{32,48},{48,64},{64,80},{80,96},{96,112},{112,0},{1... | collective-permute-start | bytes 786440 | tf_op jit(solution)/shard_map/ppermute | solution.py:175
  252.3 8.9 %collective-permute-start.8 = (bf16[2,512,128]{2,1,0:T(8,128)(2,1)}, bf16[2,512,128]{2,1,0:T(8,128)(2,1)S(1)}, u32[]{:S(2)}, u32[]{:S(2)}) collective-permute-start(bf16[2,512,128]{2,1,0:T(8,128)(2,1)} %collective-permute-done.6), channel_id=1, source_target_pairs={{0,112},{16,0},{32,16},{48,32},{64,48},{80,64},{96,80},{112,96},{1... | collective-permute-start | bytes 786440 | tf_op jit(solution)/shard_map/ppermute | solution.py:176
  256.0 8.8 %collective-permute-start.7 = (bf16[2,512,128]{2,1,0:T(8,128)(2,1)}, bf16[2,512,128]{2,1,0:T(8,128)(2,1)S(1)}, u32[]{:S(2)}, u32[]{:S(2)}) collective-permute-start(bf16[2,512,128]{2,1,0:T(8,128)(2,1)} %collective-permute-done.5), channel_id=1, source_target_pairs={{0,16},{16,32},{32,48},{48,64},{64,80},{80,96},{96,112},{112,0},{1... | collective-permute-start | bytes 786440 | tf_op jit(solution)/shard_map/ppermute | solution.py:175
  261.2 13.2 %collective-permute-start.10 = (bf16[2,512,128]{2,1,0:T(8,128)(2,1)S(1)}, bf16[2,512,128]{2,1,0:T(8,128)(2,1)S(1)}, u32[]{:S(2)}, u32[]{:S(2)}) collective-permute-start(bf16[2,512,128]{2,1,0:T(8,128)(2,1)S(1)} %collective-permute-done.8), channel_id=1, source_target_pairs={{0,112},{16,0},{32,16},{48,32},{64,48},{80,64},{96,80},{112,96},{1... | collective-permute-start | bytes 786440 | tf_op jit(solution)/shard_map/ppermute | solution.py:176
  264.8 7.6 %collective-permute-start.9 = (bf16[2,512,128]{2,1,0:T(8,128)(2,1)S(1)}, bf16[2,512,128]{2,1,0:T(8,128)(2,1)S(1)}, u32[]{:S(2)}, u32[]{:S(2)}) collective-permute-start(bf16[2,512,128]{2,1,0:T(8,128)(2,1)S(1)} %collective-permute-done.7), channel_id=1, source_target_pairs={{0,16},{16,32},{32,48},{48,64},{64,80},{80,96},{96,112},{112,0},{1... | collective-permute-start | bytes 786440 | tf_op jit(solution)/shard_map/ppermute | solution.py:175
  273.1 1.2 copy-start.1
  274.4 7.0 %copy-start.2 = (bf16[2,4,2,16,32,256]{5,4,3,2,1,0:T(8,128)(2,1)}, bf16[2,4,2,16,32,256]{5,4,3,2,1,0:T(8,128)(2,1)S(1)}, u32[]{:S(2)}) copy-start(bf16[2,4,2,16,32,256]{5,4,3,2,1,0:T(8,128)(2,1)S(1)} %constant_dynamic-update-slice_fusion) | copy-start | bytes 12582916
  274.5 6.3 %collective-permute-start.11 = (bf16[1,512,128]{2,1,0:T(8,128)(2,1)S(1)}, bf16[1,512,128]{2,1,0:T(8,128)(2,1)S(1)}, u32[]{:S(2)}, u32[]{:S(2)}) collective-permute-start(bf16[1,512,128]{2,1,0:T(8,128)(2,1)S(1)} %slice.47), channel_id=1, source_target_pairs={{0,16},{16,32},{32,48},{48,64},{64,80},{80,96},{96,112},{112,0},{1... | collective-permute-start | bytes 393224 | tf_op jit(solution)/shard_map/ppermute | solution.py:180
  275.5 5.9 %collective-permute-start.12 = (bf16[1,512,128]{2,1,0:T(8,128)(2,1)S(1)}, bf16[1,512,128]{2,1,0:T(8,128)(2,1)S(1)}, u32[]{:S(2)}, u32[]{:S(2)}) collective-permute-start(bf16[1,512,128]{2,1,0:T(8,128)(2,1)S(1)} %slice.48), channel_id=1, source_target_pairs={{0,112},{16,0},{32,16},{48,32},{64,48},{80,64},{96,80},{112,96},{1... | collective-permute-start | bytes 393224 | tf_op jit(solution)/shard_map/ppermute | solution.py:181

commit v6 on v4

--- a/solution.py
+++ b/solution.py
@@ -222,12 +222,16 @@
     rows = lax.all_to_all(weights.reshape(16, 32, 128), TP, split_axis=0, concat_axis=0, tiled=True)
     others = [lax.ppermute(rows, "zh", [(k, (k + step) % 4) for k in range(4)]) for step in (3, 2, 1)]
     zh = lax.axis_index("zh")
-    slot_weights = jnp.zeros((2, 4, 2, 16, 32, slot_width), weights.dtype)
+    slot_weights = None
     distance = 0
     for pieces in (rows[None], jnp.stack(others)):
         outgoing = slot_columns(pieces, lengths, place)
         incoming = lax.all_to_all(outgoing, GROUP, split_axis=0, concat_axis=0, tiled=True)
         incoming = incoming.reshape(2, 2, 16, -1, 32, slot_width).transpose(0, 3, 1, 2, 4, 5)
+        if slot_weights is None:
+            slot_weights = jnp.broadcast_to(incoming, (2, 4, *incoming.shape[2:]))
+            distance = 1
+            continue
         for piece in range(incoming.shape[1]):
             slot_weights = lax.dynamic_update_slice(
                 slot_weights, incoming[:, piece : piece + 1], (0, (zh + distance) % 4, 0, 0, 0, 0)

time: 285 us -> 283 us (level)
  waiting for transfers between devices: 141 us -> 135 us
    dynamic_update_slice x8, local copies, waits for them, and re-layouts: 2.17 us -> 7.6 us  [put(): lax.dynamic_update_slice(out, piece[:, None], (first, (z + distance) % 8,...]
    ppermute x3, waiting for transfers between devices: 15 us -> 10.2 us  [all_rows(): up = lax.ppermute(up, Z, ring(1))]
    dynamic_update_slice x4 -> x3, local copies, waits for them, and re-layouts: 4.15 us -> 0.26 us  [on_device(): lax.dynamic_update_slice(slot_weights, incoming[:, piece:piece + 1], (0,...]
  transfers between devices with their start and end apart: 20 -> 20, of which waited for: 11 -> 11; matrix products, arithmetic and copies ran while one was open for 5% -> 7% of each run, Pallas kernels for 1% -> 1%
where the time goes in v6:
time: 283 us; the launch traced here: 282 us
  waiting for transfers between devices  135 us (48%)
  starting transfers between devices  59.5 us (21%)
  blocking collectives  48.9 us (17%)
  local copies, waits for them, and re-layouts  15.4 us (5%)
  Pallas kernels  9.84 us (3%)
  matrix products  7.84 us (3%)
  other arithmetic  4.92 us (2%)
    ppermute x1, waiting for transfers between devices, on_device(): across = lax.ppermute(tokens, 'z0', SWAP)  46.3 us
    ppermute x1, waiting for transfers between devices, all_rows(): other = lax.ppermute(weights, 'yl', SWAP)  38.2 us
    all_to_all x1, blocking collectives, on_device(): lax.all_to_all(jnp.stack(blocks), SUM, split_axis=0, concat_axis=0, tiled...  37.8 us
    ppermute x3, waiting for transfers between devices, on_device(): lax.ppermute(rows, 'zh', [(k, (k + step) % 4) for k in range(4)])  19.9 us
    all_to_all x2, starting transfers between devices, on_device(): lax.all_to_all(outgoing, GROUP, split_axis=0, concat_axis=0, tiled=True)  17.3 us
    ppermute x1, waiting for transfers between devices, on_device(): gradient = lax.ppermute(summed, AXES, home_permutation())  11.8 us
    all_to_all x1, blocking collectives, on_device(): lax.all_to_all(weights.reshape(16, 32, 128), TP, split_axis=0, concat_axi...  11.2 us
    ppermute x3, waiting for transfers between devices, all_rows(): up = lax.ppermute(up, Z, ring(1))  10.2 us
  transfers between devices with their start and end apart: 20, of which 11 were waited for; matrix products, arithmetic and copies ran while one was open for 7% of the time, Pallas kernels for 1%

profile of v6, /device:TPU:22, one launch (start us, length us, event | category | flops | bytes accessed | tf_op | source)
XLA Modules:
  0.0 281.8 jit_solution(3422812499952245127)
XLA Ops:
  0.6 7.2 %all-to-all-start = ((bf16[16,64,256]{2,1,0:T(8,128)(2,1)}), bf16[16,64,256]{2,1,0:T(8,128)(2,1)S(1)}, u32[]{:S(2)}, u32[]{:S(2)}) async-start(bf16[16,64,256]{2,1,0:T(8,128)(2,1)} %bitcast.126), calls=%async_computation | async-start | bytes 1048576 | tf_op jit(solution)/shard_map/all_to_all | solution.py:200
  7.8 0.6 pad_add_fusion.place_ref
  8.4 6.7 %all-to-all-done.slots_ref = bf16[16,64,256]{2,1,0:T(8,128)(2,1)S(1)} async-done(((bf16[16,64,256]{2,1,0:T(8,128)(2,1)}), bf16[16,64,256]{2,1,0:T(8,128)(2,1)S(1)}, u32[]{:S(2)}, u32[]{:S(2)}) %all-to-all-start) | async-done | bytes 524320 | tf_op jit(solution)/shard_map/all_to_all | solution.py:200
  15.1 0.8 copy-done.2
  15.9 3.1 %pack.1 = bf16[2,8,2,64,512]{4,3,2,1,0:T(8,128)(2,1)} custom-call(s32[2]{0:T(128)} %pad_add_fusion.place_ref, s32[16,16]{1,0:T(8,128)} %lengths_ref.5, bf16[16,64,256]{2,1,0:T(8,128)(2,1)} %copy-done.2), custom_call_target="tpu_custom_call" | custom-call | flops 1000000 | bytes 5000000 | tf_op jit(solution)/shard_map/pack/pallas_call | solution.py:102
  19.0 9.1 %all-to-all-start.1 = ((bf16[32,64,512]{2,1,0:T(8,128)(2,1)}), bf16[32,64,512]{2,1,0:T(8,128)(2,1)S(1)}, u32[]{:S(2)}, u32[]{:S(2)}) async-start(bf16[32,64,512]{2,1,0:T(8,128)(2,1)} %bitcast.117), calls=%async_computation.1 | async-start | bytes 4194304 | tf_op jit(solution)/shard_map/all_to_all | solution.py:202
  28.1 1.6 collective-permute-start
  29.7 46.3 %collective-permute-done = bf16[1024,512]{1,0:T(8,128)(2,1)} collective-permute-done((bf16[1024,512]{1,0:T(8,128)(2,1)}, bf16[1024,512]{1,0:T(8,128)(2,1)}, u32[]{:S(2)}, u32[]{:S(2)}) %collective-permute-start) | collective-permute-done | bytes 1048608 | tf_op jit(solution)/shard_map/ppermute | solution.py:195
  76.0 2.0 fusion.11
  78.0 2.0 fusion.3
  80.0 2.0 fusion.9
  81.9 0.0 collective-permute-done.2
  82.0 2.0 fusion.2
  84.0 0.0 copy-start.4
  84.0 0.0 copy-start.5
  84.0 0.0 copy-start.6
  84.1 37.8 %all_to_all.30 = bf16[8,512,128]{1,2,0:T(8,128)(2,1)S(1)} all-to-all(bf16[8,512,128]{1,2,0:T(8,128)(2,1)S(1)} %fusion.19), channel_id=1, replica_groups=mesh['yl'=2,'zh'=4,'z0'=2,'x'=4,'yh'=2,'co'=2] {'yl','zh'}, dimensions={0} | all-to-all | bytes 2097152 | tf_op jit(solution)/shard_map/all_to_all | solution.py:214
  121.9 0.1 reduce_sum.12
  122.0 0.1 copy.21
  122.1 1.9 collective-permute-start.3
  124.1 11.8 %collective-permute-done.3 = bf16[512,128]{1,0:T(8,128)(2,1)S(1)} collective-permute-done((bf16[512,128]{1,0:T(8,128)(2,1)S(1)}, bf16[512,128]{1,0:T(8,128)(2,1)S(1)}, u32[]{:S(2)}, u32[]{:S(2)}) %collective-permute-start.3) | collective-permute-done | bytes 131104 | tf_op jit(solution)/shard_map/ppermute | solution.py:216
  135.9 1.0 fusion.31
  136.9 11.2 %all_to_all.31 = bf16[16,32,128]{2,1,0:T(8,128)(2,1)} all-to-all(bf16[16,32,128]{2,1,0:T(8,128)(2,1)S(1)} %bitcast.124), channel_id=1, replica_groups=mesh['yl'=2,'zh'=4,'z0'=2,'x'=4,'yh'=2,'co'=2] {'x','yh','co'}, dimensions={0} | all-to-all | bytes 262144 | tf_op jit(solution)/shard_map/all_to_all | solution.py:222
  148.0 3.0 %unpack.2 = bf16[64,1,32,256]{3,2,1,0:T(8,128)(2,1)} custom-call(s32[2]{0:T(128)} %pad_add_fusion.place_ref, s32[16,16]{1,0:T(8,128)} %lengths_ref.5, bf16[1,16,32,128]{3,2,1,0:T(8,128)(2,1)} %bitcast.125), custom_call_target="tpu_custom_call" | custom-call | flops 3000000 | bytes 1300000 | tf_op jit(solution)/shard_map/unpack/pallas_call | solution.py:147
  151.0 8.8 %all-to-all-start.4 = ((bf16[64,1,32,256]{3,2,1,0:T(8,128)(2,1)}), bf16[64,1,32,256]{3,2,1,0:T(8,128)(2,1)S(1)}, u32[]{:S(2)}, u32[]{:S(2)}) async-start(bf16[64,1,32,256]{3,2,1,0:T(8,128)(2,1)} %unpack.2), calls=%async_computation.4 | async-start | bytes 2097152 | tf_op jit(solution)/shard_map/all_to_all | solution.py:229
  159.8 2.0 collective-permute-start.13
  161.8 3.3 %collective-permute-start.14 = (bf16[16,32,128]{2,1,0:T(8,128)(2,1)S(1)}, bf16[16,32,128]{2,1,0:T(8,128)(2,1)S(1)}, u32[]{:S(2)}, u32[]{:S(2)}) collective-permute-start(bf16[16,32,128]{2,1,0:T(8,128)(2,1)S(1)} %copy-done.3), channel_id=1, source_target_pairs={{0,64},{32,96},{64,0},{96,32},{1,65},{33,97},{65,1},{97,33},{2,66}... | collective-permute-start | bytes 393224 | tf_op jit(solution)/shard_map/ppermute | solution.py:223
  165.0 1.4 collective-permute-done.13
  166.4 14.9 %collective-permute-done.14 = bf16[16,32,128]{2,1,0:T(8,128)(2,1)S(1)} collective-permute-done((bf16[16,32,128]{2,1,0:T(8,128)(2,1)S(1)}, bf16[16,32,128]{2,1,0:T(8,128)(2,1)S(1)}, u32[]{:S(2)}, u32[]{:S(2)}) %collective-permute-start.14) | collective-permute-done | bytes 131104 | tf_op jit(solution)/shard_map/ppermute | solution.py:223
  181.3 3.7 %collective-permute-done.15 = bf16[16,32,128]{2,1,0:T(8,128)(2,1)S(1)} collective-permute-done((bf16[16,32,128]{2,1,0:T(8,128)(2,1)S(1)}, bf16[16,32,128]{2,1,0:T(8,128)(2,1)S(1)}, u32[]{:S(2)}, u32[]{:S(2)}) %collective-permute-start.15) | collective-permute-done | bytes 131104 | tf_op jit(solution)/shard_map/ppermute | solution.py:223
  184.9 0.8 pad_maximum_fusion.weights_ref
  185.8 3.7 %unpack.3 = bf16[64,3,32,256]{3,2,1,0:T(8,128)(2,1)} custom-call(s32[2]{0:T(128)} %pad_add_fusion.place_ref, s32[16,16]{1,0:T(8,128)} %lengths_ref.5, bf16[3,16,32,128]{3,2,1,0:T(8,128)(2,1)} %pad_maximum_fusion.weights_ref), custom_call_target="tpu_custom_call" | custom-call | flops 9000000 | bytes 3900000 | tf_op jit(solution)/shard_map/unpack/pallas_call | solution.py:147
  189.5 1.0 copy-done.1
  190.5 8.5 %all-to-all-start.5 = ((bf16[64,3,32,256]{3,2,1,0:T(8,128)(2,1)}), bf16[64,3,32,256]{3,2,1,0:T(8,128)(2,1)S(1)}, u32[]{:S(2)}, u32[]{:S(2)}) async-start(bf16[64,3,32,256]{3,2,1,0:T(8,128)(2,1)} %unpack.3), calls=%async_computation.5 | async-start | bytes 6291456 | tf_op jit(solution)/shard_map/all_to_all | solution.py:229
  199.0 1.4 collective-permute-start.4
  200.4 38.2 %collective-permute-done.4 = bf16[512,128]{1,0:T(8,128)(2,1)} collective-permute-done((bf16[512,128]{1,0:T(8,128)(2,1)S(1)}, bf16[512,128]{1,0:T(8,128)(2,1)}, u32[]{:S(2)}, u32[]{:S(2)}) %collective-permute-start.4) | collective-permute-done | bytes 131104 | tf_op jit(solution)/shard_map/ppermute | solution.py:165
  238.7 0.9 select_bitcast_fusion.1
  239.6 0.7 pad_maximum_fusion.1
  240.3 3.9 %collective-permute-start.5 = (bf16[2,512,128]{2,1,0:T(8,128)(2,1)}, bf16[2,512,128]{2,1,0:T(8,128)(2,1)}, u32[]{:S(2)}, u32[]{:S(2)}) collective-permute-start(bf16[2,512,128]{2,1,0:T(8,128)(2,1)} %pad_maximum_fusion.1), channel_id=1, source_target_pairs={{0,16},{16,32},{32,48},{48,64},{64,80},{80,96},{96,112},{112,0},{1... | collective-permute-start | bytes 786440 | tf_op jit(solution)/shard_map/ppermute | solution.py:175
  244.3 1.9 collective-permute-start.6
  246.2 1.7 broadcast_in_dim.40
  247.9 0.7 bitcast_dynamic-update-slice_fusion.6
  248.6 4.4 %collective-permute-done.5 = bf16[2,512,128]{2,1,0:T(8,128)(2,1)} collective-permute-done((bf16[2,512,128]{2,1,0:T(8,128)(2,1)}, bf16[2,512,128]{2,1,0:T(8,128)(2,1)}, u32[]{:S(2)}, u32[]{:S(2)}) %collective-permute-start.5) | collective-permute-done | bytes 262176 | tf_op jit(solution)/shard_map/ppermute | solution.py:175
  253.0 3.2 %collective-permute-start.8 = (bf16[2,512,128]{2,1,0:T(8,128)(2,1)}, bf16[2,512,128]{2,1,0:T(8,128)(2,1)S(1)}, u32[]{:S(2)}, u32[]{:S(2)}) collective-permute-start(bf16[2,512,128]{2,1,0:T(8,128)(2,1)} %collective-permute-done.6), channel_id=1, source_target_pairs={{0,112},{16,0},{32,16},{48,32},{64,48},{80,64},{96,80},{112,96},{1... | collective-permute-start | bytes 786440 | tf_op jit(solution)/shard_map/ppermute | solution.py:176
  256.2 1.7 bitcast_dynamic-update-slice_fusion.5
  257.9 1.7 bitcast_dynamic-update-slice_fusion.4
  259.6 2.5 collective-permute-done.7
  262.1 3.2 %collective-permute-start.10 = (bf16[2,512,128]{2,1,0:T(8,128)(2,1)S(1)}, bf16[2,512,128]{2,1,0:T(8,128)(2,1)S(1)}, u32[]{:S(2)}, u32[]{:S(2)}) collective-permute-start(bf16[2,512,128]{2,1,0:T(8,128)(2,1)S(1)} %collective-permute-done.8), channel_id=1, source_target_pairs={{0,112},{16,0},{32,16},{48,32},{64,48},{80,64},{96,80},{112,96},{1... | collective-permute-start | bytes 786440 | tf_op jit(solution)/shard_map/ppermute | solution.py:176
  265.4 0.7 bitcast_dynamic-update-slice_fusion.3
  266.1 0.7 bitcast_dynamic-update-slice_fusion.2
  266.8 3.4 %collective-permute-done.9 = bf16[2,512,128]{2,1,0:T(8,128)(2,1)S(1)} collective-permute-done((bf16[2,512,128]{2,1,0:T(8,128)(2,1)S(1)}, bf16[2,512,128]{2,1,0:T(8,128)(2,1)S(1)}, u32[]{:S(2)}, u32[]{:S(2)}) %collective-permute-start.9) | collective-permute-done | bytes 262176 | tf_op jit(solution)/shard_map/ppermute | solution.py:175
  270.2 0.1 collective-permute-start.11
  270.3 3.3 %collective-permute-start.12 = (bf16[1,512,128]{2,1,0:T(8,128)(2,1)S(1)}, bf16[1,512,128]{2,1,0:T(8,128)(2,1)S(1)}, u32[]{:S(2)}, u32[]{:S(2)}) collective-permute-start(bf16[1,512,128]{2,1,0:T(8,128)(2,1)S(1)} %slice.61), channel_id=1, source_target_pairs={{0,112},{16,0},{32,16},{48,32},{64,48},{80,64},{96,80},{112,96},{1... | collective-permute-start | bytes 393224 | tf_op jit(solution)/shard_map/ppermute | solution.py:180
  273.6 0.7 bitcast_dynamic-update-slice_fusion.1
  274.3 0.7 bitcast_dynamic-update-slice_fusion
  275.0 1.4 collective-permute-done.11
  276.4 0.7 bitcast_dynamic-update-slice_fusion.8
  277.1 0.7 bitcast_dynamic-update-slice_fusion.7
  277.8 1.7 broadcast_in_dim.52
  279.5 0.1 fusion.6
  279.6 0.1 fusion.5
  279.7 0.1 fusion.4
  279.8 0.0 copy-start
  279.8 2.0 copy-done
  (30 shorter events, 0.2 us)
Async XLA Ops:
  0.6 14.5 %all-to-all-start = ((bf16[16,64,256]{2,1,0:T(8,128)(2,1)}), bf16[16,64,256]{2,1,0:T(8,128)(2,1)S(1)}, u32[]{:S(2)}, u32[]{:S(2)}) async-start(bf16[16,64,256]{2,1,0:T(8,128)(2,1)} %bitcast.126), calls=%async_computation | async-start | bytes 1048576 | tf_op jit(solution)/shard_map/all_to_all | solution.py:200
  15.1 0.8 copy-start.2
  19.0 57.0 %all-to-all-start.1 = ((bf16[32,64,512]{2,1,0:T(8,128)(2,1)}), bf16[32,64,512]{2,1,0:T(8,128)(2,1)S(1)}, u32[]{:S(2)}, u32[]{:S(2)}) async-start(bf16[32,64,512]{2,1,0:T(8,128)(2,1)} %bitcast.117), calls=%async_computation.1 | async-start | bytes 4194304 | tf_op jit(solution)/shard_map/all_to_all | solution.py:202
  28.1 47.9 %collective-permute-start = (bf16[1024,512]{1,0:T(8,128)(2,1)}, bf16[1024,512]{1,0:T(8,128)(2,1)}, u32[]{:S(2)}, u32[]{:S(2)}) collective-permute-start(bf16[1024,512]{1,0:T(8,128)(2,1)} %param.6), channel_id=1, source_target_pairs={{0,16},{16,0},{1,17},{17,1},{2,18},{18,2},{3,19},{19,3},{4,20},{20... | collective-permute-start | bytes 3145736 | tf_op jit(solution)/shard_map/ppermute | solution.py:195
  29.7 50.2 %collective-permute-start.1 = (bf16[1024,512]{1,0:T(8,128)(2,1)}, bf16[1024,512]{1,0:T(8,128)(2,1)}, u32[]{:S(2)}, u32[]{:S(2)}) collective-permute-start(bf16[1024,512]{1,0:T(8,128)(2,1)} %param.6), channel_id=1, source_target_pairs={{0,1},{1,0},{2,3},{3,2},{4,5},{5,4},{6,7},{7,6},{8,9},{9,8},{10,11... | collective-permute-start | bytes 3145736 | tf_op jit(solution)/shard_map/ppermute | solution.py:197
  76.0 6.0 %collective-permute-start.2 = (bf16[1024,512]{1,0:T(8,128)(2,1)}, bf16[1024,512]{1,0:T(8,128)(2,1)}, u32[]{:S(2)}, u32[]{:S(2)}) collective-permute-start(bf16[1024,512]{1,0:T(8,128)(2,1)} %collective-permute-done), channel_id=1, source_target_pairs={{0,1},{1,0},{2,3},{3,2},{4,5},{5,4},{6,7},{7,6},{8,9},{9,8},{10,11... | collective-permute-start | bytes 3145736 | tf_op jit(solution)/shard_map/ppermute | solution.py:197
  84.0 51.8 %copy-start.4 = (f32[512,128]{1,0:T(8,128)S(1)}, f32[512,128]{1,0:T(8,128)}, u32[]{:S(2)}) copy-start(f32[512,128]{1,0:T(8,128)} %param.9) | copy-start | bytes 786436
  84.0 51.8 %copy-start.5 = (f32[512,128]{1,0:T(8,128)S(1)}, f32[512,128]{1,0:T(8,128)}, u32[]{:S(2)}) copy-start(f32[512,128]{1,0:T(8,128)} %param.11) | copy-start | bytes 786436
  84.0 51.8 %copy-start.6 = (f32[512,128]{1,0:T(8,128)S(1)}, f32[512,128]{1,0:T(8,128)}, u32[]{:S(2)}) copy-start(f32[512,128]{1,0:T(8,128)} %param.10) | copy-start | bytes 786436
  122.1 13.7 %collective-permute-start.3 = (bf16[512,128]{1,0:T(8,128)(2,1)S(1)}, bf16[512,128]{1,0:T(8,128)(2,1)S(1)}, u32[]{:S(2)}, u32[]{:S(2)}) collective-permute-start(bf16[512,128]{1,0:T(8,128)(2,1)S(1)} %copy.21), channel_id=1, source_target_pairs={{0,0},{1,20},{2,36},{3,48},{4,76},{5,88},{6,104},{7,124},{8,128},{... | collective-permute-start | bytes 393224 | tf_op jit(solution)/shard_map/ppermute | solution.py:216
  148.0 11.8 %copy-start.3 = (bf16[16,32,128]{2,1,0:T(8,128)(2,1)S(1)}, bf16[16,32,128]{2,1,0:T(8,128)(2,1)}, u32[]{:S(2)}) copy-start(bf16[16,32,128]{2,1,0:T(8,128)(2,1)} %all_to_all.31) | copy-start | bytes 393220
  151.0 38.5 %all-to-all-start.4 = ((bf16[64,1,32,256]{3,2,1,0:T(8,128)(2,1)}), bf16[64,1,32,256]{3,2,1,0:T(8,128)(2,1)S(1)}, u32[]{:S(2)}, u32[]{:S(2)}) async-start(bf16[64,1,32,256]{3,2,1,0:T(8,128)(2,1)} %unpack.2), calls=%async_computation.4 | async-start | bytes 2097152 | tf_op jit(solution)/shard_map/all_to_all | solution.py:229
  159.8 6.6 %collective-permute-start.13 = (bf16[16,32,128]{2,1,0:T(8,128)(2,1)S(1)}, bf16[16,32,128]{2,1,0:T(8,128)(2,1)S(1)}, u32[]{:S(2)}, u32[]{:S(2)}) collective-permute-start(bf16[16,32,128]{2,1,0:T(8,128)(2,1)S(1)} %copy-done.3), channel_id=1, source_target_pairs={{0,96},{32,0},{64,32},{96,64},{1,97},{33,1},{65,33},{97,65},{2,98}... | collective-permute-start | bytes 393224 | tf_op jit(solution)/shard_map/ppermute | solution.py:223
  161.8 19.5 %collective-permute-start.14 = (bf16[16,32,128]{2,1,0:T(8,128)(2,1)S(1)}, bf16[16,32,128]{2,1,0:T(8,128)(2,1)S(1)}, u32[]{:S(2)}, u32[]{:S(2)}) collective-permute-start(bf16[16,32,128]{2,1,0:T(8,128)(2,1)S(1)} %copy-done.3), channel_id=1, source_target_pairs={{0,64},{32,96},{64,0},{96,32},{1,65},{33,97},{65,1},{97,33},{2,66}... | collective-permute-start | bytes 393224 | tf_op jit(solution)/shard_map/ppermute | solution.py:223
  165.0 19.9 %collective-permute-start.15 = (bf16[16,32,128]{2,1,0:T(8,128)(2,1)S(1)}, bf16[16,32,128]{2,1,0:T(8,128)(2,1)S(1)}, u32[]{:S(2)}, u32[]{:S(2)}) collective-permute-start(bf16[16,32,128]{2,1,0:T(8,128)(2,1)S(1)} %copy-done.3), channel_id=1, source_target_pairs={{0,32},{32,64},{64,96},{96,0},{1,33},{33,65},{65,97},{97,1},{2,34}... | collective-permute-start | bytes 393224 | tf_op jit(solution)/shard_map/ppermute | solution.py:223
  189.5 1.0 copy-start.1
  190.5 87.3 %all-to-all-start.5 = ((bf16[64,3,32,256]{3,2,1,0:T(8,128)(2,1)}), bf16[64,3,32,256]{3,2,1,0:T(8,128)(2,1)S(1)}, u32[]{:S(2)}, u32[]{:S(2)}) async-start(bf16[64,3,32,256]{3,2,1,0:T(8,128)(2,1)} %unpack.3), calls=%async_computation.5 | async-start | bytes 6291456 | tf_op jit(solution)/shard_map/all_to_all | solution.py:229
  199.0 39.7 %collective-permute-start.4 = (bf16[512,128]{1,0:T(8,128)(2,1)S(1)}, bf16[512,128]{1,0:T(8,128)(2,1)}, u32[]{:S(2)}, u32[]{:S(2)}) collective-permute-start(bf16[512,128]{1,0:T(8,128)(2,1)S(1)} %get-tuple-element.5), channel_id=1, source_target_pairs={{0,128},{128,0},{1,129},{129,1},{2,130},{130,2},{3,131},{131,3},{4... | collective-permute-start | bytes 393224 | tf_op jit(solution)/shard_map/ppermute | solution.py:165
  240.3 12.7 %collective-permute-start.5 = (bf16[2,512,128]{2,1,0:T(8,128)(2,1)}, bf16[2,512,128]{2,1,0:T(8,128)(2,1)}, u32[]{:S(2)}, u32[]{:S(2)}) collective-permute-start(bf16[2,512,128]{2,1,0:T(8,128)(2,1)} %pad_maximum_fusion.1), channel_id=1, source_target_pairs={{0,16},{16,32},{32,48},{48,64},{64,80},{80,96},{96,112},{112,0},{1... | collective-permute-start | bytes 786440 | tf_op jit(solution)/shard_map/ppermute | solution.py:175
  244.3 8.8 %collective-permute-start.6 = (bf16[2,512,128]{2,1,0:T(8,128)(2,1)}, bf16[2,512,128]{2,1,0:T(8,128)(2,1)}, u32[]{:S(2)}, u32[]{:S(2)}) collective-permute-start(bf16[2,512,128]{2,1,0:T(8,128)(2,1)} %pad_maximum_fusion.1), channel_id=1, source_target_pairs={{0,112},{16,0},{32,16},{48,32},{64,48},{80,64},{96,80},{112,96},{1... | collective-permute-start | bytes 786440 | tf_op jit(solution)/shard_map/ppermute | solution.py:176
  253.0 9.1 %collective-permute-start.7 = (bf16[2,512,128]{2,1,0:T(8,128)(2,1)}, bf16[2,512,128]{2,1,0:T(8,128)(2,1)S(1)}, u32[]{:S(2)}, u32[]{:S(2)}) collective-permute-start(bf16[2,512,128]{2,1,0:T(8,128)(2,1)} %collective-permute-done.5), channel_id=1, source_target_pairs={{0,16},{16,32},{32,48},{48,64},{64,80},{80,96},{96,112},{112,0},{1... | collective-permute-start | bytes 786440 | tf_op jit(solution)/shard_map/ppermute | solution.py:175
  253.0 9.1 %collective-permute-start.8 = (bf16[2,512,128]{2,1,0:T(8,128)(2,1)}, bf16[2,512,128]{2,1,0:T(8,128)(2,1)S(1)}, u32[]{:S(2)}, u32[]{:S(2)}) collective-permute-start(bf16[2,512,128]{2,1,0:T(8,128)(2,1)} %collective-permute-done.6), channel_id=1, source_target_pairs={{0,112},{16,0},{32,16},{48,32},{64,48},{80,64},{96,80},{112,96},{1... | collective-permute-start | bytes 786440 | tf_op jit(solution)/shard_map/ppermute | solution.py:176
  262.1 8.1 %collective-permute-start.9 = (bf16[2,512,128]{2,1,0:T(8,128)(2,1)S(1)}, bf16[2,512,128]{2,1,0:T(8,128)(2,1)S(1)}, u32[]{:S(2)}, u32[]{:S(2)}) collective-permute-start(bf16[2,512,128]{2,1,0:T(8,128)(2,1)S(1)} %collective-permute-done.7), channel_id=1, source_target_pairs={{0,16},{16,32},{32,48},{48,64},{64,80},{80,96},{96,112},{112,0},{1... | collective-permute-start | bytes 786440 | tf_op jit(solution)/shard_map/ppermute | solution.py:175
  262.1 8.2 %collective-permute-start.10 = (bf16[2,512,128]{2,1,0:T(8,128)(2,1)S(1)}, bf16[2,512,128]{2,1,0:T(8,128)(2,1)S(1)}, u32[]{:S(2)}, u32[]{:S(2)}) collective-permute-start(bf16[2,512,128]{2,1,0:T(8,128)(2,1)S(1)} %collective-permute-done.8), channel_id=1, source_target_pairs={{0,112},{16,0},{32,16},{48,32},{64,48},{80,64},{96,80},{112,96},{1... | collective-permute-start | bytes 786440 | tf_op jit(solution)/shard_map/ppermute | solution.py:176
  270.2 6.3 %collective-permute-start.11 = (bf16[1,512,128]{2,1,0:T(8,128)(2,1)S(1)}, bf16[1,512,128]{2,1,0:T(8,128)(2,1)S(1)}, u32[]{:S(2)}, u32[]{:S(2)}) collective-permute-start(bf16[1,512,128]{2,1,0:T(8,128)(2,1)S(1)} %slice.60), channel_id=1, source_target_pairs={{0,16},{16,32},{32,48},{48,64},{64,80},{80,96},{96,112},{112,0},{1... | collective-permute-start | bytes 393224 | tf_op jit(solution)/shard_map/ppermute | solution.py:179
  270.3 6.8 %collective-permute-start.12 = (bf16[1,512,128]{2,1,0:T(8,128)(2,1)S(1)}, bf16[1,512,128]{2,1,0:T(8,128)(2,1)S(1)}, u32[]{:S(2)}, u32[]{:S(2)}) collective-permute-start(bf16[1,512,128]{2,1,0:T(8,128)(2,1)S(1)} %slice.61), channel_id=1, source_target_pairs={{0,112},{16,0},{32,16},{48,32},{64,48},{80,64},{96,80},{112,96},{1... | collective-permute-start | bytes 393224 | tf_op jit(solution)/shard_map/ppermute | solution.py:180
  279.8 2.0 copy-start
